TPU v7x, 128 devices: a whole 4x4x4 slice. The times are simulated.
128 devices in a mesh: blk: 32 (over x, z, core), tok: 4 (over y).
Axes of the slice: x: 4, y: 4, z: 4, core: 2. Of those that a mesh axis runs over, the one named last changes fastest.
Arguments:
- stream: bfloat16 [16384, 1664], P(('tok', 'blk'))
- queries: bfloat16 [16384, 1664], P(('tok', 'blk'))
- key_cache: bfloat16 [16384, 1664], P(('tok', 'blk'))
- value_cache: bfloat16 [16384, 1664], P(('tok', 'blk')), may hold values from -6 to 6
- segments: int32 [16384], P('tok'), may hold values from 63 to 16383, as said below
- stale_rows: int32 [1536], P(('tok', 'blk')), may hold values from 0 to 16383, as said below
- owners: int32 [4096], P(('tok', 'blk')), may hold values from 0 to 3, as said below
- attn_gain: float32 [1664], replicated, may hold values from 0.1 to 1.9
- w_key: bfloat16 [1664, 1664], replicated, may hold values from -0.15625 to 0.15625
- key_bias: float32 [1664], replicated, may hold values from -3 to 3
- mlp_gain: float32 [1664], replicated, may hold values from 0.1 to 1.9
- w_fc: bfloat16 [1664, 8192], P(None, 'blk'), may hold values from -0.15625 to 0.15625
- b_fc: float32 [8192], P('blk'), may hold values from -3 to 3
- w_proj: bfloat16 [8192, 1664], P('blk'), may hold values from -0.125 to 0.125
- b_proj: float32 [1664], replicated, may hold values from -3 to 3
- merge_gain: float32 [1664], replicated, may hold values from 0.1 to 1.9
- w_merge: bfloat16 [1664, 1664], replicated, may hold values from -0.15625 to 0.15625
- b_merge: float32 [1664], replicated, may hold values from -3 to 3
Outputs:
- refreshed_keys: bfloat16 [16384, 1664], P(('tok', 'blk'))
- delivered: bfloat16 [4, 32, 128, 1664], P('tok', 'blk')
Inputs may be any that keep to these rules, and one draw needn't show every extreme that they name: `segments`: A segment's id is the index of its last row, so ids never fall; each segment has 4 to 128 rows, a multiple of 4, and lies inside one aligned block of 4096 rows; each such block begins with a segment of 64 rows followed by one of exactly 128 rows. `stale_rows`: Distinct; the aligned block of 128 rows of each device holds exactly 12 of them, all inside that block and listed on that device; row 0 and the last row are always listed. `owners`: all merged tokens of one segment (the segment of row 4 m for merged token m) have the same owner.
All inputs are finite; a program needn't handle non-finite values.
Results may differ from a plain program's by a relative error of at most 0.011.
Values may be sent and summed in bfloat16 or wider, within the bound.
No kernel may reach another device: no remote copies, remote signals or barrier semaphores. Data moves between devices by JAX's collectives and lax.ppermute only.
A program may use at most 192 MiB of HBM per device.

v0:
```python
import jax
import jax.numpy as jnp
from jax import lax
from jax.sharding import PartitionSpec as P

HEADS = 16


def passed_along(block, axis, distance):
    devices = range(lax.axis_size(axis))
    route = [(i - distance, i) for i in devices if i - distance in devices]
    return lax.ppermute(block, axis, route)


def layer_norm(values, gain):
    center = values - jnp.mean(values, axis=-1, keepdims=True)
    spread = jnp.mean(center * center, axis=-1, keepdims=True)
    return center * lax.rsqrt(spread + 1e-06) * gain


def body(
    stream,
    queries,
    key_cache,
    value_cache,
    segments,
    stale_rows,
    owners,
    attn_gain,
    w_key,
    key_bias,
    mlp_gain,
    w_fc,
    b_fc,
    w_proj,
    b_proj,
    merge_gain,
    w_merge,
    b_merge,
):
    row_count = stream.shape[0]
    model_width = stream.shape[1]
    head_size = model_width // HEADS
    local_rows = stale_rows % row_count
    held = layer_norm(stream[local_rows].astype(jnp.float32), attn_gain).astype(jnp.bfloat16)
    fresh_keys = (jnp.dot(held, w_key, preferred_element_type=jnp.float32) + key_bias).astype(
        jnp.bfloat16
    )
    refreshed = key_cache.at[local_rows].set(fresh_keys)
    below = passed_along((refreshed, value_cache), "blk", 1)
    above = passed_along((refreshed, value_cache), "blk", -1)
    key_window = jnp.concatenate([below[0], refreshed, above[0]], axis=0).reshape(
        3 * row_count, HEADS, head_size
    )
    value_window = jnp.concatenate([below[1], value_cache, above[1]], axis=0).reshape(
        3 * row_count, HEADS, head_size
    )
    position = lax.axis_index("blk")
    minus_ones = jnp.full((row_count,), -1, jnp.int32)
    seg_padded = jnp.concatenate([minus_ones, segments, minus_ones], axis=0)
    key_seg = lax.dynamic_slice_in_dim(seg_padded, position * row_count, 3 * row_count, 0)
    query_seg = lax.dynamic_slice_in_dim(segments, position * row_count, row_count, 0)
    query_heads = queries.reshape(row_count, HEADS, head_size)
    scores = jnp.einsum(
        "qhd,khd->hqk", query_heads, key_window, preferred_element_type=jnp.float32
    ) * (1.0 / head_size**0.5)
    allowed = (query_seg[:, None] == key_seg[None, :])[None]
    scores = jnp.where(allowed, scores, -jnp.inf)
    top_score = jnp.max(scores, axis=-1, keepdims=True)
    weights = jnp.exp(scores - top_score)
    probs = (weights / jnp.sum(weights, axis=-1, keepdims=True)).astype(jnp.bfloat16)
    attended = jnp.einsum("hqk,khd->qhd", probs, value_window, preferred_element_type=jnp.float32)
    attended = attended.reshape(row_count, model_width).astype(jnp.bfloat16)
    mixed = stream.astype(jnp.float32) + attended.astype(jnp.float32)
    normed = layer_norm(mixed, mlp_gain).astype(jnp.bfloat16)
    group_units = jax.nn.gelu(
        jnp.dot(
            lax.all_gather(normed, "blk", axis=0, tiled=True),
            w_fc,
            preferred_element_type=jnp.float32,
        )
        + b_fc,
        approximate=False,
    ).astype(jnp.bfloat16)
    summed = lax.psum_scatter(
        jnp.dot(group_units, w_proj, preferred_element_type=jnp.float32).astype(jnp.bfloat16),
        "blk",
        scatter_dimension=0,
        tiled=True,
    ).astype(jnp.float32)
    pooled = jnp.mean((mixed + summed).reshape(row_count // 4, 4, model_width), axis=1) + b_proj
    merge_in = layer_norm(pooled, merge_gain).astype(jnp.bfloat16)
    merged = (jnp.dot(merge_in, w_merge, preferred_element_type=jnp.float32) + b_merge).astype(
        jnp.bfloat16
    )
    owner_count = lax.axis_size("tok")
    merged_rows = row_count // 4
    owner_hot = (owners[:, None] == jnp.arange(owner_count, dtype=jnp.int32)[None, :]).astype(
        jnp.int32
    )
    ranking = jnp.sum(jnp.cumsum(owner_hot, axis=0) * owner_hot, axis=-1) - 1
    selector = (
        owners[None, None, :] == jnp.arange(owner_count, dtype=jnp.int32)[:, None, None]
    ) & (ranking[None, None, :] == jnp.arange(merged_rows, dtype=jnp.int32)[None, :, None])
    outgoing = jnp.einsum(
        "osm,md->osd", selector.astype(jnp.bfloat16), merged, preferred_element_type=jnp.float32
    ).astype(jnp.bfloat16)
    arrived = lax.all_to_all(outgoing, "tok", split_axis=0, concat_axis=0, tiled=True)
    delivered = arrived.reshape(1, 1, owner_count * merged_rows, model_width)
    return (refreshed, delivered)


def solution(mesh):
    return jax.shard_map(
        body,
        mesh=mesh,
        in_specs=(
            P(("tok", "blk"), None),
            P(("tok", "blk"), None),
            P(("tok", "blk"), None),
            P(("tok", "blk"), None),
            P("tok"),
            P(("tok", "blk")),
            P(("tok", "blk")),
            P(),
            P(),
            P(),
            P(),
            P(None, "blk"),
            P("blk"),
            P("blk", None),
            P(),
            P(),
            P(),
            P(),
        ),
        out_specs=(P(("tok", "blk"), None), P("tok", "blk", None, None)),
        check_vma=False,
    )
```

profile of v0, /device:TPU:0, one launch (start us, length us, event | category | flops | bytes accessed | tf_op | source)
XLA Modules:
  0.0 274.7 jit_solution(774383592987161788)
XLA Ops:
  7.3 0.8 compare_select_fusion
  8.1 1.7 gather_fusion
  9.9 0.2 fusion.58
  10.1 3.4 %fusion.14 = bf16[12,1664]{1,0:T(8,128)(2,1)S(1)} fusion(bf16[1664,1664]{1,0:T(8,128)(2,1)} %param.26, bf16[12,1664]{1,0:T(8,128)(2,1)S(1)} %gather_fusion, f32[1664]{0:T(1024)} %param.27, f32[1664]{0:T(1024)} %param.25, f32[12]{0:T(128)S(1)} %add_rsqrt_fusion.2, f32[12]{0:T(128)S(1)} %broadcast_multiply_fusion.2), kind=kOutput, calls=%fused_computation.33 | convolution fusion | flops 66593280 | bytes 5631072 | tf_op jit(solution)/shard_map/dot_general | solution.py:46
  13.6 0.9 scatter_fusion
  14.5 1.3 collective-permute-start.2
  15.9 1.3 collective-permute-start.3
  17.2 5.3 %collective-permute-start = (bf16[128,1664]{1,0:T(8,128)(2,1)S(1)}, bf16[128,1664]{1,0:T(8,128)(2,1)S(1)}, u32[]{:S(2)}, u32[]{:S(2)}) collective-permute-start(bf16[128,1664]{1,0:T(8,128)(2,1)S(1)} %copy-done.5), channel_id=1, source_target_pairs={{0,4},{4,8},{8,12},{12,16},{16,20},{20,24},{24,28},{28,32},{32,36}... | collective-permute-start | bytes 1277960 | tf_op jit(solution)/shard_map/ppermute | solution.py:12
  22.4 1.3 collective-permute-start.1
  23.8 1.0 copy.32
  25.1 0.7 copy-done.6
  25.8 1.2 pad_maximum_fusion.1
  27.0 1.5 copy.31
  28.6 1.1 pad_maximum_fusion
  29.7 1.6 copy.30
  31.3 4.4 %fusion.118 = (f32[16,128]{1,0:T(8,128)S(1)}, f32[16,128,384]{1,2,0:T(8,128)}) fusion(pred[128,384]{0,1:T(8,128)(4,1)S(1)} %broadcast_compare_fusion, bf16[384,16,104]{0,2,1:T(8,128)(2,1)} %bitcast.33, bf16[128,16,104]{0,2,1:T(8,128)(2,1)} %bitcast.36), kind=kOutput, calls=%fused_computation.159 | convolution fusion | flops 166723968 | bytes 4907008 | tf_op jit(solution)/shard_map/sub | solution.py:70
  35.7 2.5 fusion.52
  38.2 0.3 copy.34
  38.7 0.3 multiply_reduce_fusion
  39.0 1.0 multiply_convert_fusion
  40.0 0.2 reduce-scatter.2.cloned.1.call-start
  40.2 74.5 %all-gather.2.cloned.1.call-done = bf16[4096,1664]{1,0:T(8,128)(2,1)} async-done(((bf16[128,1664]{1,0:T(8,128)(2,1)}), bf16[4096,1664]{1,0:T(8,128)(2,1)}) %all-gather.2.cloned.1.call-update) | async-done | bytes 13631504 | tf_op jit(solution)/shard_map/all_gather | solution.py:78
  114.7 27.8 %convolution_convert_fusion = bf16[4096,1664]{1,0:T(8,128)(2,1)} fusion(bf16[256,1664]{1,0:T(8,128)(2,1)S(1)} %copy-done, bf16[4096,1664]{1,0:T(8,128)(2,1)} %all-gather.2.cloned.1.call-done, bf16[1664,256]{1,0:T(8,128)(2,1)S(1)} %copy-done.14, f32[256]{0:T(256)S(1)} %copy-done.15), kind=kOutput, calls=%fused_computation.3 | convolution fusion | flops 7055343616 | bytes 28967936 | tf_op jit(solution)/shard_map/dot_general | solution.py:86
  142.6 0.6 copy-done.13
  143.6 105.9 %reduce-scatter.2.cloned.1.call-done = bf16[128,1664]{1,0:T(8,128)(2,1)} async-done(((bf16[4096,1664]{1,0:T(8,128)(2,1)}), bf16[128,1664]{1,0:T(8,128)(2,1)}) %reduce-scatter.2.cloned.1.call-update) | async-done | bytes 426000 | tf_op jit(solution)/shard_map/reduce_scatter | solution.py:85
  249.4 1.1 convert_add_fusion
  250.6 0.2 reshape.147
  250.8 0.5 reduce_sum.87
  251.5 0.2 multiply_reduce_fusion.1
  251.7 3.8 %convolution_convert_fusion.1 = bf16[4,32,1664]{2,1,0:T(8,128)(2,1)S(1)} fusion(bf16[1664,1664]{1,0:T(8,128)(2,1)} %param.34, f32[32,1664]{1,0:T(8,128)S(1)} %reduce_sum.87, f32[1664]{0:T(1024)S(1)} %copy-done.11, f32[1664]{0:T(1024)S(1)} %copy-done.12, f32[32]{0:T(128)S(1)} %add_rsqrt_fusion, f32[32]{0:T(128)S(1)} %broadcast_multiply_fusion, ...), kind=kOutput, calls=%fused_computation.27 | convolution fusion | flops 191483904 | bytes 6198144 | tf_op jit(solution)/shard_map/osm,md->osd/dot_general | solution.py:105
  255.5 11.6 %all_to_all.5 = bf16[4,32,1664]{2,1,0:T(8,128)(2,1)S(1)} all-to-all(bf16[4,32,1664]{2,1,0:T(8,128)(2,1)S(1)} %convolution_convert_fusion.1), channel_id=1, replica_groups=mesh['blk'=32,'tok'=4] {'tok'}, dimensions={0} | all-to-all | bytes 851968 | tf_op jit(solution)/shard_map/all_to_all | solution.py:108
  267.1 0.8 copy.40
  (57 shorter events, 1.3 us)
Async XLA Ops:
  7.2 107.6 %copy-start = (bf16[256,1664]{1,0:T(8,128)(2,1)S(1)}, bf16[256,1664]{1,0:T(8,128)(2,1)}, u32[]{:S(2)}) copy-start(bf16[256,1664]{1,0:T(8,128)(2,1)} %param.31) | copy-start | bytes 2555908
  7.2 16.6 %copy-start.7 = (bf16[128,1664]{1,0:T(8,128)(2,1)S(1)}, bf16[128,1664]{1,0:T(8,128)(2,1)}, u32[]{:S(2)}) copy-start(bf16[128,1664]{1,0:T(8,128)(2,1)} %param.19) | copy-start | bytes 1277956
  7.2 6.4 %copy-start.3 = (bf16[128,1664]{1,0:T(8,128)(2,1)S(1)}, bf16[128,1664]{1,0:T(8,128)(2,1)}, u32[]{:S(2)}) copy-start(bf16[128,1664]{1,0:T(8,128)(2,1)} %param.20) | copy-start | bytes 1277956
  7.2 10.0 %copy-start.5 = (bf16[128,1664]{1,0:T(8,128)(2,1)S(1)}, bf16[128,1664]{1,0:T(8,128)(2,1)}, u32[]{:S(2)}) copy-start(bf16[128,1664]{1,0:T(8,128)(2,1)} %param.21) | copy-start | bytes 1277956
  7.2 107.5 %all-gather.2.cloned.1.call-start = ((), (), s32[]{:S(2)}) async-start(), calls=%async_computation.2 | async-start | bytes 14057472 | tf_op jit(solution)/shard_map/all_gather | solution.py:78
  7.3 17.5 %copy-start.9 = (s32[4096]{0:T(1024)S(1)}, s32[4096]{0:T(1024)}, u32[]{:S(2)}) copy-start(s32[4096]{0:T(1024)} %param.22) | copy-start | bytes 49156
  14.5 15.2 %copy-start.2 = (bf16[128,1664]{1,0:T(8,128)(2,1)}, bf16[128,1664]{1,0:T(8,128)(2,1)S(1)}, u32[]{:S(2)}) copy-start(bf16[128,1664]{1,0:T(8,128)(2,1)S(1)} %scatter_fusion) | copy-start | bytes 1277956
  14.5 10.5 %collective-permute-start.2 = (bf16[128,1664]{1,0:T(8,128)(2,1)S(1)}, bf16[128,1664]{1,0:T(8,128)(2,1)S(1)}, u32[]{:S(2)}, u32[]{:S(2)}) collective-permute-start(bf16[128,1664]{1,0:T(8,128)(2,1)S(1)} %scatter_fusion), channel_id=1, source_target_pairs={{0,4},{4,8},{8,12},{12,16},{16,20},{20,24},{24,28},{28,32},{32,36}... | collective-permute-start | bytes 1277960 | tf_op jit(solution)/shard_map/ppermute | solution.py:12
  15.9 9.9 %collective-permute-start.3 = (bf16[128,1664]{1,0:T(8,128)(2,1)S(1)}, bf16[128,1664]{1,0:T(8,128)(2,1)}, u32[]{:S(2)}, u32[]{:S(2)}) collective-permute-start(bf16[128,1664]{1,0:T(8,128)(2,1)S(1)} %scatter_fusion), channel_id=1, source_target_pairs={{4,0},{8,4},{12,8},{16,12},{20,16},{24,20},{28,24},{32,28},{36,32}... | collective-permute-start | bytes 1277960 | tf_op jit(solution)/shard_map/ppermute | solution.py:12
  17.2 11.4 %collective-permute-start = (bf16[128,1664]{1,0:T(8,128)(2,1)S(1)}, bf16[128,1664]{1,0:T(8,128)(2,1)S(1)}, u32[]{:S(2)}, u32[]{:S(2)}) collective-permute-start(bf16[128,1664]{1,0:T(8,128)(2,1)S(1)} %copy-done.5), channel_id=1, source_target_pairs={{0,4},{4,8},{8,12},{12,16},{16,20},{20,24},{24,28},{28,32},{32,36}... | collective-permute-start | bytes 1277960 | tf_op jit(solution)/shard_map/ppermute | solution.py:12
  22.4 6.1 %collective-permute-start.1 = (bf16[128,1664]{1,0:T(8,128)(2,1)S(1)}, bf16[128,1664]{1,0:T(8,128)(2,1)}, u32[]{:S(2)}, u32[]{:S(2)}) collective-permute-start(bf16[128,1664]{1,0:T(8,128)(2,1)S(1)} %copy-done.5), channel_id=1, source_target_pairs={{4,0},{8,4},{12,8},{16,12},{20,16},{24,20},{28,24},{32,28},{36,32}... | collective-permute-start | bytes 1277960 | tf_op jit(solution)/shard_map/ppermute | solution.py:12
  25.0 0.8 copy-start.6
  31.3 4.4 %copy-start.4 = (bf16[384,1664]{0,1:T(8,128)(2,1)S(1)}, bf16[384,1664]{0,1:T(8,128)(2,1)}, u32[]{:S(2)}) copy-start(bf16[384,1664]{0,1:T(8,128)(2,1)} %copy.30) | copy-start | bytes 3833860
  35.7 2.9 %copy-start.1 = (bf16[128,1664]{1,0:T(8,128)(2,1)S(1)}, bf16[128,1664]{1,0:T(8,128)(2,1)}, u32[]{:S(2)}) copy-start(bf16[128,1664]{1,0:T(8,128)(2,1)} %param.18) | copy-start | bytes 1277956
  38.2 0.8 copy-start.10
  38.2 76.5 %copy-start.15 = (f32[256]{0:T(256)S(1)}, f32[256]{0:T(256)}, u32[]{:S(2)}) copy-start(f32[256]{0:T(256)} %param.30) | copy-start | bytes 3076
  38.5 76.2 %copy-start.14 = (bf16[1664,256]{1,0:T(8,128)(2,1)S(1)}, bf16[1664,256]{1,0:T(8,128)(2,1)}, u32[]{:S(2)}) copy-start(bf16[1664,256]{1,0:T(8,128)(2,1)} %param.29) | copy-start | bytes 2555908
  40.0 209.4 %reduce-scatter.2.cloned.1.call-start = ((), (), s32[]{:S(2)}) async-start(), calls=%async_computation.3 | async-start | bytes 14057472 | tf_op jit(solution)/shard_map/reduce_scatter | solution.py:85
  142.6 0.7 copy-start.13
  143.2 108.1 %copy-start.8 = (f32[1664]{0:T(1024)S(1)}, f32[1664]{0:T(1024)}, u32[]{:S(2)}) copy-start(f32[1664]{0:T(1024)} %param.32) | copy-start | bytes 19972
  143.2 108.5 %copy-start.11 = (f32[1664]{0:T(1024)S(1)}, f32[1664]{0:T(1024)}, u32[]{:S(2)}) copy-start(f32[1664]{0:T(1024)} %param.35) | copy-start | bytes 19972
  143.2 108.5 %copy-start.12 = (f32[1664]{0:T(1024)S(1)}, f32[1664]{0:T(1024)}, u32[]{:S(2)}) copy-start(f32[1664]{0:T(1024)} %param.33) | copy-start | bytes 19972
Sparse Core Ops, SparseCore 0:
  40.1 74.5 all-gather.1
  142.7 106.6 reduce-scatter.1
where the time goes:
time: 275 us
  waiting for transfers between devices  180 us (65%)
  matrix products  42 us (15%)
  between operations  14.3 us (5%)
  blocking collectives  11.6 us (4%)
  local copies, waits for them, and re-layouts  9.54 us (3%)
  starting transfers between devices  9.43 us (3%)
  other arithmetic  7.38 us (3%)
    reduce_scatter x1, waiting for transfers between devices, body(): lax.psum_scatter(jnp.dot(group_units, w_proj, preferred_element_type=jnp....  106 us
    all_gather x1, waiting for transfers between devices, body(): lax.all_gather(normed, 'blk', axis=0, tiled=True)  74.5 us
    dot_general x1, matrix products, body(): jnp.dot(group_units, w_proj, preferred_element_type=jnp.float32)  27.8 us
    all_to_all x1, blocking collectives, body(): lax.all_to_all(outgoing, 'tok', split_axis=0, concat_axis=0, tiled=True)  11.6 us
    ppermute x4, starting transfers between devices, passed_along(): return lax.ppermute(block, axis, route)  9.17 us
  transfers between devices with their start and end apart: 6, of which 2 were waited for; matrix products, arithmetic and copies ran while one was open for 2% of the time, Pallas kernels for 0%

commit v1 on v0

v1 whole, which is shorter than its diff:
```python
import jax
import jax.numpy as jnp
from jax import lax
from jax.sharding import Mesh
from jax.sharding import PartitionSpec as P

HEADS = 16
ROWS = ("tok", "x", "z", "c")


def passed_along(block, axes, distance):
    count = 1
    for axis in axes:
        count *= lax.axis_size(axis)
    route = [(i - distance, i) for i in range(count) if 0 <= i - distance < count]
    return lax.ppermute(block, axes, route)


def layer_norm(values, gain):
    center = values - jnp.mean(values, axis=-1, keepdims=True)
    spread = jnp.mean(center * center, axis=-1, keepdims=True)
    return center * lax.rsqrt(spread + 1e-06) * gain


def body(
    stream,
    queries,
    key_cache,
    value_cache,
    segments,
    stale_rows,
    owners,
    attn_gain,
    w_key,
    key_bias,
    mlp_gain,
    w_fc,
    b_fc,
    w_proj,
    b_proj,
    merge_gain,
    w_merge,
    b_merge,
):
    row_count = stream.shape[0]
    model_width = stream.shape[1]
    head_size = model_width // HEADS
    tok_count = lax.axis_size("tok")
    x_count = lax.axis_size("x")
    tok = lax.axis_index("tok")
    units_here = w_fc.shape[1]

    fc_part = model_width // tok_count
    fc_piece = lax.dynamic_slice_in_dim(w_fc, tok * fc_part, fc_part, 0)
    fc_all = lax.all_gather(fc_piece, ("x", "tok"), axis=0, tiled=True)
    fc_all = fc_all.reshape(x_count, model_width, units_here)
    proj_part = units_here // tok_count
    proj_piece = lax.dynamic_slice_in_dim(w_proj, tok * proj_part, proj_part, 0)
    proj_all = lax.all_gather(proj_piece, ("x", "tok"), axis=0, tiled=True)
    bias_all = lax.all_gather(b_fc, "x", axis=0, tiled=True)

    local_rows = stale_rows % row_count
    held = layer_norm(stream[local_rows].astype(jnp.float32), attn_gain).astype(jnp.bfloat16)
    fresh_keys = (jnp.dot(held, w_key, preferred_element_type=jnp.float32) + key_bias).astype(
        jnp.bfloat16
    )
    refreshed = key_cache.at[local_rows].set(fresh_keys)
    blk = ("x", "z", "c")
    below = passed_along((refreshed, value_cache), blk, 1)
    above = passed_along((refreshed, value_cache), blk, -1)
    key_window = jnp.concatenate([below[0], refreshed, above[0]], axis=0).reshape(
        3 * row_count, HEADS, head_size
    )
    value_window = jnp.concatenate([below[1], value_cache, above[1]], axis=0).reshape(
        3 * row_count, HEADS, head_size
    )
    position = lax.axis_index(blk)
    minus_ones = jnp.full((row_count,), -1, jnp.int32)
    seg_padded = jnp.concatenate([minus_ones, segments, minus_ones], axis=0)
    key_seg = lax.dynamic_slice_in_dim(seg_padded, position * row_count, 3 * row_count, 0)
    query_seg = lax.dynamic_slice_in_dim(segments, position * row_count, row_count, 0)
    query_heads = queries.reshape(row_count, HEADS, head_size)
    scores = jnp.einsum(
        "qhd,khd->hqk", query_heads, key_window, preferred_element_type=jnp.float32
    ) * (1.0 / head_size**0.5)
    allowed = (query_seg[:, None] == key_seg[None, :])[None]
    scores = jnp.where(allowed, scores, -jnp.inf)
    top_score = jnp.max(scores, axis=-1, keepdims=True)
    weights = jnp.exp(scores - top_score)
    probs = (weights / jnp.sum(weights, axis=-1, keepdims=True)).astype(jnp.bfloat16)
    attended = jnp.einsum("hqk,khd->qhd", probs, value_window, preferred_element_type=jnp.float32)
    attended = attended.reshape(row_count, model_width).astype(jnp.bfloat16)
    mixed = stream.astype(jnp.float32) + attended.astype(jnp.float32)
    normed = layer_norm(mixed, mlp_gain).astype(jnp.bfloat16)

    rows = lax.all_gather(normed, ("z", "c"), axis=0, tiled=True)
    group_rows = rows.shape[0]
    pooled_units = []
    for i in range(x_count):
        bias = lax.slice_in_dim(bias_all, i * units_here, (i + 1) * units_here)
        units = jax.nn.gelu(
            jnp.dot(rows, fc_all[i], preferred_element_type=jnp.float32) + bias,
            approximate=False,
        ).astype(jnp.bfloat16)
        pooled_units.append(
            jnp.mean(units.astype(jnp.float32).reshape(group_rows // 4, 4, units_here), axis=1)
        )
    pooled_units = jnp.concatenate(pooled_units, axis=1).astype(jnp.bfloat16)
    partial = jnp.dot(pooled_units, proj_all, preferred_element_type=jnp.float32)
    summed = lax.psum_scatter(
        partial.astype(jnp.bfloat16), ("z", "c"), scatter_dimension=0, tiled=True
    ).astype(jnp.float32)
    pooled = jnp.mean(mixed.reshape(row_count // 4, 4, model_width), axis=1) + summed + b_proj
    merge_in = layer_norm(pooled, merge_gain).astype(jnp.bfloat16)
    merged = (jnp.dot(merge_in, w_merge, preferred_element_type=jnp.float32) + b_merge).astype(
        jnp.bfloat16
    )
    merged_rows = row_count // 4
    owner_hot = (owners[:, None] == jnp.arange(tok_count, dtype=jnp.int32)[None, :]).astype(
        jnp.int32
    )
    ranking = jnp.sum(jnp.cumsum(owner_hot, axis=0) * owner_hot, axis=-1) - 1
    selector = (
        owners[None, None, :] == jnp.arange(tok_count, dtype=jnp.int32)[:, None, None]
    ) & (ranking[None, None, :] == jnp.arange(merged_rows, dtype=jnp.int32)[None, :, None])
    outgoing = jnp.einsum(
        "osm,md->osd", selector.astype(jnp.bfloat16), merged, preferred_element_type=jnp.float32
    ).astype(jnp.bfloat16)
    arrived = lax.all_to_all(outgoing, "tok", split_axis=0, concat_axis=0, tiled=True)
    delivered = arrived.reshape(1, 1, tok_count * merged_rows, model_width)
    return (refreshed, delivered)


def solution(mesh):
    fine = Mesh(mesh.devices.reshape(4, 4, 2, 4), ("x", "z", "c", "tok"))
    blk = ("x", "z", "c")
    return jax.shard_map(
        body,
        mesh=fine,
        in_specs=(
            P(ROWS, None),
            P(ROWS, None),
            P(ROWS, None),
            P(ROWS, None),
            P("tok"),
            P(ROWS),
            P(ROWS),
            P(),
            P(),
            P(),
            P(),
            P(None, blk),
            P(blk),
            P(blk, None),
            P(),
            P(),
            P(),
            P(),
        ),
        out_specs=(P(ROWS, None), P("tok", blk, None, None)),
        check_vma=False,
    )
```

time: 275 us -> 203 us (0.74)
  waiting for transfers between devices: 180 us -> 71.1 us
  blocking collectives: 11.6 us -> 28 us
  local copies, waits for them, and re-layouts: 9.54 us -> 20.7 us
  other arithmetic: 7.38 us -> 13.6 us
    reduce_scatter x1, waiting for transfers between devices: 106 us -> 29.6 us  [body(): lax.psum_scatter(partial.astype(jnp.bfloat16), ('z', 'c'), scatter_dimens...]
    all_gather x1 -> x3, waiting for transfers between devices: 74.5 us -> 41.4 us  [the longest x1 28.6 us: body(): rows = lax.all_gather(normed, ('z', 'c'), axis=0, tiled=True)]
    all_gather x0 -> x1, blocking collectives: none -> 16.4 us  [body(): bias_all = lax.all_gather(b_fc, 'x', axis=0, tiled=True)]
    reshape x1 -> x5, local copies, waits for them, and re-layouts: 0.25 us -> 7.32 us  [the longest x4 7.08 us: body(): units.astype(jnp.float32).reshape(group_rows // 4, 4, units_here)]
    reduce_sum x1 -> x5, other arithmetic: 0.5 us -> 4.96 us  [the longest x4 4.46 us: body(): jnp.mean(units.astype(jnp.float32).reshape(group_rows // 4, 4, units_here...]
    dot_general x1 -> x5, matrix products: 27.8 us -> 29.3 us  [the longest x4 25.3 us: body(): jnp.dot(rows, fc_all[i], preferred_element_type=jnp.float32) + bias]
  transfers between devices with their start and end apart: 6 -> 8, of which waited for: 2 -> 3; matrix products, arithmetic and copies ran while one was open for 2% -> 32% of each run, Pallas kernels for 0% -> 0%
where the time goes in v1:
time: 203 us; the launch traced here: 202 us
  waiting for transfers between devices  71.1 us (35%)
  matrix products  44.6 us (22%)
  blocking collectives  28 us (14%)
  local copies, waits for them, and re-layouts  20.7 us (10%)
  between operations  14.1 us (7%)
  other arithmetic  13.6 us (7%)
  starting transfers between devices  10.1 us (5%)
    reduce_scatter x1, waiting for transfers between devices, body(): lax.psum_scatter(partial.astype(jnp.bfloat16), ('z', 'c'), scatter_dimens...  29.6 us
    all_gather x1, waiting for transfers between devices, body(): rows = lax.all_gather(normed, ('z', 'c'), axis=0, tiled=True)  28.6 us
    dot_general x4, matrix products, body(): jnp.dot(rows, fc_all[i], preferred_element_type=jnp.float32) + bias  25.3 us
    all_gather x1, blocking collectives, body(): bias_all = lax.all_gather(b_fc, 'x', axis=0, tiled=True)  16.4 us
    all_gather x1, waiting for transfers between devices, body(): proj_all = lax.all_gather(proj_piece, ('x', 'tok'), axis=0, tiled=True)  12.8 us
    all_to_all x1, blocking collectives, body(): lax.all_to_all(outgoing, 'tok', split_axis=0, concat_axis=0, tiled=True)  11.6 us
    ppermute x4, starting transfers between devices, passed_along(): return lax.ppermute(block, axes, route)  9.96 us
    reshape x4, local copies, waits for them, and re-layouts, body(): units.astype(jnp.float32).reshape(group_rows // 4, 4, units_here)  7.08 us
  transfers between devices with their start and end apart: 8, of which 3 were waited for; matrix products, arithmetic and copies ran while one was open for 32% of the time, Pallas kernels for 0%

profile of v1, /device:TPU:0, one launch (start us, length us, event | category | flops | bytes accessed | tf_op | source)
XLA Modules:
  0.0 202.1 jit_solution(1446879762778651455)
XLA Ops:
  9.8 1.7 gather_fusion
  11.9 3.5 %fusion.4 = bf16[12,1664]{1,0:T(8,128)(2,1)S(1)} fusion(bf16[1664,1664]{1,0:T(8,128)(2,1)} %param.26, bf16[12,1664]{1,0:T(8,128)(2,1)S(1)} %gather_fusion, f32[1664]{0:T(1024)} %param.27, f32[1664]{0:T(1024)} %param.25, f32[12]{0:T(128)S(1)} %add_rsqrt_fusion.2, f32[12]{0:T(128)S(1)} %broadcast_multiply_fusion.2), kind=kOutput, calls=%fused_computation.13 | convolution fusion | flops 66593280 | bytes 5631072 | tf_op jit(solution)/shard_map/dot_general | solution.py:64
  16.4 1.3 collective-permute-start.2
  17.7 1.3 collective-permute-start.3
  19.0 6.1 %collective-permute-start = (bf16[128,1664]{1,0:T(8,128)(2,1)S(1)}, bf16[128,1664]{1,0:T(8,128)(2,1)}, u32[]{:S(2)}, u32[]{:S(2)}) collective-permute-start(bf16[128,1664]{1,0:T(8,128)(2,1)S(1)} %copy-done.5), channel_id=1, source_target_pairs={{0,4},{4,8},{8,12},{12,16},{16,20},{20,24},{24,28},{28,32},{32,36}... | collective-permute-start | bytes 1277960 | tf_op jit(solution)/shard_map/ppermute | solution.py:16
  25.1 1.3 collective-permute-start.1
  28.5 1.2 pad_maximum_fusion.1
  29.7 1.6 copy.31
  31.3 1.2 pad_maximum_fusion
  32.5 1.6 copy.30
  34.1 4.4 %fusion.99 = (f32[16,128]{1,0:T(8,128)S(1)}, f32[16,128,384]{1,2,0:T(8,128)}) fusion(pred[128,384]{0,1:T(8,128)(4,1)S(1)} %broadcast_compare_fusion, bf16[384,16,104]{0,2,1:T(8,128)(2,1)} %bitcast.40, bf16[128,16,104]{0,2,1:T(8,128)(2,1)} %bitcast.43), kind=kOutput, calls=%fused_computation.178 | convolution fusion | flops 166723968 | bytes 4907008 | tf_op jit(solution)/shard_map/sub | solution.py:89
  38.5 3.5 %fusion.10 = f32[16,104,128]{2,1,0:T(8,128)} fusion(bf16[384,16,104]{0,2,1:T(8,128)(2,1)S(1)} %bitcast.41, f32[16,128,384]{1,2,0:T(8,128)} %get-tuple-element.9, f32[16,128]{1,0:T(8,128)S(1)} %get-tuple-element.8), kind=kOutput, calls=%fused_computation.29 | convolution fusion | flops 165576704 | bytes 5283840 | tf_op jit(solution)/shard_map/hqk,khd->qhd/dot_general | solution.py:91
  42.0 1.5 copy.34
  45.0 1.6 constant_dynamic-slice_fusion
  46.7 16.4 %all-gather = f32[4,1,256]{2,1,0:T(1,128)S(1)} all-gather(f32[1,1,256]{2,1,0:T(1,128)S(1)} %bitcast.44), channel_id=1, replica_groups=mesh['x'=4,'z'=4,'c'=2,'tok'=4] {'x'}, dimensions={0}, use_global_device_ids=true | all-gather | bytes 5120 | tf_op jit(solution)/shard_map/all_gather | solution.py:60
  63.0 28.6 %all-gather.5.cloned.1.call-done = bf16[1024,1664]{1,0:T(8,128)(2,1)} async-done(((bf16[128,1664]{1,0:T(8,128)(2,1)}), bf16[1024,1664]{1,0:T(8,128)(2,1)}) %all-gather.5.cloned.1.call-update) | async-done | bytes 3407888 | tf_op jit(solution)/shard_map/all_gather | solution.py:96
  91.7 6.3 %fusion.54 = f32[1024,256]{1,0:T(8,128)} fusion(bf16[1024,1664]{1,0:T(8,128)(2,1)} %all-gather.5.cloned.1.call-done, bf16[6656,256]{1,0:T(8,128)(2,1)} %all-gather.7.cloned.1.call-done, f32[256]{0:T(256)S(1)} %bitcast.48), kind=kOutput, calls=%fused_computation.105 | convolution fusion | flops 889978880 | bytes 5309440 | tf_op jit(solution)/shard_map/dot_general | solution.py:102
  97.9 1.5 reshape.195
  99.4 6.3 %fusion.52 = f32[1024,256]{1,0:T(8,128)} fusion(bf16[1024,1664]{1,0:T(8,128)(2,1)} %all-gather.5.cloned.1.call-done, bf16[6656,256]{1,0:T(8,128)(2,1)} %all-gather.7.cloned.1.call-done, f32[256]{0:T(256)S(1)} %bitcast.47), kind=kOutput, calls=%fused_computation.102 | convolution fusion | flops 889978880 | bytes 5309440 | tf_op jit(solution)/shard_map/dot_general | solution.py:102
  105.7 2.5 %reshape.197 = f32[256,4,256]{2,1,0:T(4,128)} reshape(f32[1024,256]{1,0:T(8,128)} %fusion.52) | data formatting | bytes 2097152 | tf_op jit(solution)/shard_map/reshape | solution.py:106
  108.8 1.9 reduce_sum.125
  110.7 6.3 %fusion.50 = f32[1024,256]{1,0:T(8,128)} fusion(bf16[1024,1664]{1,0:T(8,128)(2,1)} %all-gather.5.cloned.1.call-done, bf16[6656,256]{1,0:T(8,128)(2,1)} %all-gather.7.cloned.1.call-done, f32[256]{0:T(256)S(1)} %bitcast.46), kind=kOutput, calls=%fused_computation.99 | convolution fusion | flops 889978880 | bytes 5309440 | tf_op jit(solution)/shard_map/dot_general | solution.py:102
  117.0 1.5 reshape.199
  119.1 6.5 %fusion.48 = f32[1024,256]{1,0:T(8,128)} fusion(bf16[1024,1664]{1,0:T(8,128)(2,1)} %all-gather.5.cloned.1.call-done, bf16[6656,256]{1,0:T(8,128)(2,1)} %all-gather.7.cloned.1.call-done, f32[256]{0:T(256)S(1)} %bitcast.45), kind=kOutput, calls=%fused_computation.96 | convolution fusion | flops 889978880 | bytes 5309440 | tf_op jit(solution)/shard_map/dot_general | solution.py:102
  125.6 1.5 reshape.201
  127.1 1.4 reduce_sum.127
  129.5 12.8 %all-gather.9.cloned.1.call-done = bf16[1024,1664]{1,0:T(8,128)(2,1)} async-done(((bf16[64,1664]{1,0:T(8,128)(2,1)}), bf16[1024,1664]{1,0:T(8,128)(2,1)}) %all-gather.9.cloned.1.call-update) | async-done | bytes 3407888 | tf_op jit(solution)/shard_map/all_gather | solution.py:59
  142.3 4.0 %convolution_convert_fusion = bf16[256,1664]{1,0:T(8,128)(2,1)} fusion(bf16[1024,1664]{1,0:T(8,128)(2,1)} %all-gather.9.cloned.1.call-done, bf16[256,256]{1,0:T(8,128)(2,1)S(1)} %get-tuple-element.10, bf16[256,256]{1,0:T(8,128)(2,1)S(1)} %get-tuple-element.11, bf16[256,256]{1,0:T(8,128)(2,1)S(1)} %get-tuple-element.12, ...), kind=kOutput, calls=%fused_computation.6 | convolution fusion | flops 874938368 | bytes 4784128 | tf_op jit(solution)/shard_map/dot_general | solution.py:109
  147.4 29.6 %reduce-scatter.2.cloned.1.call-done = bf16[32,1664]{1,0:T(8,128)(2,1)} async-done(((bf16[256,1664]{1,0:T(8,128)(2,1)}), bf16[32,1664]{1,0:T(8,128)(2,1)}) %reduce-scatter.2.cloned.1.call-update) | async-done | bytes 106512 | tf_op jit(solution)/shard_map/reduce_scatter | solution.py:110
  178.1 1.1 multiply_reduce_fusion.1
  179.3 3.9 %convolution_convert_fusion.1 = bf16[4,32,1664]{2,1,0:T(8,128)(2,1)S(1)} fusion(bf16[1664,1664]{1,0:T(8,128)(2,1)} %param.34, f32[1664]{0:T(1024)S(1)} %copy-done.11, f32[1664]{0:T(1024)S(1)} %copy-done.12, f32[32]{0:T(128)S(1)} %add_rsqrt_fusion, f32[32]{0:T(128)S(1)} %broadcast_multiply_fusion, pred[32,32]{1,0:T(8,128)(4,1)S(1)} %iota_compare_fusion, ...), kind=kOutput, calls=%fused_computation.7 | convolution fusion | flops 191590400 | bytes 6304640 | tf_op jit(solution)/shard_map/osm,md->osd/dot_general | solution.py:126
  183.1 11.6 %all_to_all.5 = bf16[4,32,1664]{2,1,0:T(8,128)(2,1)S(1)} all-to-all(bf16[4,32,1664]{2,1,0:T(8,128)(2,1)S(1)} %convolution_convert_fusion.1), channel_id=1, replica_groups=mesh['x'=4,'z'=4,'c'=2,'tok'=4] {'tok'}, dimensions={0} | all-to-all | bytes 851968 | tf_op jit(solution)/shard_map/all_to_all | solution.py:129
  (78 shorter events, 12.6 us)
Async XLA Ops:
  7.2 1.2 copy-start
  7.2 55.9 %all-gather.7.cloned.1.call-start = ((), (), s32[]{:S(2)}) async-start(), calls=%async_computation.3 | async-start | bytes 3620864 | tf_op jit(solution)/shard_map/all_gather | solution.py:55
  9.1 6.4 %copy-start.2 = (bf16[128,1664]{1,0:T(8,128)(2,1)S(1)}, bf16[128,1664]{1,0:T(8,128)(2,1)}, u32[]{:S(2)}) copy-start(bf16[128,1664]{1,0:T(8,128)(2,1)} %param.20) | copy-start | bytes 1277956
  9.1 82.6 %all-gather.5.cloned.1.call-start = ((), (), s32[]{:S(2)}) async-start(), calls=%async_computation.2 | async-start | bytes 3833856 | tf_op jit(solution)/shard_map/all_gather | solution.py:96
  11.9 7.2 %copy-start.5 = (bf16[128,1664]{1,0:T(8,128)(2,1)S(1)}, bf16[128,1664]{1,0:T(8,128)(2,1)}, u32[]{:S(2)}) copy-start(bf16[128,1664]{1,0:T(8,128)(2,1)} %param.21) | copy-start | bytes 1277956
  11.9 14.5 %copy-start.7 = (bf16[128,1664]{1,0:T(8,128)(2,1)S(1)}, bf16[128,1664]{1,0:T(8,128)(2,1)}, u32[]{:S(2)}) copy-start(bf16[128,1664]{1,0:T(8,128)(2,1)} %param.19) | copy-start | bytes 1277956
  11.9 15.5 %copy-start.9 = (s32[4096]{0:T(1024)S(1)}, s32[4096]{0:T(1024)}, u32[]{:S(2)}) copy-start(s32[4096]{0:T(1024)} %param.22) | copy-start | bytes 49156
  16.4 16.1 %copy-start.1 = (bf16[128,1664]{1,0:T(8,128)(2,1)}, bf16[128,1664]{1,0:T(8,128)(2,1)S(1)}, u32[]{:S(2)}) copy-start(bf16[128,1664]{1,0:T(8,128)(2,1)S(1)} %scatter_fusion) | copy-start | bytes 1277956
  16.4 11.3 %collective-permute-start.2 = (bf16[128,1664]{1,0:T(8,128)(2,1)S(1)}, bf16[128,1664]{1,0:T(8,128)(2,1)S(1)}, u32[]{:S(2)}, u32[]{:S(2)}) collective-permute-start(bf16[128,1664]{1,0:T(8,128)(2,1)S(1)} %scatter_fusion), channel_id=1, source_target_pairs={{0,4},{4,8},{8,12},{12,16},{16,20},{20,24},{24,28},{28,32},{32,36}... | collective-permute-start | bytes 1277960 | tf_op jit(solution)/shard_map/ppermute | solution.py:16
  17.7 10.7 %collective-permute-start.3 = (bf16[128,1664]{1,0:T(8,128)(2,1)S(1)}, bf16[128,1664]{1,0:T(8,128)(2,1)}, u32[]{:S(2)}, u32[]{:S(2)}) collective-permute-start(bf16[128,1664]{1,0:T(8,128)(2,1)S(1)} %scatter_fusion), channel_id=1, source_target_pairs={{4,0},{8,4},{12,8},{16,12},{20,16},{24,20},{28,24},{32,28},{36,32}... | collective-permute-start | bytes 1277960 | tf_op jit(solution)/shard_map/ppermute | solution.py:16
  19.0 12.2 %collective-permute-start = (bf16[128,1664]{1,0:T(8,128)(2,1)S(1)}, bf16[128,1664]{1,0:T(8,128)(2,1)}, u32[]{:S(2)}, u32[]{:S(2)}) collective-permute-start(bf16[128,1664]{1,0:T(8,128)(2,1)S(1)} %copy-done.5), channel_id=1, source_target_pairs={{0,4},{4,8},{8,12},{12,16},{16,20},{20,24},{24,28},{28,32},{32,36}... | collective-permute-start | bytes 1277960 | tf_op jit(solution)/shard_map/ppermute | solution.py:16
  25.1 6.2 %collective-permute-start.1 = (bf16[128,1664]{1,0:T(8,128)(2,1)S(1)}, bf16[128,1664]{1,0:T(8,128)(2,1)}, u32[]{:S(2)}, u32[]{:S(2)}) collective-permute-start(bf16[128,1664]{1,0:T(8,128)(2,1)S(1)} %copy-done.5), channel_id=1, source_target_pairs={{4,0},{8,4},{12,8},{16,12},{20,16},{24,20},{28,24},{32,28},{36,32}... | collective-permute-start | bytes 1277960 | tf_op jit(solution)/shard_map/ppermute | solution.py:16
  27.7 0.8 copy-start.6
  34.1 4.4 %copy-start.4 = (bf16[384,1664]{0,1:T(8,128)(2,1)S(1)}, bf16[384,1664]{0,1:T(8,128)(2,1)}, u32[]{:S(2)}) copy-start(bf16[384,1664]{0,1:T(8,128)(2,1)} %copy.30) | copy-start | bytes 3833860
  38.5 5.0 %copy-start.3 = (bf16[128,1664]{1,0:T(8,128)(2,1)S(1)}, bf16[128,1664]{1,0:T(8,128)(2,1)}, u32[]{:S(2)}) copy-start(bf16[128,1664]{1,0:T(8,128)(2,1)} %param.18) | copy-start | bytes 1277956
  42.0 1.9 copy-start.10
  42.0 4.7 %copy-start.14 = (f32[256]{0:T(256)S(1)}, f32[256]{0:T(256)}, u32[]{:S(2)}) copy-start(f32[256]{0:T(256)} %param.30) | copy-start | bytes 3076
  44.9 97.4 %all-gather.9.cloned.1.call-start = ((), (), s32[]{:S(2)}) async-start(), calls=%async_computation.4 | async-start | bytes 3620864 | tf_op jit(solution)/shard_map/all_gather | solution.py:59
  46.6 130.4 %reduce-scatter.2.cloned.1.call-start = ((), (), s32[]{:S(2)}) async-start(), calls=%async_computation.5 | async-start | bytes 958464 | tf_op jit(solution)/shard_map/reduce_scatter | solution.py:110
  142.3 4.0 %copy-start.13 = (s32[32]{0:T(128)S(1)}, s32[32]{0:T(128)}, u32[]{:S(2)}) copy-start(s32[32]{0:T(128)} %param.24) | copy-start | bytes 388
  146.3 30.8 %copy-start.8 = (f32[1664]{0:T(1024)S(1)}, f32[1664]{0:T(1024)}, u32[]{:S(2)}) copy-start(f32[1664]{0:T(1024)} %param.32) | copy-start | bytes 19972
  146.3 32.9 %copy-start.11 = (f32[1664]{0:T(1024)S(1)}, f32[1664]{0:T(1024)}, u32[]{:S(2)}) copy-start(f32[1664]{0:T(1024)} %param.35) | copy-start | bytes 19972
  146.3 32.9 %copy-start.12 = (f32[1664]{0:T(1024)S(1)}, f32[1664]{0:T(1024)}, u32[]{:S(2)}) copy-start(f32[1664]{0:T(1024)} %param.33) | copy-start | bytes 19972
Sparse Core Ops, SparseCore 0:
  10.2 51.1 all-gather.6
  63.7 27.9 all-gather.4
  93.8 48.3 all-gather.8
  146.4 30.5 reduce-scatter.1

commit v2 on v1

v2 whole, which is shorter than its diff:
```python
import jax
import jax.numpy as jnp
from jax import lax
from jax.experimental import pallas as pl
from jax.experimental.pallas import tpu as pltpu
from jax.sharding import Mesh
from jax.sharding import PartitionSpec as P

HEADS = 16
ROWS = ("tok", "x", "z", "c")
BLK = ("x", "z", "c")
FC_CUT = 768


def passed_along(block, distance):
    count = lax.axis_size("x") * lax.axis_size("z") * lax.axis_size("c")
    route = [(i - distance, i) for i in range(count) if 0 <= i - distance < count]
    return lax.ppermute(block, BLK, route)


def shift(block, axis, distance):
    count = lax.axis_size(axis)
    return lax.ppermute(block, axis, [(i, (i + distance) % count) for i in range(count)])


def layer_norm(values, gain):
    center = values - jnp.mean(values, axis=-1, keepdims=True)
    spread = jnp.mean(center * center, axis=-1, keepdims=True)
    return center * lax.rsqrt(spread + 1e-06) * gain


def three_terms(values):
    high = values.astype(jnp.bfloat16)
    rest = values - high.astype(jnp.float32)
    middle = rest.astype(jnp.bfloat16)
    low = (rest - middle.astype(jnp.float32)).astype(jnp.bfloat16)
    return jnp.stack([high, middle, low])


def dot(left, right):
    return jnp.dot(left, right, preferred_element_type=jnp.float32)


def iota(shape, axis):
    return lax.broadcasted_iota(jnp.int32, shape, axis)


def mean_of_fours(rows):
    hit = iota((rows // 4, rows), 1) // 4 == iota((rows // 4, rows), 0)
    return jnp.where(hit, 0.25, 0.0).astype(jnp.bfloat16)


def call(kernel, outs, name, flops, limit, *args):
    moved = sum(a.size * a.dtype.itemsize for a in args)
    return pl.pallas_call(
        kernel,
        out_shape=outs,
        in_specs=[pl.BlockSpec(memory_space=pltpu.VMEM) for _ in args],
        out_specs=jax.tree.map(lambda _: pl.BlockSpec(memory_space=pltpu.VMEM), outs),
        compiler_params=pltpu.CompilerParams(vmem_limit_bytes=limit << 20),
        cost_estimate=pl.CostEstimate(flops=flops, bytes_accessed=moved, transcendentals=0),
        name=name,
    )(*args)


def refresh_kernel(stream, keys, rows_col, rows_row, gain, w_key, key_bias, out):
    count = rows_col.shape[0]
    block = stream.shape[0]
    pick = jnp.where(rows_col[...] == iota((count, block), 1), 1.0, 0.0).astype(jnp.bfloat16)
    held = layer_norm(dot(pick, stream[...]), gain[...]).astype(jnp.bfloat16)
    fresh = (dot(held, w_key[...]) + key_bias[...]).astype(jnp.bfloat16)
    place = jnp.where(rows_row[...] == iota((block, count), 0), 1.0, 0.0)
    hit = jnp.sum(place, axis=1, keepdims=True) > 0.5
    spread = dot(place.astype(jnp.bfloat16), fresh)
    old = keys[...].astype(jnp.float32)
    out[...] = jnp.where(hit, spread, old).astype(jnp.bfloat16)


def attention_kernel(
    queries,
    keys_below,
    keys,
    keys_above,
    values_below,
    values,
    values_above,
    stream,
    seg_col,
    seg_row,
    gain,
    normed,
    mixed_mean,
    attended,
):
    rows, width = queries.shape
    size = width // HEADS
    allowed = seg_col[...] == seg_row[...]
    scale = 1.0 / size**0.5
    for h in range(HEADS):
        low = h * size // 128 * 128
        high = min(-(-(h + 1) * size // 128) * 128, width)
        lane = iota((1, high - low), 1) + low
        mine = (lane >= h * size) & (lane < (h + 1) * size)
        picked = jnp.where(mine, 1.0, 0.0).astype(jnp.bfloat16)
        query = queries[:, low:high] * picked
        key = jnp.concatenate(
            [keys_below[:, low:high], keys[:, low:high], keys_above[:, low:high]], axis=0
        )
        value = jnp.concatenate(
            [values_below[:, low:high], values[:, low:high], values_above[:, low:high]], axis=0
        )
        scores = lax.dot_general(
            query, key, (((1,), (1,)), ((), ())), preferred_element_type=jnp.float32
        )
        scores = jnp.where(allowed, scores * scale, -jnp.inf)
        weights = jnp.exp(scores - jnp.max(scores, axis=-1, keepdims=True))
        share = 1.0 / jnp.sum(weights, axis=-1, keepdims=True)
        found = dot((weights * share).astype(jnp.bfloat16), value)
        attended[:, low:high] = jnp.where(mine, found, attended[:, low:high])
    rounded = attended[...].astype(jnp.bfloat16)
    fours = mean_of_fours(rows)
    mixed_mean[...] = dot(fours, stream[...]) + dot(fours, rounded)
    mixed = stream[...].astype(jnp.float32) + rounded.astype(jnp.float32)
    normed[...] = layer_norm(mixed, gain[...]).astype(jnp.bfloat16)


def mlp_kernel(counts, here, *refs):
    row_refs = refs[: sum(counts)]
    own, left, right, far_a, far_b, proj = refs[sum(counts) : sum(counts) + 6]
    outs = refs[sum(counts) + 6 :]
    width = row_refs[0].shape[1]
    shards, depth, _ = proj.shape
    x = here[0]
    sides = []
    at = 0
    for count, out in zip(counts, outs):
        group = row_refs[at : at + count]
        at += count
        chunk, chunk_rows = [], 0
        done = 0
        for ref in group:
            chunk.append(ref)
            chunk_rows += ref.shape[0]
            if chunk_rows == 256 or ref is group[-1]:
                sides.append((tuple(chunk), chunk_rows, out, done))
                done += chunk_rows // 4
                chunk, chunk_rows = [], 0
    if len(sides) == 2 and sides[0][1] + sides[1][1] <= 256:
        passes = [sides]
    else:
        passes = [[side] for side in sides]
    for parts in passes:
        rows = jnp.concatenate([ref[...] for part in parts for ref in part[0]], axis=0)
        fours = mean_of_fours(rows.shape[0])
        total = None
        for number, (fc, step) in enumerate(
            ((own, 0), (left, shards - 1), (right, 1), (None, 2))
        ):
            if fc is not None:
                terms = fc[width : width + 16, :]
                units = dot(rows, fc[:width, :])
            else:
                rest = width - FC_CUT
                terms = far_b[rest : rest + 16, :]
                units = dot(rows[:, :FC_CUT], far_a[...]) + dot(rows[:, FC_CUT:], far_b[:rest, :])
            units = units + jnp.sum(terms.astype(jnp.float32), axis=0, keepdims=True)
            units = 0.5 * units * (1.0 + lax.erf(units * (0.5**0.5)))
            mean = dot(fours, units.astype(jnp.bfloat16)).astype(jnp.bfloat16)
            term = dot(mean, proj[lax.rem(x + step, shards)])
            total = term if total is None else total + term
        start = 0
        for _, count, out, done in parts:
            n = count // 4
            out[done : done + n, :] = total[start : start + n, :].astype(out.dtype)
            start += n


def pooled_parts(mine, other, weights, here, name):
    counts = (len(mine), len(other))
    rows_mine = sum(r.shape[0] for r in mine) // 4
    rows_other = sum(r.shape[0] for r in other) // 4
    width = mine[0].shape[1]
    units = weights[-1].shape[0] * weights[-1].shape[1]
    refs = [*mine, *other, *weights]
    flops = 2 * (rows_mine + rows_other) * 5 * width * units
    outs = (
        jax.ShapeDtypeStruct((rows_mine, width), jnp.float32),
        jax.ShapeDtypeStruct((rows_other, width), jnp.bfloat16),
    )
    return pl.pallas_call(
        lambda *r: mlp_kernel(counts, *r),
        out_shape=outs,
        in_specs=[pl.BlockSpec(memory_space=pltpu.SMEM)]
        + [pl.BlockSpec(memory_space=pltpu.VMEM) for _ in refs],
        out_specs=tuple(pl.BlockSpec(memory_space=pltpu.VMEM) for _ in outs),
        compiler_params=pltpu.CompilerParams(vmem_limit_bytes=24 << 20),
        cost_estimate=pl.CostEstimate(flops=flops, bytes_accessed=8 << 20, transcendentals=0),
        name=name,
    )(here, *refs)


def merge_kernel(
    own,
    other,
    from_low,
    from_high,
    from_far,
    mixed_mean,
    b_proj,
    gain,
    w_merge,
    b_merge,
    owner_col,
    owner_row,
    out,
):
    rows = own.shape[0]
    summed = own[...] + other[...].astype(jnp.float32)
    summed = summed + from_low[...].astype(jnp.float32)
    summed = summed + from_high[...].astype(jnp.float32)
    summed = summed + from_far[...].astype(jnp.float32)
    pooled = mixed_mean[...] + summed + b_proj[...]
    merge_in = layer_norm(pooled, gain[...]).astype(jnp.bfloat16)
    merged = (dot(merge_in, w_merge[...]) + b_merge[...]).astype(jnp.bfloat16)
    earlier = iota((rows, rows), 0) < iota((rows, rows), 1)
    same = owner_col[...] == owner_row[...]
    rank = jnp.sum(jnp.where(earlier & same, 1.0, 0.0), axis=0, keepdims=True).astype(jnp.int32)
    place = iota((out.shape[0], rows), 0)
    pick = (place // rows == owner_row[...]) & (place % rows == rank)
    out[...] = dot(jnp.where(pick, 1.0, 0.0).astype(jnp.bfloat16), merged).astype(jnp.bfloat16)


def attention(*args):
    rows, width = args[0].shape
    outs = (
        jax.ShapeDtypeStruct((rows, width), jnp.bfloat16),
        jax.ShapeDtypeStruct((rows // 4, width), jnp.float32),
    )
    return pl.pallas_call(
        attention_kernel,
        out_shape=outs,
        in_specs=[pl.BlockSpec(memory_space=pltpu.VMEM) for _ in args],
        out_specs=tuple(pl.BlockSpec(memory_space=pltpu.VMEM) for _ in outs),
        scratch_shapes=[pltpu.VMEM((rows, width), jnp.float32)],
        compiler_params=pltpu.CompilerParams(vmem_limit_bytes=16 << 20),
        cost_estimate=pl.CostEstimate(
            flops=24 * rows * rows * width, bytes_accessed=4 << 20, transcendentals=0
        ),
        name="attention",
    )(*args)


def body(
    stream,
    queries,
    key_cache,
    value_cache,
    segments,
    stale_rows,
    owners,
    attn_gain,
    w_key,
    key_bias,
    mlp_gain,
    w_fc,
    b_fc,
    w_proj,
    b_proj,
    merge_gain,
    w_merge,
    b_merge,
):
    row_count = stream.shape[0]
    model_width = stream.shape[1]
    tok_count = lax.axis_size("tok")
    x_count = lax.axis_size("x")
    tok = lax.axis_index("tok")
    here = lax.axis_index("x").astype(jnp.int32).reshape(1)
    units_here = w_fc.shape[1]

    below_values = passed_along(value_cache, 1)
    above_values = passed_along(value_cache, -1)

    local_rows = stale_rows % row_count
    listed = jnp.concatenate([local_rows, jnp.full((16 - local_rows.shape[0],), -1, jnp.int32)])
    refreshed = call(
        refresh_kernel,
        jax.ShapeDtypeStruct(key_cache.shape, jnp.bfloat16),
        "refresh",
        2 * 16 * model_width * model_width,
        16,
        stream,
        key_cache,
        listed[:, None],
        listed[None, :],
        attn_gain[None, :],
        w_key,
        key_bias[None, :],
    )
    below_keys = passed_along(refreshed, 1)
    above_keys = passed_along(refreshed, -1)

    fc_own = jnp.concatenate(
        [w_fc, three_terms(b_fc), jnp.zeros((13, units_here), jnp.bfloat16)], axis=0
    )
    fc_left = shift(fc_own, "x", 1)
    fc_right = shift(fc_own, "x", -1)
    fc_far_a = shift(fc_left[:FC_CUT], "x", 1)
    fc_far_b = shift(fc_right[FC_CUT:], "x", -1)
    proj_part = units_here // tok_count
    proj_piece = lax.dynamic_slice_in_dim(w_proj, tok * proj_part, proj_part, 0)
    proj_all = lax.all_gather(proj_piece, ("x", "tok"), axis=0, tiled=True)
    proj_all = proj_all.reshape(x_count, units_here, model_width)
    weights = (fc_own, fc_left, fc_right, fc_far_a, fc_far_b, proj_all)

    position = lax.axis_index(BLK)
    minus_ones = jnp.full((row_count,), -1, jnp.int32)
    seg_padded = jnp.concatenate([minus_ones, segments, minus_ones], axis=0)
    key_seg = lax.dynamic_slice_in_dim(seg_padded, position * row_count, 3 * row_count, 0)
    query_seg = lax.dynamic_slice_in_dim(segments, position * row_count, row_count, 0)
    merged_rows = row_count // 4
    m = merged_rows
    normed, mixed_mean = attention(
        queries,
        below_keys,
        refreshed,
        above_keys,
        below_values,
        value_cache,
        above_values,
        stream,
        query_seg[:, None],
        key_seg[None, :],
        mlp_gain[None, :],
    )

    half = row_count // 2
    z_low = shift(normed, "z", 1)
    z_high = shift(normed, "z", -1)
    swapped = shift(normed, "c", 1)
    near, near_sent = pooled_parts([normed], [swapped], weights, here, "mlp_near")
    z_far_a = shift(z_low[:half], "z", 1)
    z_far_b = shift(z_high[half:], "z", -1)
    z_low_other = shift(z_low, "c", 1)
    z_high_other = shift(z_high, "c", 1)
    next_to, next_sent = pooled_parts(
        [z_low, z_high], [z_low_other, z_high_other], weights, here, "mlp_next"
    )
    far_a_other = shift(z_far_a, "c", 1)
    far_b_other = shift(z_far_b, "c", 1)
    far, far_sent = pooled_parts(
        [z_far_a, z_far_b], [far_a_other, far_b_other], weights, here, "mlp_far"
    )

    near_other = shift(near_sent, "c", 1)
    next_other = shift(next_sent, "c", 1)
    next_sum = (next_to + next_other.astype(jnp.float32)).astype(jnp.bfloat16)
    from_high = shift(next_sum[:m], "z", -1)
    from_low = shift(next_sum[m:], "z", 1)
    far_other = shift(far_sent, "c", 1)
    far_sum = (far + far_other.astype(jnp.float32)).astype(jnp.bfloat16)
    from_far = shift(far_sum, "z", 2)
    outgoing = call(
        merge_kernel,
        jax.ShapeDtypeStruct((tok_count * m, model_width), jnp.bfloat16),
        "merge",
        2 * m * model_width * model_width,
        16,
        near,
        near_other,
        from_low,
        from_high,
        from_far,
        mixed_mean,
        b_proj[None, :],
        merge_gain[None, :],
        w_merge,
        b_merge[None, :],
        owners[:, None],
        owners[None, :],
    ).reshape(tok_count, m, model_width)
    arrived = lax.all_to_all(outgoing, "tok", split_axis=0, concat_axis=0, tiled=True)
    delivered = arrived.reshape(1, 1, tok_count * merged_rows, model_width)
    return (refreshed, delivered)


def solution(mesh):
    fine = Mesh(mesh.devices.reshape(4, 4, 2, 4), ("x", "z", "c", "tok"))
    return jax.shard_map(
        body,
        mesh=fine,
        in_specs=(
            P(ROWS, None),
            P(ROWS, None),
            P(ROWS, None),
            P(ROWS, None),
            P("tok"),
            P(ROWS),
            P(ROWS),
            P(),
            P(),
            P(),
            P(),
            P(None, BLK),
            P(BLK),
            P(BLK, None),
            P(),
            P(),
            P(),
            P(),
        ),
        out_specs=(P(ROWS, None), P("tok", BLK, None, None)),
        check_vma=False,
    )
```

time: 203 us -> 163 us (0.80)
  waiting for transfers between devices: 71.1 us -> 8.63 us
  starting transfers between devices: 10.1 us -> 66.3 us
  matrix products: 44.6 us -> 0 us
  Pallas kernels: 0 us -> 27.5 us
  blocking collectives: 28 us -> 12.5 us
  other arithmetic: 13.6 us -> 0.83 us
  local copies, waits for them, and re-layouts: 20.7 us -> 29.8 us
    ppermute x4 -> x23, starting transfers between devices: 9.96 us -> 66.3 us  [the longest x19 57.4 us: shift(): lax.ppermute(block, axis, [(i, (i + distance) % count) for i in range(cou...]
    dot_general x8 -> x0, matrix products: 40.2 us -> none  [the longest x4 25.3 us: body(): jnp.dot(rows, fc_all[i], preferred_element_type=jnp.float32) + bias]
    reduce_scatter x1 -> x0, waiting for transfers between devices: 29.6 us -> none  [body(): lax.psum_scatter(partial.astype(jnp.bfloat16), ('z', 'c'), scatter_dimens...]
    all_gather x2 -> x0, waiting for transfers between devices: 28.6 us -> none  [the longest x1 28.6 us: body(): rows = lax.all_gather(normed, ('z', 'c'), axis=0, tiled=True)]
    pallas_call x0 -> x6, Pallas kernels: none -> 27.5 us  [the longest x3 17.1 us: pooled_parts(): pl.pallas_call(lambda *r: mlp_kernel(counts, *r), out_shape=outs, in_spec...]
    unnamed x32 -> x67, local copies, waits for them, and re-layouts: 3.66 us -> 24.7 us
    all_gather x1 -> x0, blocking collectives: 16.4 us -> none  [body(): bias_all = lax.all_gather(b_fc, 'x', axis=0, tiled=True)]
    all_gather x1, waiting for transfers between devices: 12.8 us -> 0.01 us  [body(): proj_all = lax.all_gather(proj_piece, ('x', 'tok'), axis=0, tiled=True)]
  transfers between devices with their start and end apart: 8 -> 24, of which waited for: 3 -> 6; matrix products, arithmetic and copies ran while one was open for 32% -> 3% of each run, Pallas kernels for 0% -> 16%
where the time goes in v2:
time: 163 us; the launch traced here: 160 us
  starting transfers between devices  66.3 us (41%)
  local copies, waits for them, and re-layouts  29.8 us (18%)
  Pallas kernels  27.5 us (17%)
  between operations  14.4 us (9%)
  blocking collectives  12.5 us (8%)
  waiting for transfers between devices  8.63 us (5%)
    ppermute x19, starting transfers between devices, shift(): lax.ppermute(block, axis, [(i, (i + distance) % count) for i in range(cou...  57.4 us
    unnamed x67, local copies, waits for them, and re-layouts  24.7 us
    pallas_call x3, Pallas kernels, pooled_parts(): pl.pallas_call(lambda *r: mlp_kernel(counts, *r), out_shape=outs, in_spec...  17.1 us
    all_to_all x1, blocking collectives, body(): lax.all_to_all(outgoing, 'tok', split_axis=0, concat_axis=0, tiled=True)  12.5 us
    ppermute x4, starting transfers between devices, passed_along(): return lax.ppermute(block, BLK, route)  8.92 us
    ppermute x19, waiting for transfers between devices, shift(): lax.ppermute(block, axis, [(i, (i + distance) % count) for i in range(cou...  8.6 us
    pallas_call x1, Pallas kernels, attention(): pl.pallas_call(attention_kernel, out_shape=outs, in_specs=[pl.BlockSpec(m...  6.87 us
    pallas_call x2, Pallas kernels, call(): pl.pallas_call(kernel, out_shape=outs, in_specs=[pl.BlockSpec(memory_spac...  3.52 us
  transfers between devices with their start and end apart: 24, of which 6 were waited for; matrix products, arithmetic and copies ran while one was open for 3% of the time, Pallas kernels for 16%

profile of v2, /device:TPU:0, one launch (start us, length us, event | category | flops | bytes accessed | tf_op | source)
XLA Modules:
  0.0 160.1 jit_solution(9926859510368651492)
XLA Ops:
  7.3 1.1 copy-done
  11.2 2.6 %copy-done.3 = bf16[1664,1664]{1,0:T(8,128)(2,1)S(1)} copy-done((bf16[1664,1664]{1,0:T(8,128)(2,1)S(1)}, bf16[1664,1664]{1,0:T(8,128)(2,1)}, u32[]{:S(2)}) %copy-start.3) | copy-done | bytes 5537816
  13.8 1.0 copy-done.10
  14.8 1.0 copy-done.16
  15.8 2.1 %refresh.1.keys = bf16[128,1664]{1,0:T(8,128)(2,1)} custom-call(bf16[128,1664]{1,0:T(8,128)(2,1)S(1)} %copy-done.10, bf16[128,1664]{1,0:T(8,128)(2,1)S(1)} %copy-done.16, s32[16,1]{1,0:T(8,128)S(1)} %copy.20.rows_col, s32[1,16]{1,0:T(1,128)S(1)} %get-tuple-element.23.rows_row, f32[1,1664]{1,0:T(1,128)S(1)} %broadcast_in_dim.44.gain, ...), custom_call_target="tpu_custom_call" | custom-call | flops 88604672 | bytes 6403200 | tf_op jit(solution)/shard_map/refresh/pallas_call | solution.py:55
  17.9 1.3 collective-permute-start
  20.0 2.2 %collective-permute-start.5 = (bf16[1680,256]{1,0:T(8,128)(2,1)S(1)}, bf16[1680,256]{1,0:T(8,128)(2,1)S(1)}, u32[]{:S(2)}, u32[]{:S(2)}) collective-permute-start(bf16[1680,256]{1,0:T(8,128)(2,1)S(1)} %concatenate.11.r_3_.r_5_), channel_id=1, source_target_pairs={{0,32},{32,64},{64,96},{96,0},{1,33},{33,65},{65,97},{97,1},{2,34}... | collective-permute-start | bytes 2580488 | tf_op jit(solution)/shard_map/ppermute | solution.py:23
  22.2 1.3 collective-permute-start.1
  23.5 5.1 %collective-permute-start.2 = (bf16[128,1664]{1,0:T(8,128)(2,1)}, bf16[128,1664]{1,0:T(8,128)(2,1)}, u32[]{:S(2)}, u32[]{:S(2)}) collective-permute-start(bf16[128,1664]{1,0:T(8,128)(2,1)} %values.1), channel_id=1, source_target_pairs={{0,4},{4,8},{8,12},{12,16},{16,20},{20,24},{24,28},{28,32},{32,36}... | collective-permute-start | bytes 1277960 | tf_op jit(solution)/shard_map/ppermute | solution.py:18
  28.6 1.3 collective-permute-start.3
  30.6 8.3 %collective-permute-start.6 = (bf16[1680,256]{1,0:T(8,128)(2,1)S(1)}, bf16[1680,256]{1,0:T(8,128)(2,1)S(1)}, u32[]{:S(2)}, u32[]{:S(2)}) collective-permute-start(bf16[1680,256]{1,0:T(8,128)(2,1)S(1)} %concatenate.11.r_3_.r_5_), channel_id=1, source_target_pairs={{0,96},{32,0},{64,32},{96,64},{1,97},{33,1},{65,33},{97,65},{2,98}... | collective-permute-start | bytes 2580488 | tf_op jit(solution)/shard_map/ppermute | solution.py:23
  40.3 1.0 copy-done.12
  41.3 1.0 copy-done.13
  43.3 6.9 %attention.1 = (bf16[128,1664]{1,0:T(8,128)(2,1)S(1)}, f32[32,1664]{1,0:T(8,128)S(1)}) custom-call(bf16[128,1664]{1,0:T(8,128)(2,1)S(1)} %copy-done.13, bf16[128,1664]{1,0:T(8,128)(2,1)S(1)} %copy-done.15, bf16[128,1664]{1,0:T(8,128)(2,1)S(1)} %copy-done.12, bf16[128,1664]{1,0:T(8,128)(2,1)} %collective-permute-done.1.keys_above, ...), custom_call_target="tpu_custom_call" | custom-call | flops 654311424 | bytes 4194304 | tf_op jit(solution)/shard_map/attention/pallas_call | solution.py:239
  50.3 3.2 %collective-permute-start.11 = (bf16[128,1664]{1,0:T(8,128)(2,1)S(1)}, bf16[128,1664]{1,0:T(8,128)(2,1)}, u32[]{:S(2)}, u32[]{:S(2)}) collective-permute-start(bf16[128,1664]{1,0:T(8,128)(2,1)S(1)} %get-tuple-element.10.r_1_), channel_id=1, source_target_pairs={{0,24},{8,0},{16,8},{24,16},{1,25},{9,1},{17,9},{25,17},{2,26},{10... | collective-permute-start | bytes 1277960 | tf_op jit(solution)/shard_map/ppermute | solution.py:23
  53.5 27.0 %collective-permute-start.4 = (bf16[128,1664]{1,0:T(8,128)(2,1)S(1)}, bf16[128,1664]{1,0:T(8,128)(2,1)S(1)}, u32[]{:S(2)}, u32[]{:S(2)}) collective-permute-start(bf16[128,1664]{1,0:T(8,128)(2,1)S(1)} %get-tuple-element.10.r_1_), channel_id=1, source_target_pairs={{0,4},{4,0},{1,5},{5,1},{2,6},{6,2},{3,7},{7,3},{8,12},{12,8},{9,1... | collective-permute-start | bytes 1277960 | tf_op jit(solution)/shard_map/ppermute | solution.py:23
  80.5 5.3 %collective-permute-start.7 = (bf16[768,256]{1,0:T(8,128)(2,1)S(1)}, bf16[768,256]{1,0:T(8,128)(2,1)S(1)}, u32[]{:S(2)}, u32[]{:S(2)}) collective-permute-start(bf16[768,256]{1,0:T(8,128)(2,1)S(1)} %slice.24), channel_id=1, source_target_pairs={{0,32},{32,64},{64,96},{96,0},{1,33},{33,65},{65,97},{97,1},{2,34}... | collective-permute-start | bytes 1179656 | tf_op jit(solution)/shard_map/ppermute | solution.py:23
  85.8 1.4 collective-permute-start.8
  89.2 3.3 %collective-permute-start.18 = (bf16[64,1664]{1,0:T(8,128)(2,1)S(1)}, bf16[64,1664]{1,0:T(8,128)(2,1)}, u32[]{:S(2)}, u32[]{:S(2)}) collective-permute-start(bf16[64,1664]{1,0:T(8,128)(2,1)S(1)} %slice.29), channel_id=1, source_target_pairs={{0,24},{8,0},{16,8},{24,16},{1,25},{9,1},{17,9},{25,17},{2,26},{10... | collective-permute-start | bytes 638984 | tf_op jit(solution)/shard_map/ppermute | solution.py:23
  93.3 3.7 %collective-permute-done.17.r_1_ = bf16[64,1664]{1,0:T(8,128)(2,1)} collective-permute-done((bf16[64,1664]{1,0:T(8,128)(2,1)S(1)}, bf16[64,1664]{1,0:T(8,128)(2,1)}, u32[]{:S(2)}, u32[]{:S(2)}) %collective-permute-start.17) | collective-permute-done | bytes 213024 | tf_op jit(solution)/shard_map/ppermute | solution.py:23
  99.5 2.0 %copy-done.1 = bf16[1024,1664]{1,0:T(8,128)(2,1)S(1)} copy-done((bf16[1024,1664]{1,0:T(8,128)(2,1)S(1)}, bf16[1024,1664]{1,0:T(8,128)(2,1)}, u32[]{:S(2)}) %copy-start.1) | copy-done | bytes 3407896
  101.5 1.0 copy-done.6
  105.5 4.1 %mlp_near.1 = (f32[32,1664]{1,0:T(8,128)S(1)}, bf16[32,1664]{1,0:T(8,128)(2,1)}) custom-call(s32[1]{0:T(128)} %bitcast.2.r_0_, bf16[128,1664]{1,0:T(8,128)(2,1)S(1)} %copy-done.18, bf16[128,1664]{1,0:T(8,128)(2,1)S(1)} %copy-done.20, bf16[1680,256]{1,0:T(8,128)(2,1)S(1)} %concatenate.11.r_3_.r_5_, bf16[1680,256]{1,0:T(8,128)(2,1)S(1)} %collective-permute-done.5.r_4_.r_6_, ...), custom_call_target="tpu_custom_call" | custom-call | flops 1090519040 | bytes 8388608 | tf_op jit(solution)/shard_map/mlp_near/pallas_call | solution.py:190
  110.4 4.8 %mlp_far.1 = (f32[32,1664]{1,0:T(8,128)S(1)}, bf16[32,1664]{1,0:T(8,128)(2,1)S(1)}) custom-call(s32[1]{0:T(128)} %bitcast.2.r_0_, bf16[64,1664]{1,0:T(8,128)(2,1)} %collective-permute-done.17.r_1_, bf16[64,1664]{1,0:T(8,128)(2,1)} %collective-permute-done.18.r_2_, bf16[64,1664]{1,0:T(8,128)(2,1)} %collective-permute-done.19.r_3_, ...), custom_call_target="tpu_custom_call" | custom-call | flops 1090519040 | bytes 8388608 | tf_op jit(solution)/shard_map/mlp_far/pallas_call | solution.py:190
  115.7 8.2 %mlp_next.1 = (f32[64,1664]{1,0:T(8,128)S(1)}, bf16[64,1664]{1,0:T(8,128)(2,1)S(1)}) custom-call(s32[1]{0:T(128)} %bitcast.2.r_0_, bf16[128,1664]{1,0:T(8,128)(2,1)} %collective-permute-done.10.r_1_, bf16[128,1664]{1,0:T(8,128)(2,1)} %collective-permute-done.11.r_2_, bf16[128,1664]{1,0:T(8,128)(2,1)} %collective-permute-done.12.r_3_, ...), custom_call_target="tpu_custom_call" | custom-call | flops 2181038080 | bytes 8388608 | tf_op jit(solution)/shard_map/mlp_next/pallas_call | solution.py:190
  124.1 2.1 %collective-permute-start.22 = (bf16[32,1664]{1,0:T(8,128)(2,1)S(1)}, bf16[32,1664]{1,0:T(8,128)(2,1)S(1)}, u32[]{:S(2)}, u32[]{:S(2)}) collective-permute-start(bf16[32,1664]{1,0:T(8,128)(2,1)S(1)} %add_convert_fusion.1), channel_id=1, source_target_pairs={{0,16},{8,24},{16,0},{24,8},{1,17},{9,25},{17,1},{25,9},{2,18},{10... | collective-permute-start | bytes 319496 | tf_op jit(solution)/shard_map/ppermute | solution.py:23
  126.3 2.4 %collective-permute-start.15 = (bf16[32,1664]{1,0:T(8,128)(2,1)S(1)}, bf16[32,1664]{1,0:T(8,128)(2,1)S(1)}, u32[]{:S(2)}, u32[]{:S(2)}) collective-permute-start(bf16[32,1664]{1,0:T(8,128)(2,1)S(1)} %get-tuple-element.19), channel_id=1, source_target_pairs={{0,8},{8,16},{16,24},{24,0},{1,9},{9,17},{17,25},{25,1},{2,10},{10... | collective-permute-start | bytes 319496 | tf_op jit(solution)/shard_map/ppermute | solution.py:23
  129.7 1.4 collective-permute-done.22.from_far
  131.1 2.2 %collective-permute-done.15.from_low = bf16[32,1664]{1,0:T(8,128)(2,1)S(1)} collective-permute-done((bf16[32,1664]{1,0:T(8,128)(2,1)S(1)}, bf16[32,1664]{1,0:T(8,128)(2,1)S(1)}, u32[]{:S(2)}, u32[]{:S(2)}) %collective-permute-start.15) | collective-permute-done | bytes 106528 | tf_op jit(solution)/shard_map/ppermute | solution.py:23
  134.1 2.6 %copy-done.4 = bf16[1664,1664]{1,0:T(8,128)(2,1)S(1)} copy-done((bf16[1664,1664]{1,0:T(8,128)(2,1)S(1)}, bf16[1664,1664]{1,0:T(8,128)(2,1)}, u32[]{:S(2)}) %copy-start.4) | copy-done | bytes 5537816
  138.6 1.4 merge.1
  140.0 12.5 %all_to_all.5 = bf16[4,32,1664]{2,1,0:T(8,128)(2,1)S(1)} all-to-all(bf16[4,32,1664]{2,1,0:T(8,128)(2,1)S(1)} %bitcast.15), channel_id=1, replica_groups=mesh['x'=4,'z'=4,'c'=2,'tok'=4] {'tok'}, dimensions={0} | all-to-all | bytes 851968 | tf_op jit(solution)/shard_map/all_to_all | solution.py:382
  (120 shorter events, 21.1 us)
Async XLA Ops:
  7.2 31.7 %copy-start.27 = (s32[4096]{0:T(1024)S(1)}, s32[4096]{0:T(1024)}, u32[]{:S(2)}) copy-start(s32[4096]{0:T(1024)} %param.22) | copy-start | bytes 49156
  7.2 32.0 %copy-start.28 = (f32[1664]{0:T(1024)S(1)}, f32[1664]{0:T(1024)}, u32[]{:S(2)}) copy-start(f32[1664]{0:T(1024)} %param.28) | copy-start | bytes 19972
  7.2 92.3 %all-gather.2.cloned.1.call-start = ((), (), s32[]{:S(2)}) async-start(), calls=%async_computation.1 | async-start | bytes 3620864 | tf_op jit(solution)/shard_map/all_gather | solution.py:312
  17.9 11.9 %collective-permute-start = (bf16[128,1664]{1,0:T(8,128)(2,1)}, bf16[128,1664]{1,0:T(8,128)(2,1)S(1)}, u32[]{:S(2)}, u32[]{:S(2)}) collective-permute-start(bf16[128,1664]{1,0:T(8,128)(2,1)} %refresh.1.keys), channel_id=1, source_target_pairs={{0,4},{4,8},{8,12},{12,16},{16,20},{20,24},{24,28},{28,32},{32,36}... | collective-permute-start | bytes 1277960 | tf_op jit(solution)/shard_map/ppermute | solution.py:18
  20.0 60.5 %collective-permute-start.5 = (bf16[1680,256]{1,0:T(8,128)(2,1)S(1)}, bf16[1680,256]{1,0:T(8,128)(2,1)S(1)}, u32[]{:S(2)}, u32[]{:S(2)}) collective-permute-start(bf16[1680,256]{1,0:T(8,128)(2,1)S(1)} %concatenate.11.r_3_.r_5_), channel_id=1, source_target_pairs={{0,32},{32,64},{64,96},{96,0},{1,33},{33,65},{65,97},{97,1},{2,34}... | collective-permute-start | bytes 2580488 | tf_op jit(solution)/shard_map/ppermute | solution.py:23
  22.2 17.0 %collective-permute-start.1 = (bf16[128,1664]{1,0:T(8,128)(2,1)}, bf16[128,1664]{1,0:T(8,128)(2,1)}, u32[]{:S(2)}, u32[]{:S(2)}) collective-permute-start(bf16[128,1664]{1,0:T(8,128)(2,1)} %refresh.1.keys), channel_id=1, source_target_pairs={{4,0},{8,4},{12,8},{16,12},{20,16},{24,20},{28,24},{32,28},{36,32}... | collective-permute-start | bytes 1277960 | tf_op jit(solution)/shard_map/ppermute | solution.py:18
  23.5 15.7 %collective-permute-start.2 = (bf16[128,1664]{1,0:T(8,128)(2,1)}, bf16[128,1664]{1,0:T(8,128)(2,1)}, u32[]{:S(2)}, u32[]{:S(2)}) collective-permute-start(bf16[128,1664]{1,0:T(8,128)(2,1)} %values.1), channel_id=1, source_target_pairs={{0,4},{4,8},{8,12},{12,16},{16,20},{20,24},{24,28},{28,32},{32,36}... | collective-permute-start | bytes 1277960 | tf_op jit(solution)/shard_map/ppermute | solution.py:18
  28.6 10.7 %collective-permute-start.3 = (bf16[128,1664]{1,0:T(8,128)(2,1)}, bf16[128,1664]{1,0:T(8,128)(2,1)}, u32[]{:S(2)}, u32[]{:S(2)}) collective-permute-start(bf16[128,1664]{1,0:T(8,128)(2,1)} %values.1), channel_id=1, source_target_pairs={{4,0},{8,4},{12,8},{16,12},{20,16},{24,20},{28,24},{32,28},{36,32}... | collective-permute-start | bytes 1277960 | tf_op jit(solution)/shard_map/ppermute | solution.py:18
  30.6 55.2 %collective-permute-start.6 = (bf16[1680,256]{1,0:T(8,128)(2,1)S(1)}, bf16[1680,256]{1,0:T(8,128)(2,1)S(1)}, u32[]{:S(2)}, u32[]{:S(2)}) collective-permute-start(bf16[1680,256]{1,0:T(8,128)(2,1)S(1)} %concatenate.11.r_3_.r_5_), channel_id=1, source_target_pairs={{0,96},{32,0},{64,32},{96,64},{1,97},{33,1},{65,33},{97,65},{2,98}... | collective-permute-start | bytes 2580488 | tf_op jit(solution)/shard_map/ppermute | solution.py:23
  50.2 47.3 %copy-start.17 = (bf16[128,1664]{1,0:T(8,128)(2,1)}, bf16[128,1664]{1,0:T(8,128)(2,1)S(1)}, u32[]{:S(2)}) copy-start(bf16[128,1664]{1,0:T(8,128)(2,1)S(1)} %get-tuple-element.10.r_1_) | copy-start | bytes 1277956
  50.2 48.2 %copy-start.21 = (f32[32,1664]{1,0:T(8,128)}, f32[32,1664]{1,0:T(8,128)S(1)}, u32[]{:S(2)}) copy-start(f32[32,1664]{1,0:T(8,128)S(1)} %get-tuple-element.17.mixed_mean) | copy-start | bytes 638980
  50.2 37.0 %collective-permute-start.10 = (bf16[128,1664]{1,0:T(8,128)(2,1)S(1)}, bf16[128,1664]{1,0:T(8,128)(2,1)}, u32[]{:S(2)}, u32[]{:S(2)}) collective-permute-start(bf16[128,1664]{1,0:T(8,128)(2,1)S(1)} %get-tuple-element.10.r_1_), channel_id=1, source_target_pairs={{0,8},{8,16},{16,24},{24,0},{1,9},{9,17},{17,25},{25,1},{2,10},{10... | collective-permute-start | bytes 1277960 | tf_op jit(solution)/shard_map/ppermute | solution.py:23
  50.3 38.0 %collective-permute-start.11 = (bf16[128,1664]{1,0:T(8,128)(2,1)S(1)}, bf16[128,1664]{1,0:T(8,128)(2,1)}, u32[]{:S(2)}, u32[]{:S(2)}) collective-permute-start(bf16[128,1664]{1,0:T(8,128)(2,1)S(1)} %get-tuple-element.10.r_1_), channel_id=1, source_target_pairs={{0,24},{8,0},{16,8},{24,16},{1,25},{9,1},{17,9},{25,17},{2,26},{10... | collective-permute-start | bytes 1277960 | tf_op jit(solution)/shard_map/ppermute | solution.py:23
  53.5 39.0 %collective-permute-start.4 = (bf16[128,1664]{1,0:T(8,128)(2,1)S(1)}, bf16[128,1664]{1,0:T(8,128)(2,1)S(1)}, u32[]{:S(2)}, u32[]{:S(2)}) collective-permute-start(bf16[128,1664]{1,0:T(8,128)(2,1)S(1)} %get-tuple-element.10.r_1_), channel_id=1, source_target_pairs={{0,4},{4,0},{1,5},{5,1},{2,6},{6,2},{3,7},{7,3},{8,12},{12,8},{9,1... | collective-permute-start | bytes 1277960 | tf_op jit(solution)/shard_map/ppermute | solution.py:23
  80.5 16.9 %collective-permute-start.7 = (bf16[768,256]{1,0:T(8,128)(2,1)S(1)}, bf16[768,256]{1,0:T(8,128)(2,1)S(1)}, u32[]{:S(2)}, u32[]{:S(2)}) collective-permute-start(bf16[768,256]{1,0:T(8,128)(2,1)S(1)} %slice.24), channel_id=1, source_target_pairs={{0,32},{32,64},{64,96},{96,0},{1,33},{33,65},{65,97},{97,1},{2,34}... | collective-permute-start | bytes 1179656 | tf_op jit(solution)/shard_map/ppermute | solution.py:23
  85.8 12.9 %collective-permute-start.8 = (bf16[912,256]{1,0:T(8,128)(2,1)S(1)}, bf16[912,256]{1,0:T(8,128)(2,1)S(1)}, u32[]{:S(2)}, u32[]{:S(2)}) collective-permute-start(bf16[912,256]{1,0:T(8,128)(2,1)S(1)} %slice.25), channel_id=1, source_target_pairs={{0,96},{32,0},{64,32},{96,64},{1,97},{33,1},{65,33},{97,65},{2,98}... | collective-permute-start | bytes 1400840 | tf_op jit(solution)/shard_map/ppermute | solution.py:23
  88.2 8.8 %collective-permute-start.17 = (bf16[64,1664]{1,0:T(8,128)(2,1)S(1)}, bf16[64,1664]{1,0:T(8,128)(2,1)}, u32[]{:S(2)}, u32[]{:S(2)}) collective-permute-start(bf16[64,1664]{1,0:T(8,128)(2,1)S(1)} %slice.28), channel_id=1, source_target_pairs={{0,8},{8,16},{16,24},{24,0},{1,9},{9,17},{17,25},{25,1},{2,10},{10... | collective-permute-start | bytes 638984 | tf_op jit(solution)/shard_map/ppermute | solution.py:23
  89.2 7.9 %collective-permute-start.18 = (bf16[64,1664]{1,0:T(8,128)(2,1)S(1)}, bf16[64,1664]{1,0:T(8,128)(2,1)}, u32[]{:S(2)}, u32[]{:S(2)}) collective-permute-start(bf16[64,1664]{1,0:T(8,128)(2,1)S(1)} %slice.29), channel_id=1, source_target_pairs={{0,24},{8,0},{16,8},{24,16},{1,25},{9,1},{17,9},{25,17},{2,26},{10... | collective-permute-start | bytes 638984 | tf_op jit(solution)/shard_map/ppermute | solution.py:23
  93.3 22.5 %collective-permute-start.12 = (bf16[128,1664]{1,0:T(8,128)(2,1)}, bf16[128,1664]{1,0:T(8,128)(2,1)}, u32[]{:S(2)}, u32[]{:S(2)}) collective-permute-start(bf16[128,1664]{1,0:T(8,128)(2,1)} %collective-permute-done.10.r_1_), channel_id=1, source_target_pairs={{0,4},{4,0},{1,5},{5,1},{2,6},{6,2},{3,7},{7,3},{8,12},{12,8},{9,1... | collective-permute-start | bytes 1277960 | tf_op jit(solution)/shard_map/ppermute | solution.py:23
  96.9 18.8 %collective-permute-start.13 = (bf16[128,1664]{1,0:T(8,128)(2,1)}, bf16[128,1664]{1,0:T(8,128)(2,1)}, u32[]{:S(2)}, u32[]{:S(2)}) collective-permute-start(bf16[128,1664]{1,0:T(8,128)(2,1)} %collective-permute-done.11.r_2_), channel_id=1, source_target_pairs={{0,4},{4,0},{1,5},{5,1},{2,6},{6,2},{3,7},{7,3},{8,12},{12,8},{9,1... | collective-permute-start | bytes 1277960 | tf_op jit(solution)/shard_map/ppermute | solution.py:23
  97.1 13.2 %collective-permute-start.19 = (bf16[64,1664]{1,0:T(8,128)(2,1)}, bf16[64,1664]{1,0:T(8,128)(2,1)}, u32[]{:S(2)}, u32[]{:S(2)}) collective-permute-start(bf16[64,1664]{1,0:T(8,128)(2,1)} %collective-permute-done.17.r_1_), channel_id=1, source_target_pairs={{0,4},{4,0},{1,5},{5,1},{2,6},{6,2},{3,7},{7,3},{8,12},{12,8},{9,1... | collective-permute-start | bytes 638984 | tf_op jit(solution)/shard_map/ppermute | solution.py:23
  98.2 12.1 %collective-permute-start.20 = (bf16[64,1664]{1,0:T(8,128)(2,1)}, bf16[64,1664]{1,0:T(8,128)(2,1)}, u32[]{:S(2)}, u32[]{:S(2)}) collective-permute-start(bf16[64,1664]{1,0:T(8,128)(2,1)} %collective-permute-done.18.r_2_), channel_id=1, source_target_pairs={{0,4},{4,0},{1,5},{5,1},{2,6},{6,2},{3,7},{7,3},{8,12},{12,8},{9,1... | collective-permute-start | bytes 638984 | tf_op jit(solution)/shard_map/ppermute | solution.py:23
  110.3 19.4 %collective-permute-start.9 = (bf16[32,1664]{1,0:T(8,128)(2,1)}, bf16[32,1664]{1,0:T(8,128)(2,1)S(1)}, u32[]{:S(2)}, u32[]{:S(2)}) collective-permute-start(bf16[32,1664]{1,0:T(8,128)(2,1)} %get-tuple-element.12), channel_id=1, source_target_pairs={{0,4},{4,0},{1,5},{5,1},{2,6},{6,2},{3,7},{7,3},{8,12},{12,8},{9,1... | collective-permute-start | bytes 319496 | tf_op jit(solution)/shard_map/ppermute | solution.py:23
  115.1 14.4 %copy-start.29 = (f32[1664]{0:T(1024)S(1)}, f32[1664]{0:T(1024)}, u32[]{:S(2)}) copy-start(f32[1664]{0:T(1024)} %param.32) | copy-start | bytes 19972
  115.2 14.4 %copy-start.30 = (f32[1664]{0:T(1024)S(1)}, f32[1664]{0:T(1024)}, u32[]{:S(2)}) copy-start(f32[1664]{0:T(1024)} %param.33) | copy-start | bytes 19972
  115.2 14.4 %copy-start.31 = (f32[1664]{0:T(1024)S(1)}, f32[1664]{0:T(1024)}, u32[]{:S(2)}) copy-start(f32[1664]{0:T(1024)} %param.35) | copy-start | bytes 19972
  115.2 14.5 %copy-start.25 = (s32[32]{0:T(128)S(1)}, s32[32]{0:T(128)}, u32[]{:S(2)}) copy-start(s32[32]{0:T(128)} %param.24) | copy-start | bytes 388
  115.2 8.9 %collective-permute-start.21 = (bf16[32,1664]{1,0:T(8,128)(2,1)S(1)}, bf16[32,1664]{1,0:T(8,128)(2,1)S(1)}, u32[]{:S(2)}, u32[]{:S(2)}) collective-permute-start(bf16[32,1664]{1,0:T(8,128)(2,1)S(1)} %get-tuple-element.16), channel_id=1, source_target_pairs={{0,4},{4,0},{1,5},{5,1},{2,6},{6,2},{3,7},{7,3},{8,12},{12,8},{9,1... | collective-permute-start | bytes 319496 | tf_op jit(solution)/shard_map/ppermute | solution.py:23
  124.0 2.2 %collective-permute-start.14 = (bf16[64,1664]{1,0:T(8,128)(2,1)S(1)}, bf16[64,1664]{1,0:T(8,128)(2,1)S(1)}, u32[]{:S(2)}, u32[]{:S(2)}) collective-permute-start(bf16[64,1664]{1,0:T(8,128)(2,1)S(1)} %get-tuple-element.14), channel_id=1, source_target_pairs={{0,4},{4,0},{1,5},{5,1},{2,6},{6,2},{3,7},{7,3},{8,12},{12,8},{9,1... | collective-permute-start | bytes 638984 | tf_op jit(solution)/shard_map/ppermute | solution.py:23
  124.1 7.0 %collective-permute-start.22 = (bf16[32,1664]{1,0:T(8,128)(2,1)S(1)}, bf16[32,1664]{1,0:T(8,128)(2,1)S(1)}, u32[]{:S(2)}, u32[]{:S(2)}) collective-permute-start(bf16[32,1664]{1,0:T(8,128)(2,1)S(1)} %add_convert_fusion.1), channel_id=1, source_target_pairs={{0,16},{8,24},{16,0},{24,8},{1,17},{9,25},{17,1},{25,9},{2,18},{10... | collective-permute-start | bytes 319496 | tf_op jit(solution)/shard_map/ppermute | solution.py:23
  126.3 7.1 %collective-permute-start.15 = (bf16[32,1664]{1,0:T(8,128)(2,1)S(1)}, bf16[32,1664]{1,0:T(8,128)(2,1)S(1)}, u32[]{:S(2)}, u32[]{:S(2)}) collective-permute-start(bf16[32,1664]{1,0:T(8,128)(2,1)S(1)} %get-tuple-element.19), channel_id=1, source_target_pairs={{0,8},{8,16},{16,24},{24,0},{1,9},{9,17},{17,25},{25,1},{2,10},{10... | collective-permute-start | bytes 319496 | tf_op jit(solution)/shard_map/ppermute | solution.py:23
  128.7 5.5 %collective-permute-start.16 = (bf16[32,1664]{1,0:T(8,128)(2,1)S(1)}, bf16[32,1664]{1,0:T(8,128)(2,1)S(1)}, u32[]{:S(2)}, u32[]{:S(2)}) collective-permute-start(bf16[32,1664]{1,0:T(8,128)(2,1)S(1)} %get-tuple-element.18), channel_id=1, source_target_pairs={{0,24},{8,0},{16,8},{24,16},{1,25},{9,1},{17,9},{25,17},{2,26},{10... | collective-permute-start | bytes 319496 | tf_op jit(solution)/shard_map/ppermute | solution.py:23
  (25 other events, 49.8 us)
Sparse Core Ops, SparseCore 0:
  10.2 60.8 all-gather.1

commit v3 on v1

v3 whole, which is shorter than its diff:
```python
import jax
import jax.numpy as jnp
from jax import lax
from jax.experimental import pallas as pl
from jax.experimental.pallas import tpu as pltpu
from jax.sharding import Mesh
from jax.sharding import PartitionSpec as P

HEADS = 16
ROWS = ("tok", "x", "z", "c")
BLK = ("x", "z", "c")
FC_CUT = 768


def passed_along(block, distance):
    count = lax.axis_size("x") * lax.axis_size("z") * lax.axis_size("c")
    route = [(i - distance, i) for i in range(count) if 0 <= i - distance < count]
    return lax.ppermute(block, BLK, route)


def shift(block, axis, distance):
    count = lax.axis_size(axis)
    return lax.ppermute(block, axis, [(i, (i + distance) % count) for i in range(count)])


def after(value, *others):
    return lax.optimization_barrier((value, *others))[0]


def layer_norm(values, gain):
    center = values - jnp.mean(values, axis=-1, keepdims=True)
    spread = jnp.mean(center * center, axis=-1, keepdims=True)
    return center * lax.rsqrt(spread + 1e-06) * gain


def three_terms(values):
    high = values.astype(jnp.bfloat16)
    rest = values - high.astype(jnp.float32)
    middle = rest.astype(jnp.bfloat16)
    low = (rest - middle.astype(jnp.float32)).astype(jnp.bfloat16)
    return jnp.stack([high, middle, low])


def dot(left, right):
    return jnp.dot(left, right, preferred_element_type=jnp.float32)


def iota(shape, axis):
    return lax.broadcasted_iota(jnp.int32, shape, axis)


def mean_of_fours(rows):
    hit = iota((rows // 4, rows), 1) // 4 == iota((rows // 4, rows), 0)
    return jnp.where(hit, 0.25, 0.0).astype(jnp.bfloat16)


def column_of(row):
    count = row.shape[1]
    same = iota((count, count), 0) == iota((count, count), 1)
    wide = jnp.where(same, row.astype(jnp.float32), 0.0)
    return jnp.sum(wide, axis=1, keepdims=True).astype(jnp.int32)


class Fetch:
    def __init__(self, source, target, semaphore):
        self.copy = pltpu.make_async_copy(source, target, semaphore)
        self.copy.start()
        self.target = target

    def ref(self):
        if self.copy is not None:
            self.copy.wait()
            self.copy = None
        return self.target


def call(kernel, name, outs, flops, limit, fetched, direct=(), scalars=(), buffers=None, scratch=(), semaphores=None):
    n_s, n_f, n_d = len(scalars), len(fetched), len(direct)
    single = not isinstance(outs, tuple)
    n_o = 1 if single else len(outs)
    shapes = [pltpu.VMEM(a.shape, a.dtype) for a in fetched] if buffers is None else buffers

    def wrapped(*refs):
        scalar_refs = refs[:n_s]
        sources = refs[n_s : n_s + n_f]
        direct_refs = refs[n_s + n_f : n_s + n_f + n_d]
        out_refs = refs[n_s + n_f + n_d : n_s + n_f + n_d + n_o]
        rest = refs[n_s + n_f + n_d + n_o :]
        targets, semaphores, extra = rest[: len(shapes)], rest[len(shapes)], rest[len(shapes) + 1 :]
        kernel(scalar_refs, sources, targets, semaphores, direct_refs, out_refs, extra)

    moved = sum(a.size * a.dtype.itemsize for a in fetched)
    vmem = pl.BlockSpec(memory_space=pltpu.VMEM)
    return pl.pallas_call(
        wrapped,
        out_shape=outs,
        in_specs=[pl.BlockSpec(memory_space=pltpu.SMEM)] * n_s
        + [pl.BlockSpec(memory_space=pltpu.HBM)] * n_f
        + [vmem] * n_d,
        out_specs=vmem if single else tuple(vmem for _ in outs),
        scratch_shapes=[*shapes, pltpu.SemaphoreType.DMA((semaphores or len(shapes),)), *scratch],
        compiler_params=pltpu.CompilerParams(vmem_limit_bytes=60 << 20),
        cost_estimate=pl.CostEstimate(flops=flops, bytes_accessed=moved, transcendentals=0),
        name=name,
    )(*scalars, *fetched, *direct)


def fetch_all(sources, targets, semaphores):
    return [Fetch(s, t, semaphores.at[i]) for i, (s, t) in enumerate(zip(sources, targets))]


def refresh_kernel(_, sources, targets, semaphores, direct, outs, __):
    stream, keys, w_key = fetch_all(sources, targets, semaphores)
    listed, gain, key_bias = direct
    (out,) = outs
    block = keys.target.shape[0]
    rows = listed[...][None, :] % block
    place = jnp.where(rows == iota((block, rows.shape[1]), 0), 1.0, 0.0)
    hit = jnp.sum(place, axis=1, keepdims=True) > 0.5
    place = place.astype(jnp.bfloat16)
    picked = lax.dot_general(
        place, stream.ref()[...], (((0,), (0,)), ((), ())), preferred_element_type=jnp.float32
    )
    held = layer_norm(picked, gain[...][None, :]).astype(jnp.bfloat16)
    fresh = (dot(held, w_key.ref()[...]) + key_bias[...][None, :]).astype(jnp.bfloat16)
    spread = dot(place, fresh)
    old = keys.ref()[...].astype(jnp.float32)
    out[...] = jnp.where(hit, spread, old).astype(jnp.bfloat16)


def attention_kernel(scalars, sources, targets, semaphores, direct, outs, extra):
    fetches = fetch_all(sources, targets, semaphores)
    queries, keys_below, keys, keys_above, values_below, values, values_above, stream = fetches
    position = scalars[0][0]
    segments, gain = direct
    normed, mixed_mean = outs
    (attended,) = extra
    rows, width = queries.target.shape
    size = width // HEADS
    blocks = segments.shape[0]
    middle = segments[pl.ds(position, 1), :]
    before = segments[pl.ds(jnp.maximum(position - 1, 0), 1), :]
    behind = segments[pl.ds(jnp.minimum(position + 1, blocks - 1), 1), :]
    before = jnp.where(position > 0, before, -1)
    behind = jnp.where(position < blocks - 1, behind, -1)
    allowed = column_of(middle) == jnp.concatenate([before, middle, behind], axis=1)
    scale = 1.0 / size**0.5
    for h in range(HEADS):
        low = h * size // 128 * 128
        high = min(-(-(h + 1) * size // 128) * 128, width)
        lane = iota((1, high - low), 1) + low
        mine = (lane >= h * size) & (lane < (h + 1) * size)
        picked = jnp.where(mine, 1.0, 0.0).astype(jnp.bfloat16)
        query = queries.ref()[:, low:high] * picked
        key = jnp.concatenate(
            [k.ref()[:, low:high] for k in (keys_below, keys, keys_above)], axis=0
        )
        scores = lax.dot_general(
            query, key, (((1,), (1,)), ((), ())), preferred_element_type=jnp.float32
        )
        scores = jnp.where(allowed, scores * scale, -jnp.inf)
        weights = jnp.exp(scores - jnp.max(scores, axis=-1, keepdims=True))
        share = 1.0 / jnp.sum(weights, axis=-1, keepdims=True)
        value = jnp.concatenate(
            [v.ref()[:, low:high] for v in (values_below, values, values_above)], axis=0
        )
        found = dot((weights * share).astype(jnp.bfloat16), value)
        attended[:, low:high] = jnp.where(mine, found, attended[:, low:high])
    rounded = attended[...].astype(jnp.bfloat16)
    here = stream.ref()[...]
    fours = mean_of_fours(rows)
    mixed_mean[...] = dot(fours, here) + dot(fours, rounded)
    mixed = here.astype(jnp.float32) + rounded.astype(jnp.float32)
    normed[...] = layer_norm(mixed, gain[...][None, :]).astype(jnp.bfloat16)


def mlp_kernel(n_mine, n_other, scalars, sources, targets, semaphores, _, outs, __):
    x = scalars[0][0]
    n_rows = n_mine + n_other
    row_blocks = fetch_all(sources[:n_rows], targets[:n_rows], semaphores)
    gathered = sources[-1]
    shards, pieces, depth, width = gathered.shape
    depth = depth - 16
    fc, terms, proj = [], [], []
    at = n_rows
    units = targets[-1].shape[0]
    for number, step in enumerate((0, shards - 1, 1, 2)):
        shard = gathered.at[lax.rem(x + step, shards)]
        upper, lower = sources[n_rows + 2 * number : n_rows + 2 * number + 2]
        fc.append([Fetch(upper, targets[at], semaphores.at[at])])
        fc[-1].append(Fetch(lower, targets[at + 1], semaphores.at[at + 1]))
        terms.append(Fetch(shard.at[0, depth:, :units], targets[at + 2], semaphores.at[at + 2]))
        at += 3
    at_piece = at
    for number, step in enumerate((0, shards - 1, 1, 2)):
        shard = gathered.at[lax.rem(x + step, shards)]
        proj.append(
            [
                Fetch(
                    shard.at[piece, :depth, :],
                    targets[at].at[piece * depth : (piece + 1) * depth, :],
                    semaphores.at[at_piece + piece],
                )
                for piece in range(pieces)
            ]
        )
        at += 1
        at_piece += pieces
    if n_mine == 1:
        passes = [row_blocks]
    else:
        passes = [row_blocks[:n_mine], row_blocks[n_mine:]]
    for number, blocks in enumerate(passes):
        rows = jnp.concatenate([b.ref()[...] for b in blocks], axis=0)
        fours = mean_of_fours(rows.shape[0])
        total = None
        for (upper, lower), bias, projection, whole in zip(fc, terms, proj, targets[-shards:]):
            units = dot(rows[:, :FC_CUT], upper.ref()[...])
            units = units + dot(rows[:, FC_CUT:], lower.ref()[...])
            bias = jnp.sum(bias.ref()[...].astype(jnp.float32), axis=0, keepdims=True)
            units = units + bias
            units = 0.5 * units * (1.0 + lax.erf(units * (0.5**0.5)))
            mean = dot(fours, units.astype(jnp.bfloat16)).astype(jnp.bfloat16)
            for piece in projection:
                piece.ref()
            term = dot(mean, whole[...])
            total = term if total is None else total + term
        if len(passes) == 1:
            half = total.shape[0] // 2
            outs[0][...] = total[:half, :].astype(outs[0].dtype)
            outs[1][...] = total[half:, :].astype(outs[1].dtype)
        else:
            outs[number][...] = total.astype(outs[number].dtype)


def pooled_parts(mine, other, weights, here, name):
    rows, width = mine[0].shape
    *fc, proj = weights
    shards, pieces, _, _ = proj.shape
    units = fc[0].shape[1]
    fetched = [*mine, *other, *fc, proj]
    buffers = [pltpu.VMEM(a.shape, a.dtype) for a in (*mine, *other)]
    for number in range(shards):
        buffers += [pltpu.VMEM(a.shape, a.dtype) for a in fc[2 * number : 2 * number + 2]]
        buffers.append(pltpu.VMEM((16, units), proj.dtype))
    buffers += [pltpu.VMEM((units, width), proj.dtype)] * shards
    pooled_mine, pooled_other = len(mine) * rows // 4, len(other) * rows // 4
    return call(
        lambda *a: mlp_kernel(len(mine), len(other), *a),
        name,
        (
            jax.ShapeDtypeStruct((pooled_mine, width), jnp.float32),
            jax.ShapeDtypeStruct((pooled_other, width), jnp.bfloat16),
        ),
        2 * (pooled_mine + pooled_other) * 5 * width * units * shards,
        24,
        fetched,
        scalars=(here,),
        buffers=buffers,
        semaphores=len(buffers) + shards * pieces,
    )


def merge_kernel(_, sources, targets, semaphores, direct, outs, __):
    fetches = fetch_all(sources, targets, semaphores)
    parts, mixed_mean, w_merge = fetches[:5], fetches[5], fetches[6]
    b_proj, gain, b_merge, owners = direct
    (out,) = outs
    pooled = mixed_mean.ref()[...] + b_proj[...][None, :]
    for part in parts:
        pooled = pooled + part.ref()[...].astype(jnp.float32)
    rows = pooled.shape[0]
    merge_in = layer_norm(pooled, gain[...][None, :]).astype(jnp.bfloat16)
    merged = (dot(merge_in, w_merge.ref()[...]) + b_merge[...][None, :]).astype(jnp.bfloat16)
    owner = owners[...][None, :]
    earlier = iota((rows, rows), 0) < iota((rows, rows), 1)
    same = column_of(owner) == owner
    rank = jnp.sum(jnp.where(earlier & same, 1.0, 0.0), axis=0, keepdims=True).astype(jnp.int32)
    place = iota((out.shape[0], rows), 0)
    pick = (place // rows == owner) & (place % rows == rank)
    out[...] = dot(jnp.where(pick, 1.0, 0.0).astype(jnp.bfloat16), merged).astype(jnp.bfloat16)


def body(
    stream,
    queries,
    key_cache,
    value_cache,
    segments,
    stale_rows,
    owners,
    attn_gain,
    w_key,
    key_bias,
    mlp_gain,
    w_fc,
    b_fc,
    w_proj,
    b_proj,
    merge_gain,
    w_merge,
    b_merge,
):
    row_count = stream.shape[0]
    model_width = stream.shape[1]
    tok_count = lax.axis_size("tok")
    x_count = lax.axis_size("x")
    tok = lax.axis_index("tok")
    here = lax.axis_index("x").astype(jnp.int32).reshape(1)
    position = lax.axis_index(BLK).astype(jnp.int32).reshape(1)
    units_here = w_fc.shape[1]
    m = row_count // 4

    below_values = passed_along(value_cache, 1)
    above_values = passed_along(value_cache, -1)
    refreshed = call(
        refresh_kernel,
        "refresh",
        jax.ShapeDtypeStruct(key_cache.shape, jnp.bfloat16),
        2 * 16 * model_width * model_width,
        16,
        (stream, key_cache, w_key),
        (stale_rows, attn_gain, key_bias),
    )
    fc_a, fc_b = after(w_fc[:FC_CUT], stale_rows), w_fc[FC_CUT:]
    left_a = shift(fc_a, "x", 1)
    right_a = shift(fc_a, "x", -1)
    sent_keys = after(refreshed, below_values, above_values)
    below_keys = passed_along(sent_keys, 1)
    above_keys = passed_along(sent_keys, -1)
    sent_b = after(fc_b, below_keys, above_keys)
    left_b = shift(sent_b, "x", 1)
    right_b = shift(sent_b, "x", -1)
    far_a = shift(after(left_a, below_keys, above_keys), "x", 1)
    far_b = shift(right_b, "x", -1)
    proj_part = units_here // tok_count
    proj_piece = lax.dynamic_slice_in_dim(w_proj, tok * proj_part, proj_part, 0)
    terms = jnp.pad(three_terms(b_fc), ((0, 13), (0, model_width - units_here)))
    gathered = lax.all_gather(
        jnp.concatenate([proj_piece, terms], axis=0), ("x", "tok"), axis=0, tiled=False
    )
    gathered = gathered.reshape(x_count, tok_count, proj_part + 16, model_width)
    weights = (fc_a, fc_b, left_a, left_b, right_a, right_b, far_a, far_b, gathered)

    normed, mixed_mean = call(
        attention_kernel,
        "attention",
        (
            jax.ShapeDtypeStruct((row_count, model_width), jnp.bfloat16),
            jax.ShapeDtypeStruct((m, model_width), jnp.float32),
        ),
        24 * row_count * row_count * model_width,
        16,
        (
            queries,
            below_keys,
            refreshed,
            above_keys,
            below_values,
            value_cache,
            above_values,
            stream,
        ),
        (segments.reshape(-1, row_count), mlp_gain),
        scalars=(position,),
        scratch=(pltpu.VMEM((row_count, model_width), jnp.float32),),
    )

    z_low = shift(normed, "z", 1)
    z_high = shift(normed, "z", -1)
    z_far = shift(normed, "z", 2)
    swapped = shift(normed, "c", 1)
    near, near_sent = pooled_parts([normed], [swapped], weights, here, "mlp_near")
    z_low_other = shift(z_low, "c", 1)
    z_high_other = shift(z_high, "c", 1)
    next_to, next_sent = pooled_parts(
        [z_low, z_high], [z_low_other, z_high_other], weights, here, "mlp_next"
    )
    z_far_other = shift(z_far, "c", 1)
    far, far_sent = pooled_parts(
        [after(z_far, next_to)], [z_far_other], weights, here, "mlp_far"
    )

    near_other = shift(near_sent, "c", 1)
    next_other = shift(next_sent, "c", 1)
    next_sum = (next_to + next_other.astype(jnp.float32)).astype(jnp.bfloat16)
    from_high = shift(next_sum[:m], "z", -1)
    from_low = shift(next_sum[m:], "z", 1)
    far_other = shift(far_sent, "c", 1)
    far_sum = (far + far_other.astype(jnp.float32)).astype(jnp.bfloat16)
    from_far = shift(far_sum, "z", 2)
    outgoing = call(
        merge_kernel,
        "merge",
        jax.ShapeDtypeStruct((tok_count * m, model_width), jnp.bfloat16),
        2 * m * model_width * model_width,
        16,
        (near, near_other, from_low, from_high, from_far, mixed_mean, w_merge),
        (b_proj, merge_gain, b_merge, owners),
    ).reshape(tok_count, m, model_width)
    arrived = lax.all_to_all(outgoing, "tok", split_axis=0, concat_axis=0, tiled=True)
    delivered = arrived.reshape(1, 1, tok_count * m, model_width)
    return (refreshed, delivered)


def solution(mesh):
    fine = Mesh(mesh.devices.reshape(4, 4, 2, 4), ("x", "z", "c", "tok"))
    return jax.shard_map(
        body,
        mesh=fine,
        in_specs=(
            P(ROWS, None),
            P(ROWS, None),
            P(ROWS, None),
            P(ROWS, None),
            P("tok"),
            P(ROWS),
            P(ROWS),
            P(),
            P(),
            P(),
            P(),
            P(None, BLK),
            P(BLK),
            P(BLK, None),
            P(),
            P(),
            P(),
            P(),
        ),
        out_specs=(P(ROWS, None), P("tok", BLK, None, None)),
        check_vma=False,
    )
```

time: 203 us -> 147 us (0.72)
  waiting for transfers between devices: 71.1 us -> 25.8 us
  matrix products: 44.6 us -> 0 us
  Pallas kernels: 0 us -> 44.6 us
  starting transfers between devices: 10.1 us -> 40.5 us
  blocking collectives: 28 us -> 12 us
  local copies, waits for them, and re-layouts: 20.7 us -> 7.91 us
  other arithmetic: 13.6 us -> 1.56 us
    pallas_call x0 -> x6, Pallas kernels: none -> 44.6 us  [call(): pl.pallas_call(wrapped, out_shape=outs, in_specs=[pl.BlockSpec(memory_spa...]
    all_gather x3 -> x1, waiting for transfers between devices: 41.4 us -> 0.01 us  [body(): lax.all_gather(jnp.concatenate([proj_piece, terms], axis=0), ('x', 'tok')...]
    dot_general x8 -> x0, matrix products: 40.2 us -> none  [the longest x4 25.3 us: body(): jnp.dot(rows, fc_all[i], preferred_element_type=jnp.float32) + bias]
    ppermute x4 -> x23, starting transfers between devices: 9.96 us -> 40.4 us  [the longest x19 29 us: shift(): lax.ppermute(block, axis, [(i, (i + distance) % count) for i in range(cou...]
    reduce_scatter x1 -> x0, waiting for transfers between devices: 29.6 us -> none  [body(): lax.psum_scatter(partial.astype(jnp.bfloat16), ('z', 'c'), scatter_dimens...]
    ppermute x4 -> x23, waiting for transfers between devices: 0.01 us -> 25.7 us  [the longest x19 25.7 us: shift(): lax.ppermute(block, axis, [(i, (i + distance) % count) for i in range(cou...]
    all_gather x1 -> x0, blocking collectives: 16.4 us -> none  [body(): bias_all = lax.all_gather(b_fc, 'x', axis=0, tiled=True)]
    reduce_sum x12 -> x0, other arithmetic: 8.01 us -> none  [the longest x4 4.46 us: body(): jnp.mean(units.astype(jnp.float32).reshape(group_rows // 4, 4, units_here...]
  transfers between devices with their start and end apart: 8 -> 24, of which waited for: 3 -> 8; matrix products, arithmetic and copies ran while one was open for 32% -> 2% of each run, Pallas kernels for 0% -> 27%
where the time goes in v3:
time: 147 us
  Pallas kernels  44.6 us (30%)
  starting transfers between devices  40.5 us (28%)
  waiting for transfers between devices  25.8 us (18%)
  between operations  14.4 us (10%)
  blocking collectives  12 us (8%)
  local copies, waits for them, and re-layouts  7.91 us (5%)
  other arithmetic  1.56 us (1%)
    pallas_call x6, Pallas kernels, call(): pl.pallas_call(wrapped, out_shape=outs, in_specs=[pl.BlockSpec(memory_spa...  44.6 us
    ppermute x19, starting transfers between devices, shift(): lax.ppermute(block, axis, [(i, (i + distance) % count) for i in range(cou...  29 us
    ppermute x19, waiting for transfers between devices, shift(): lax.ppermute(block, axis, [(i, (i + distance) % count) for i in range(cou...  25.7 us
    all_to_all x1, blocking collectives, body(): lax.all_to_all(outgoing, 'tok', split_axis=0, concat_axis=0, tiled=True)  12 us
    ppermute x4, starting transfers between devices, passed_along(): return lax.ppermute(block, BLK, route)  11.4 us
    unnamed x47, local copies, waits for them, and re-layouts  5.65 us
  transfers between devices with their start and end apart: 24, of which 8 were waited for; matrix products, arithmetic and copies ran while one was open for 2% of the time, Pallas kernels for 27%

profile of v3, /device:TPU:0, one launch (start us, length us, event | category | flops | bytes accessed | tf_op | source)
XLA Modules:
  0.0 146.6 jit_solution(18003398634942402427)
XLA Ops:
  7.2 0.8 fusion.11
  9.1 1.3 collective-permute-start
  10.5 1.3 collective-permute-start.1
  11.8 5.4 %refresh.1.refs_3_ = bf16[128,1664]{1,0:T(8,128)(2,1)} custom-call(bf16[128,1664]{1,0:T(8,128)(2,1)} %refs_8_.2, bf16[128,1664]{1,0:T(8,128)(2,1)} %refs_1_.2, bf16[1664,1664]{1,0:T(8,128)(2,1)} %refs_2_.1, s32[12]{0:T(128)} %refs_3_.1, f32[1664]{0:T(1024)} %refs_4_.1, f32[1664]{0:T(1024)} %refs_5_.1), custom_call_target="tpu_custom_call" | custom-call | flops 88604672 | bytes 6389760 | tf_op jit(solution)/shard_map/refresh/pallas_call | solution.py:94
  17.2 7.5 %collective-permute-start.2 = (bf16[128,1664]{1,0:T(8,128)(2,1)}, bf16[128,1664]{1,0:T(8,128)(2,1)S(1)}, u32[]{:S(2)}, u32[]{:S(2)}) collective-permute-start(bf16[128,1664]{1,0:T(8,128)(2,1)} %refresh.1.refs_3_), channel_id=1, source_target_pairs={{0,4},{4,8},{8,12},{12,16},{16,20},{20,24},{24,28},{28,32},{32,36}... | collective-permute-start | bytes 1277960 | tf_op jit(solution)/shard_map/ppermute | solution.py:18
  24.8 1.3 collective-permute-start.3
  26.1 1.0 slice.12.refs_3_.refs_5_
  27.1 6.1 %collective-permute-start.5 = (bf16[768,256]{1,0:T(8,128)(2,1)S(1)}, bf16[768,256]{1,0:T(8,128)(2,1)S(1)}, u32[]{:S(2)}, u32[]{:S(2)}) collective-permute-start(bf16[768,256]{1,0:T(8,128)(2,1)S(1)} %slice.12.refs_3_.refs_5_), channel_id=1, source_target_pairs={{0,32},{32,64},{64,96},{96,0},{1,33},{33,65},{65,97},{97,1},{2,34}... | collective-permute-start | bytes 1179656 | tf_op jit(solution)/shard_map/ppermute | solution.py:23
  33.2 1.3 collective-permute-start.7
  34.6 7.7 %collective-permute-done.5.refs_5_.refs_7_ = bf16[768,256]{1,0:T(8,128)(2,1)S(1)} collective-permute-done((bf16[768,256]{1,0:T(8,128)(2,1)S(1)}, bf16[768,256]{1,0:T(8,128)(2,1)S(1)}, u32[]{:S(2)}, u32[]{:S(2)}) %collective-permute-start.5) | collective-permute-done | bytes 393248 | tf_op jit(solution)/shard_map/ppermute | solution.py:23
  42.3 0.8 copy-done.10
  43.1 0.8 copy-done.11
  43.9 1.2 slice.13.refs_4_.refs_6_
  45.1 3.3 %collective-permute-start.8 = (bf16[896,256]{1,0:T(8,128)(2,1)S(1)}, bf16[896,256]{1,0:T(8,128)(2,1)S(1)}, u32[]{:S(2)}, u32[]{:S(2)}) collective-permute-start(bf16[896,256]{1,0:T(8,128)(2,1)S(1)} %slice.13.refs_4_.refs_6_), channel_id=1, source_target_pairs={{0,96},{32,0},{64,32},{96,64},{1,97},{33,1},{65,33},{97,65},{2,98}... | collective-permute-start | bytes 1376264 | tf_op jit(solution)/shard_map/ppermute | solution.py:23
  48.4 8.7 %attention.1 = (bf16[128,1664]{1,0:T(8,128)(2,1)}, f32[32,1664]{1,0:T(8,128)}) custom-call(s32[1]{0:T(128)} %bitcast.1.refs_0_, bf16[128,1664]{1,0:T(8,128)(2,1)} %refs_1_.3, bf16[128,1664]{1,0:T(8,128)(2,1)} %copy-done.10, bf16[128,1664]{1,0:T(8,128)(2,1)} %refresh.1.refs_3_, bf16[128,1664]{1,0:T(8,128)(2,1)} %copy-done.11, bf16[128,1664]{1,0:T(8,128)(2,1)} %copy-done.8, ...), custom_call_target="tpu_custom_call" | custom-call | flops 654311424 | bytes 3407872 | tf_op jit(solution)/shard_map/attention/pallas_call | solution.py:94
  57.1 1.6 %collective-permute-start.12 = (bf16[128,1664]{1,0:T(8,128)(2,1)}, bf16[128,1664]{1,0:T(8,128)(2,1)S(1)}, u32[]{:S(2)}, u32[]{:S(2)}) collective-permute-start(bf16[128,1664]{1,0:T(8,128)(2,1)} %get-tuple-element.16.refs_1_), channel_id=1, source_target_pairs={{0,8},{8,16},{16,24},{24,0},{1,9},{9,17},{17,25},{25,1},{2,10},{10... | collective-permute-start | bytes 1277960 | tf_op jit(solution)/shard_map/ppermute | solution.py:23
  58.7 1.9 %collective-permute-start.13 = (bf16[128,1664]{1,0:T(8,128)(2,1)}, bf16[128,1664]{1,0:T(8,128)(2,1)S(1)}, u32[]{:S(2)}, u32[]{:S(2)}) collective-permute-start(bf16[128,1664]{1,0:T(8,128)(2,1)} %get-tuple-element.16.refs_1_), channel_id=1, source_target_pairs={{0,24},{8,0},{16,8},{24,16},{1,25},{9,1},{17,9},{25,17},{2,26},{10... | collective-permute-start | bytes 1277960 | tf_op jit(solution)/shard_map/ppermute | solution.py:23
  60.6 1.8 %collective-permute-start.19 = (bf16[128,1664]{1,0:T(8,128)(2,1)}, bf16[128,1664]{1,0:T(8,128)(2,1)}, u32[]{:S(2)}, u32[]{:S(2)}) collective-permute-start(bf16[128,1664]{1,0:T(8,128)(2,1)} %get-tuple-element.16.refs_1_), channel_id=1, source_target_pairs={{0,16},{8,24},{16,0},{24,8},{1,17},{9,25},{17,1},{25,9},{2,18},{10... | collective-permute-start | bytes 1277960 | tf_op jit(solution)/shard_map/ppermute | solution.py:23
  62.9 5.0 %collective-permute-done.8.refs_8_.refs_10_ = bf16[896,256]{1,0:T(8,128)(2,1)S(1)} collective-permute-done((bf16[896,256]{1,0:T(8,128)(2,1)S(1)}, bf16[896,256]{1,0:T(8,128)(2,1)S(1)}, u32[]{:S(2)}, u32[]{:S(2)}) %collective-permute-start.8) | collective-permute-done | bytes 458784 | tf_op jit(solution)/shard_map/ppermute | solution.py:23
  67.9 3.7 %collective-permute-start.10 = (bf16[896,256]{1,0:T(8,128)(2,1)S(1)}, bf16[896,256]{1,0:T(8,128)(2,1)S(1)}, u32[]{:S(2)}, u32[]{:S(2)}) collective-permute-start(bf16[896,256]{1,0:T(8,128)(2,1)S(1)} %collective-permute-done.8.refs_8_.refs_10_), channel_id=1, source_target_pairs={{0,96},{32,0},{64,32},{96,64},{1,97},{33,1},{65,33},{97,65},{2,98}... | collective-permute-start | bytes 1376264 | tf_op jit(solution)/shard_map/ppermute | solution.py:23
  71.6 7.3 %collective-permute-done.13.refs_2_ = bf16[128,1664]{1,0:T(8,128)(2,1)S(1)} collective-permute-done((bf16[128,1664]{1,0:T(8,128)(2,1)}, bf16[128,1664]{1,0:T(8,128)(2,1)S(1)}, u32[]{:S(2)}, u32[]{:S(2)}) %collective-permute-start.13) | collective-permute-done | bytes 426016 | tf_op jit(solution)/shard_map/ppermute | solution.py:23
  78.9 1.8 %collective-permute-done.19.refs_1_ = bf16[128,1664]{1,0:T(8,128)(2,1)} collective-permute-done((bf16[128,1664]{1,0:T(8,128)(2,1)}, bf16[128,1664]{1,0:T(8,128)(2,1)}, u32[]{:S(2)}, u32[]{:S(2)}) %collective-permute-start.19) | collective-permute-done | bytes 426016 | tf_op jit(solution)/shard_map/ppermute | solution.py:23
  82.0 0.8 copy-done.16
  83.9 10.7 %mlp_next.1 = (f32[64,1664]{1,0:T(8,128)}, bf16[64,1664]{1,0:T(8,128)(2,1)}) custom-call(s32[1]{0:T(128)} %bitcast.refs_0_, bf16[128,1664]{1,0:T(8,128)(2,1)} %copy-done.13, bf16[128,1664]{1,0:T(8,128)(2,1)} %copy-done.14, bf16[128,1664]{1,0:T(8,128)(2,1)} %copy-done.15, bf16[128,1664]{1,0:T(8,128)(2,1)} %copy-done.16, bf16[768,256]{1,0:T(8,128)(2,1)} %copy-done.2, ...), custom_call_target="tpu_custom_call" | custom-call | flops 2181038080 | bytes 9371648 | tf_op jit(solution)/shard_map/mlp_next/pallas_call | solution.py:94
  94.7 7.0 %mlp_far.1 = (f32[32,1664]{1,0:T(8,128)}, bf16[32,1664]{1,0:T(8,128)(2,1)}) custom-call(s32[1]{0:T(128)} %bitcast.refs_0_, bf16[128,1664]{1,0:T(8,128)(2,1)} %collective-permute-done.19.refs_1_, bf16[128,1664]{1,0:T(8,128)(2,1)} %collective-permute-done.20.refs_2_, bf16[768,256]{1,0:T(8,128)(2,1)} %copy-done.2, bf16[896,256]{1,0:T(8,128)(2,1)} %copy-done.1, ...), custom_call_target="tpu_custom_call" | custom-call | flops 1090519040 | bytes 8519680 | tf_op jit(solution)/shard_map/mlp_far/pallas_call | solution.py:94
  102.3 7.1 %mlp_near.1 = (f32[32,1664]{1,0:T(8,128)}, bf16[32,1664]{1,0:T(8,128)(2,1)}) custom-call(s32[1]{0:T(128)} %bitcast.refs_0_, bf16[128,1664]{1,0:T(8,128)(2,1)} %get-tuple-element.16.refs_1_, bf16[128,1664]{1,0:T(8,128)(2,1)} %collective-permute-done.4.refs_2_, bf16[768,256]{1,0:T(8,128)(2,1)} %copy-done.2, bf16[896,256]{1,0:T(8,128)(2,1)} %copy-done.1, ...), custom_call_target="tpu_custom_call" | custom-call | flops 1090519040 | bytes 8519680 | tf_op jit(solution)/shard_map/mlp_near/pallas_call | solution.py:94
  109.6 5.0 %collective-permute-start.22 = (bf16[32,1664]{1,0:T(8,128)(2,1)S(1)}, bf16[32,1664]{1,0:T(8,128)(2,1)S(1)}, u32[]{:S(2)}, u32[]{:S(2)}) collective-permute-start(bf16[32,1664]{1,0:T(8,128)(2,1)S(1)} %add_convert_fusion.1), channel_id=1, source_target_pairs={{0,16},{8,24},{16,0},{24,8},{1,17},{9,25},{17,1},{25,9},{2,18},{10... | collective-permute-start | bytes 319496 | tf_op jit(solution)/shard_map/ppermute | solution.py:23
  115.4 2.6 %collective-permute-start.18 = (bf16[32,1664]{1,0:T(8,128)(2,1)S(1)}, bf16[32,1664]{1,0:T(8,128)(2,1)S(1)}, u32[]{:S(2)}, u32[]{:S(2)}) collective-permute-start(bf16[32,1664]{1,0:T(8,128)(2,1)S(1)} %get-tuple-element.28), channel_id=1, source_target_pairs={{0,24},{8,0},{16,8},{24,16},{1,25},{9,1},{17,9},{25,17},{2,26},{10... | collective-permute-start | bytes 319496 | tf_op jit(solution)/shard_map/ppermute | solution.py:23
  118.0 2.7 %collective-permute-done.17.refs_2_ = bf16[32,1664]{1,0:T(8,128)(2,1)S(1)} collective-permute-done((bf16[32,1664]{1,0:T(8,128)(2,1)S(1)}, bf16[32,1664]{1,0:T(8,128)(2,1)S(1)}, u32[]{:S(2)}, u32[]{:S(2)}) %collective-permute-start.17) | collective-permute-done | bytes 106528 | tf_op jit(solution)/shard_map/ppermute | solution.py:23
  121.4 5.7 %merge.1 = bf16[128,1664]{1,0:T(8,128)(2,1)} custom-call(f32[32,1664]{1,0:T(8,128)} %get-tuple-element.20.refs_0_, bf16[32,1664]{1,0:T(8,128)(2,1)} %copy-done.18, bf16[32,1664]{1,0:T(8,128)(2,1)} %copy-done.20, bf16[32,1664]{1,0:T(8,128)(2,1)} %copy-done.21, bf16[32,1664]{1,0:T(8,128)(2,1)} %copy-done.19, f32[32,1664]{1,0:T(8,128)} %get-tuple-element.27.refs_5_, ...), custom_call_target="tpu_custom_call" | custom-call | flops 177209344 | bytes 6389760 | tf_op jit(solution)/shard_map/merge/pallas_call | solution.py:94
  127.1 12.0 %all_to_all.5 = bf16[4,32,1664]{2,1,0:T(8,128)(2,1)S(1)} all-to-all(bf16[4,32,1664]{2,1,0:T(8,128)(2,1)} %bitcast.10), channel_id=1, replica_groups=mesh['x'=4,'z'=4,'c'=2,'tok'=4] {'tok'}, dimensions={0} | all-to-all | bytes 851968 | tf_op jit(solution)/shard_map/all_to_all | solution.py:401
  139.0 0.8 copy.21
  (83 shorter events, 6.5 us)
Async XLA Ops:
  7.2 76.0 %all-gather.3.cloned.1.call-start = ((), (), s32[]{:S(2)}) async-start(), calls=%async_computation.1 | async-start | bytes 4526080 | tf_op jit(solution)/shard_map/all_gather | solution.py:339
  9.1 8.1 %collective-permute-start = (bf16[128,1664]{1,0:T(8,128)(2,1)}, bf16[128,1664]{1,0:T(8,128)(2,1)S(1)}, u32[]{:S(2)}, u32[]{:S(2)}) collective-permute-start(bf16[128,1664]{1,0:T(8,128)(2,1)} %refs_6_.2), channel_id=1, source_target_pairs={{0,4},{4,8},{8,12},{12,16},{16,20},{20,24},{24,28},{28,32},{32,36}... | collective-permute-start | bytes 1277960 | tf_op jit(solution)/shard_map/ppermute | solution.py:18
  10.5 6.7 %collective-permute-start.1 = (bf16[128,1664]{1,0:T(8,128)(2,1)}, bf16[128,1664]{1,0:T(8,128)(2,1)S(1)}, u32[]{:S(2)}, u32[]{:S(2)}) collective-permute-start(bf16[128,1664]{1,0:T(8,128)(2,1)} %refs_6_.2), channel_id=1, source_target_pairs={{4,0},{8,4},{12,8},{16,12},{20,16},{24,20},{28,24},{32,28},{36,32}... | collective-permute-start | bytes 1277960 | tf_op jit(solution)/shard_map/ppermute | solution.py:18
  17.2 31.1 %copy-start.8 = (bf16[128,1664]{1,0:T(8,128)(2,1)}, bf16[128,1664]{1,0:T(8,128)(2,1)S(1)}, u32[]{:S(2)}) copy-start(bf16[128,1664]{1,0:T(8,128)(2,1)S(1)} %collective-permute-done.refs_5_) | copy-start | bytes 1277956
  17.2 26.6 %copy-start.9 = (bf16[128,1664]{1,0:T(8,128)(2,1)}, bf16[128,1664]{1,0:T(8,128)(2,1)S(1)}, u32[]{:S(2)}) copy-start(bf16[128,1664]{1,0:T(8,128)(2,1)S(1)} %collective-permute-done.1.refs_7_) | copy-start | bytes 1277956
  17.2 25.1 %collective-permute-start.2 = (bf16[128,1664]{1,0:T(8,128)(2,1)}, bf16[128,1664]{1,0:T(8,128)(2,1)S(1)}, u32[]{:S(2)}, u32[]{:S(2)}) collective-permute-start(bf16[128,1664]{1,0:T(8,128)(2,1)} %refresh.1.refs_3_), channel_id=1, source_target_pairs={{0,4},{4,8},{8,12},{12,16},{16,20},{20,24},{24,28},{28,32},{32,36}... | collective-permute-start | bytes 1277960 | tf_op jit(solution)/shard_map/ppermute | solution.py:18
  24.8 17.5 %collective-permute-start.3 = (bf16[128,1664]{1,0:T(8,128)(2,1)}, bf16[128,1664]{1,0:T(8,128)(2,1)S(1)}, u32[]{:S(2)}, u32[]{:S(2)}) collective-permute-start(bf16[128,1664]{1,0:T(8,128)(2,1)} %refresh.1.refs_3_), channel_id=1, source_target_pairs={{4,0},{8,4},{12,8},{16,12},{20,16},{24,20},{28,24},{32,28},{36,32}... | collective-permute-start | bytes 1277960 | tf_op jit(solution)/shard_map/ppermute | solution.py:18
  27.1 56.1 %copy-start.2 = (bf16[768,256]{1,0:T(8,128)(2,1)}, bf16[768,256]{1,0:T(8,128)(2,1)S(1)}, u32[]{:S(2)}) copy-start(bf16[768,256]{1,0:T(8,128)(2,1)S(1)} %slice.12.refs_3_.refs_5_) | copy-start | bytes 1179652
  27.1 15.2 %collective-permute-start.5 = (bf16[768,256]{1,0:T(8,128)(2,1)S(1)}, bf16[768,256]{1,0:T(8,128)(2,1)S(1)}, u32[]{:S(2)}, u32[]{:S(2)}) collective-permute-start(bf16[768,256]{1,0:T(8,128)(2,1)S(1)} %slice.12.refs_3_.refs_5_), channel_id=1, source_target_pairs={{0,32},{32,64},{64,96},{96,0},{1,33},{33,65},{65,97},{97,1},{2,34}... | collective-permute-start | bytes 1179656 | tf_op jit(solution)/shard_map/ppermute | solution.py:23
  33.2 27.4 %collective-permute-start.7 = (bf16[768,256]{1,0:T(8,128)(2,1)S(1)}, bf16[768,256]{1,0:T(8,128)(2,1)S(1)}, u32[]{:S(2)}, u32[]{:S(2)}) collective-permute-start(bf16[768,256]{1,0:T(8,128)(2,1)S(1)} %slice.12.refs_3_.refs_5_), channel_id=1, source_target_pairs={{0,96},{32,0},{64,32},{96,64},{1,97},{33,1},{65,33},{97,65},{2,98}... | collective-permute-start | bytes 1179656 | tf_op jit(solution)/shard_map/ppermute | solution.py:23
  42.3 40.9 %copy-start.6 = (bf16[768,256]{1,0:T(8,128)(2,1)}, bf16[768,256]{1,0:T(8,128)(2,1)S(1)}, u32[]{:S(2)}) copy-start(bf16[768,256]{1,0:T(8,128)(2,1)S(1)} %collective-permute-done.5.refs_5_.refs_7_) | copy-start | bytes 1179652
  43.9 19.1 %collective-permute-start.9 = (bf16[768,256]{1,0:T(8,128)(2,1)S(1)}, bf16[768,256]{1,0:T(8,128)(2,1)}, u32[]{:S(2)}, u32[]{:S(2)}) collective-permute-start(bf16[768,256]{1,0:T(8,128)(2,1)S(1)} %collective-permute-done.5.refs_5_.refs_7_), channel_id=1, source_target_pairs={{0,32},{32,64},{64,96},{96,0},{1,33},{33,65},{65,97},{97,1},{2,34}... | collective-permute-start | bytes 1179656 | tf_op jit(solution)/shard_map/ppermute | solution.py:23
  45.1 38.1 %copy-start.1 = (bf16[896,256]{1,0:T(8,128)(2,1)}, bf16[896,256]{1,0:T(8,128)(2,1)S(1)}, u32[]{:S(2)}) copy-start(bf16[896,256]{1,0:T(8,128)(2,1)S(1)} %slice.13.refs_4_.refs_6_) | copy-start | bytes 1376260
  45.1 22.8 %collective-permute-start.8 = (bf16[896,256]{1,0:T(8,128)(2,1)S(1)}, bf16[896,256]{1,0:T(8,128)(2,1)S(1)}, u32[]{:S(2)}, u32[]{:S(2)}) collective-permute-start(bf16[896,256]{1,0:T(8,128)(2,1)S(1)} %slice.13.refs_4_.refs_6_), channel_id=1, source_target_pairs={{0,96},{32,0},{64,32},{96,64},{1,97},{33,1},{65,33},{97,65},{2,98}... | collective-permute-start | bytes 1376264 | tf_op jit(solution)/shard_map/ppermute | solution.py:23
  57.1 14.5 %collective-permute-start.12 = (bf16[128,1664]{1,0:T(8,128)(2,1)}, bf16[128,1664]{1,0:T(8,128)(2,1)S(1)}, u32[]{:S(2)}, u32[]{:S(2)}) collective-permute-start(bf16[128,1664]{1,0:T(8,128)(2,1)} %get-tuple-element.16.refs_1_), channel_id=1, source_target_pairs={{0,8},{8,16},{16,24},{24,0},{1,9},{9,17},{17,25},{25,1},{2,10},{10... | collective-permute-start | bytes 1277960 | tf_op jit(solution)/shard_map/ppermute | solution.py:23
  58.7 20.2 %collective-permute-start.13 = (bf16[128,1664]{1,0:T(8,128)(2,1)}, bf16[128,1664]{1,0:T(8,128)(2,1)S(1)}, u32[]{:S(2)}, u32[]{:S(2)}) collective-permute-start(bf16[128,1664]{1,0:T(8,128)(2,1)} %get-tuple-element.16.refs_1_), channel_id=1, source_target_pairs={{0,24},{8,0},{16,8},{24,16},{1,25},{9,1},{17,9},{25,17},{2,26},{10... | collective-permute-start | bytes 1277960 | tf_op jit(solution)/shard_map/ppermute | solution.py:23
  60.6 20.1 %collective-permute-start.19 = (bf16[128,1664]{1,0:T(8,128)(2,1)}, bf16[128,1664]{1,0:T(8,128)(2,1)}, u32[]{:S(2)}, u32[]{:S(2)}) collective-permute-start(bf16[128,1664]{1,0:T(8,128)(2,1)} %get-tuple-element.16.refs_1_), channel_id=1, source_target_pairs={{0,16},{8,24},{16,0},{24,8},{1,17},{9,25},{17,1},{25,9},{2,18},{10... | collective-permute-start | bytes 1277960 | tf_op jit(solution)/shard_map/ppermute | solution.py:23
  62.9 18.1 %collective-permute-start.6 = (bf16[896,256]{1,0:T(8,128)(2,1)S(1)}, bf16[896,256]{1,0:T(8,128)(2,1)S(1)}, u32[]{:S(2)}, u32[]{:S(2)}) collective-permute-start(bf16[896,256]{1,0:T(8,128)(2,1)S(1)} %slice.13.refs_4_.refs_6_), channel_id=1, source_target_pairs={{0,32},{32,64},{64,96},{96,0},{1,33},{33,65},{65,97},{97,1},{2,34}... | collective-permute-start | bytes 1376264 | tf_op jit(solution)/shard_map/ppermute | solution.py:23
  67.9 15.3 %copy-start.3 = (bf16[896,256]{1,0:T(8,128)(2,1)}, bf16[896,256]{1,0:T(8,128)(2,1)S(1)}, u32[]{:S(2)}) copy-start(bf16[896,256]{1,0:T(8,128)(2,1)S(1)} %collective-permute-done.8.refs_8_.refs_10_) | copy-start | bytes 1376260
  67.9 15.2 %collective-permute-start.10 = (bf16[896,256]{1,0:T(8,128)(2,1)S(1)}, bf16[896,256]{1,0:T(8,128)(2,1)S(1)}, u32[]{:S(2)}, u32[]{:S(2)}) collective-permute-start(bf16[896,256]{1,0:T(8,128)(2,1)S(1)} %collective-permute-done.8.refs_8_.refs_10_), channel_id=1, source_target_pairs={{0,96},{32,0},{64,32},{96,64},{1,97},{33,1},{65,33},{97,65},{2,98}... | collective-permute-start | bytes 1376264 | tf_op jit(solution)/shard_map/ppermute | solution.py:23
  71.6 9.6 %copy-start.13 = (bf16[128,1664]{1,0:T(8,128)(2,1)}, bf16[128,1664]{1,0:T(8,128)(2,1)S(1)}, u32[]{:S(2)}) copy-start(bf16[128,1664]{1,0:T(8,128)(2,1)S(1)} %collective-permute-done.12.refs_1_) | copy-start | bytes 1277956
  71.6 9.6 %collective-permute-start.14 = (bf16[128,1664]{1,0:T(8,128)(2,1)S(1)}, bf16[128,1664]{1,0:T(8,128)(2,1)S(1)}, u32[]{:S(2)}, u32[]{:S(2)}) collective-permute-start(bf16[128,1664]{1,0:T(8,128)(2,1)S(1)} %collective-permute-done.12.refs_1_), channel_id=1, source_target_pairs={{0,4},{4,0},{1,5},{5,1},{2,6},{6,2},{3,7},{7,3},{8,12},{12,8},{9,1... | collective-permute-start | bytes 1277960 | tf_op jit(solution)/shard_map/ppermute | solution.py:23
  78.9 2.3 %collective-permute-start.15 = (bf16[128,1664]{1,0:T(8,128)(2,1)S(1)}, bf16[128,1664]{1,0:T(8,128)(2,1)S(1)}, u32[]{:S(2)}, u32[]{:S(2)}) collective-permute-start(bf16[128,1664]{1,0:T(8,128)(2,1)S(1)} %collective-permute-done.13.refs_2_), channel_id=1, source_target_pairs={{0,4},{4,0},{1,5},{5,1},{2,6},{6,2},{3,7},{7,3},{8,12},{12,8},{9,1... | collective-permute-start | bytes 1277960 | tf_op jit(solution)/shard_map/ppermute | solution.py:23
  80.7 14.0 %collective-permute-start.20 = (bf16[128,1664]{1,0:T(8,128)(2,1)}, bf16[128,1664]{1,0:T(8,128)(2,1)}, u32[]{:S(2)}, u32[]{:S(2)}) collective-permute-start(bf16[128,1664]{1,0:T(8,128)(2,1)} %collective-permute-done.19.refs_1_), channel_id=1, source_target_pairs={{0,4},{4,0},{1,5},{5,1},{2,6},{6,2},{3,7},{7,3},{8,12},{12,8},{9,1... | collective-permute-start | bytes 1277960 | tf_op jit(solution)/shard_map/ppermute | solution.py:23
  81.0 21.3 %collective-permute-start.4 = (bf16[128,1664]{1,0:T(8,128)(2,1)}, bf16[128,1664]{1,0:T(8,128)(2,1)}, u32[]{:S(2)}, u32[]{:S(2)}) collective-permute-start(bf16[128,1664]{1,0:T(8,128)(2,1)} %get-tuple-element.16.refs_1_), channel_id=1, source_target_pairs={{0,4},{4,0},{1,5},{5,1},{2,6},{6,2},{3,7},{7,3},{8,12},{12,8},{9,1... | collective-permute-start | bytes 1277960 | tf_op jit(solution)/shard_map/ppermute | solution.py:23
  101.7 12.9 %copy-start.12 = (f32[64,1664]{1,0:T(8,128)S(1)}, f32[64,1664]{1,0:T(8,128)}, u32[]{:S(2)}) copy-start(f32[64,1664]{1,0:T(8,128)} %get-tuple-element.22) | copy-start | bytes 1277956
  101.7 7.8 %collective-permute-start.21 = (bf16[32,1664]{1,0:T(8,128)(2,1)}, bf16[32,1664]{1,0:T(8,128)(2,1)S(1)}, u32[]{:S(2)}, u32[]{:S(2)}) collective-permute-start(bf16[32,1664]{1,0:T(8,128)(2,1)} %get-tuple-element.26), channel_id=1, source_target_pairs={{0,4},{4,0},{1,5},{5,1},{2,6},{6,2},{3,7},{7,3},{8,12},{12,8},{9,1... | collective-permute-start | bytes 319496 | tf_op jit(solution)/shard_map/ppermute | solution.py:23
  101.8 12.8 %collective-permute-start.16 = (bf16[64,1664]{1,0:T(8,128)(2,1)S(1)}, bf16[64,1664]{1,0:T(8,128)(2,1)S(1)}, u32[]{:S(2)}, u32[]{:S(2)}) collective-permute-start(bf16[64,1664]{1,0:T(8,128)(2,1)S(1)} %copy-done.22), channel_id=1, source_target_pairs={{0,4},{4,0},{1,5},{5,1},{2,6},{6,2},{3,7},{7,3},{8,12},{12,8},{9,1... | collective-permute-start | bytes 638984 | tf_op jit(solution)/shard_map/ppermute | solution.py:23
  109.4 8.6 %collective-permute-start.11 = (bf16[32,1664]{1,0:T(8,128)(2,1)}, bf16[32,1664]{1,0:T(8,128)(2,1)S(1)}, u32[]{:S(2)}, u32[]{:S(2)}) collective-permute-start(bf16[32,1664]{1,0:T(8,128)(2,1)} %get-tuple-element.21), channel_id=1, source_target_pairs={{0,4},{4,0},{1,5},{5,1},{2,6},{6,2},{3,7},{7,3},{8,12},{12,8},{9,1... | collective-permute-start | bytes 319496 | tf_op jit(solution)/shard_map/ppermute | solution.py:23
  109.6 8.4 %collective-permute-start.22 = (bf16[32,1664]{1,0:T(8,128)(2,1)S(1)}, bf16[32,1664]{1,0:T(8,128)(2,1)S(1)}, u32[]{:S(2)}, u32[]{:S(2)}) collective-permute-start(bf16[32,1664]{1,0:T(8,128)(2,1)S(1)} %add_convert_fusion.1), channel_id=1, source_target_pairs={{0,16},{8,24},{16,0},{24,8},{1,17},{9,25},{17,1},{25,9},{2,18},{10... | collective-permute-start | bytes 319496 | tf_op jit(solution)/shard_map/ppermute | solution.py:23
  114.7 6.0 %collective-permute-start.17 = (bf16[32,1664]{1,0:T(8,128)(2,1)S(1)}, bf16[32,1664]{1,0:T(8,128)(2,1)S(1)}, u32[]{:S(2)}, u32[]{:S(2)}) collective-permute-start(bf16[32,1664]{1,0:T(8,128)(2,1)S(1)} %get-tuple-element.29), channel_id=1, source_target_pairs={{0,8},{8,16},{16,24},{24,0},{1,9},{9,17},{17,25},{25,1},{2,10},{10... | collective-permute-start | bytes 319496 | tf_op jit(solution)/shard_map/ppermute | solution.py:23
  115.4 5.3 %collective-permute-start.18 = (bf16[32,1664]{1,0:T(8,128)(2,1)S(1)}, bf16[32,1664]{1,0:T(8,128)(2,1)S(1)}, u32[]{:S(2)}, u32[]{:S(2)}) collective-permute-start(bf16[32,1664]{1,0:T(8,128)(2,1)S(1)} %get-tuple-element.28), channel_id=1, source_target_pairs={{0,24},{8,0},{16,8},{24,16},{1,25},{9,1},{17,9},{25,17},{2,26},{10... | collective-permute-start | bytes 319496 | tf_op jit(solution)/shard_map/ppermute | solution.py:23
  (15 other events, 33.0 us)
Sparse Core Ops, SparseCore 0:
  10.2 68.2 all-gather.2

commit v4 on v3

--- a/solution.py
+++ b/solution.py
@@ -206,11 +206,12 @@
         )
         at += 1
         at_piece += pieces
-    if n_mine == 1:
-        passes = [row_blocks]
-    else:
-        passes = [row_blocks[:n_mine], row_blocks[n_mine:]]
-    for number, blocks in enumerate(passes):
+    passes = [
+        (out, first // 2, row_blocks[base + first : base + first + 2])
+        for out, base, count in ((outs[0], 0, n_mine), (outs[1], n_mine, n_other))
+        for first in range(0, count, 2)
+    ]
+    for out, number, blocks in passes:
         rows = jnp.concatenate([b.ref()[...] for b in blocks], axis=0)
         fours = mean_of_fours(rows.shape[0])
         total = None
@@ -225,12 +226,8 @@
                 piece.ref()
             term = dot(mean, whole[...])
             total = term if total is None else total + term
-        if len(passes) == 1:
-            half = total.shape[0] // 2
-            outs[0][...] = total[:half, :].astype(outs[0].dtype)
-            outs[1][...] = total[half:, :].astype(outs[1].dtype)
-        else:
-            outs[number][...] = total.astype(outs[number].dtype)
+        count = total.shape[0]
+        out[number * count : (number + 1) * count, :] = total.astype(out.dtype)
 
 
 def pooled_parts(mine, other, weights, here, name):
@@ -262,8 +259,17 @@
 
 
 def merge_kernel(_, sources, targets, semaphores, direct, outs, __):
-    fetches = fetch_all(sources, targets, semaphores)
-    parts, mixed_mean, w_merge = fetches[:5], fetches[5], fetches[6]
+    fetches = fetch_all(sources[:5], targets, semaphores)
+    w_source = sources[5]
+    parts, mixed_mean = fetches[:4], fetches[4]
+    depth = w_source.shape[0]
+    cuts = [(low, min(low + 512, depth)) for low in range(0, depth, 512)]
+    w_merge = [
+        Fetch(
+            w_source.at[low:high, :], targets[5].at[low:high, :], semaphores.at[5 + i]
+        )
+        for i, (low, high) in enumerate(cuts)
+    ]
     b_proj, gain, b_merge, owners = direct
     (out,) = outs
     pooled = mixed_mean.ref()[...] + b_proj[...][None, :]
@@ -271,7 +277,10 @@
         pooled = pooled + part.ref()[...].astype(jnp.float32)
     rows = pooled.shape[0]
     merge_in = layer_norm(pooled, gain[...][None, :]).astype(jnp.bfloat16)
-    merged = (dot(merge_in, w_merge.ref()[...]) + b_merge[...][None, :]).astype(jnp.bfloat16)
+    merged = b_merge[...][None, :]
+    for (low, high), fetch in zip(cuts, w_merge):
+        merged = merged + dot(merge_in[:, low:high], fetch.ref()[...])
+    merged = merged.astype(jnp.bfloat16)
     owner = owners[...][None, :]
     earlier = iota((rows, rows), 0) < iota((rows, rows), 1)
     same = column_of(owner) == owner
@@ -331,7 +340,7 @@
     sent_b = after(fc_b, below_keys, above_keys)
     left_b = shift(sent_b, "x", 1)
     right_b = shift(sent_b, "x", -1)
-    far_a = shift(after(left_a, below_keys, above_keys), "x", 1)
+    far_a = shift(left_a, "x", 1)
     far_b = shift(right_b, "x", -1)
     proj_part = units_here // tok_count
     proj_piece = lax.dynamic_slice_in_dim(w_proj, tok * proj_part, proj_part, 0)
@@ -370,33 +379,31 @@
     z_high = shift(normed, "z", -1)
     z_far = shift(normed, "z", 2)
     swapped = shift(normed, "c", 1)
-    near, near_sent = pooled_parts([normed], [swapped], weights, here, "mlp_near")
     z_low_other = shift(z_low, "c", 1)
     z_high_other = shift(z_high, "c", 1)
-    next_to, next_sent = pooled_parts(
-        [z_low, z_high], [z_low_other, z_high_other], weights, here, "mlp_next"
-    )
     z_far_other = shift(z_far, "c", 1)
-    far, far_sent = pooled_parts(
-        [after(z_far, next_to)], [z_far_other], weights, here, "mlp_far"
-    )
-
-    near_other = shift(near_sent, "c", 1)
-    next_other = shift(next_sent, "c", 1)
-    next_sum = (next_to + next_other.astype(jnp.float32)).astype(jnp.bfloat16)
-    from_high = shift(next_sum[:m], "z", -1)
-    from_low = shift(next_sum[m:], "z", 1)
-    far_other = shift(far_sent, "c", 1)
-    far_sum = (far + far_other.astype(jnp.float32)).astype(jnp.bfloat16)
-    from_far = shift(far_sum, "z", 2)
+    mine, sent = pooled_parts(
+        [normed, z_low, z_high, z_far],
+        [swapped, z_low_other, z_high_other, z_far_other],
+        weights,
+        here,
+        "mlp",
+    )
+
+    sums = mine + shift(sent, "c", 1).astype(jnp.float32)
+    own = sums[:m]
+    from_high = shift(sums[m : 2 * m].astype(jnp.bfloat16), "z", -1)
+    from_low = shift(sums[2 * m : 3 * m].astype(jnp.bfloat16), "z", 1)
+    from_far = shift(sums[3 * m :].astype(jnp.bfloat16), "z", 2)
     outgoing = call(
         merge_kernel,
         "merge",
         jax.ShapeDtypeStruct((tok_count * m, model_width), jnp.bfloat16),
         2 * m * model_width * model_width,
         16,
-        (near, near_other, from_low, from_high, from_far, mixed_mean, w_merge),
+        (own, from_low, from_high, from_far, mixed_mean, w_merge),
         (b_proj, merge_gain, b_merge, owners),
+        semaphores=9,
     ).reshape(tok_count, m, model_width)
     arrived = lax.all_to_all(outgoing, "tok", split_axis=0, concat_axis=0, tiled=True)
     delivered = arrived.reshape(1, 1, tok_count * m, model_width)

time: 147 us -> 142 us (0.966)
  Pallas kernels: 44.6 us -> 37.9 us
  waiting for transfers between devices: 25.8 us -> 30.5 us
  starting transfers between devices: 40.5 us -> 36.6 us
  local copies, waits for them, and re-layouts: 7.91 us -> 5.79 us
    pallas_call x6 -> x4, Pallas kernels: 44.6 us -> 37.9 us  [call(): pl.pallas_call(wrapped, out_shape=outs, in_specs=[pl.BlockSpec(memory_spa...]
    ppermute x19 -> x17, waiting for transfers between devices: 25.7 us -> 30.5 us  [shift(): lax.ppermute(block, axis, [(i, (i + distance) % count) for i in range(cou...]
    ppermute x4, starting transfers between devices: 11.4 us -> 7.71 us  [passed_along(): return lax.ppermute(block, BLK, route)]
    unnamed x47 -> x39, local copies, waits for them, and re-layouts: 5.65 us -> 3.23 us
    ppermute x19 -> x17, starting transfers between devices: 29 us -> 28.8 us  [shift(): lax.ppermute(block, axis, [(i, (i + distance) % count) for i in range(cou...]
  transfers between devices with their start and end apart: 24 -> 22, of which waited for: 8 -> 8; matrix products, arithmetic and copies ran while one was open for 2% -> 2% of each run, Pallas kernels for 27% -> 10%
where the time goes in v4:
time: 142 us; the launch traced here: 141 us
  Pallas kernels  37.9 us (27%)
  starting transfers between devices  36.6 us (26%)
  waiting for transfers between devices  30.5 us (21%)
  between operations  14.4 us (10%)
  blocking collectives  13.1 us (9%)
  local copies, waits for them, and re-layouts  5.79 us (4%)
  other arithmetic  2.82 us (2%)
    pallas_call x4, Pallas kernels, call(): pl.pallas_call(wrapped, out_shape=outs, in_specs=[pl.BlockSpec(memory_spa...  37.9 us
    ppermute x17, waiting for transfers between devices, shift(): lax.ppermute(block, axis, [(i, (i + distance) % count) for i in range(cou...  30.5 us
    ppermute x17, starting transfers between devices, shift(): lax.ppermute(block, axis, [(i, (i + distance) % count) for i in range(cou...  28.8 us
    all_to_all x1, blocking collectives, body(): lax.all_to_all(outgoing, 'tok', split_axis=0, concat_axis=0, tiled=True)  13.1 us
    ppermute x4, starting transfers between devices, passed_along(): return lax.ppermute(block, BLK, route)  7.71 us
    unnamed x39, local copies, waits for them, and re-layouts  3.23 us
  transfers between devices with their start and end apart: 22, of which 8 were waited for; matrix products, arithmetic and copies ran while one was open for 2% of the time, Pallas kernels for 10%

profile of v4, /device:TPU:0, one launch (start us, length us, event | category | flops | bytes accessed | tf_op | source)
XLA Modules:
  0.0 141.0 jit_solution(9866914890506406353)
XLA Ops:
  7.2 0.8 fusion.12
  8.4 0.8 pad_maximum_fusion
  9.2 1.3 collective-permute-start
  10.5 1.3 collective-permute-start.1
  11.8 1.8 %slice.21.refs_9_ = bf16[768,256]{1,0:T(8,128)(2,1)} slice(bf16[1664,256]{1,0:T(8,128)(2,1)} %param.29), slice={[0:768], [0:256]} | slice | bytes 786432 | tf_op jit(solution)/shard_map/slice | solution.py:334
  13.6 6.6 %collective-permute-start.11 = (bf16[768,256]{1,0:T(8,128)(2,1)}, bf16[768,256]{1,0:T(8,128)(2,1)}, u32[]{:S(2)}, u32[]{:S(2)}) collective-permute-start(bf16[768,256]{1,0:T(8,128)(2,1)} %slice.21.refs_9_), channel_id=1, source_target_pairs={{0,32},{32,64},{64,96},{96,0},{1,33},{33,65},{65,97},{97,1},{2,34}... | collective-permute-start | bytes 1179656 | tf_op jit(solution)/shard_map/ppermute | solution.py:23
  20.2 5.6 %refresh.1.refs_3_ = bf16[128,1664]{1,0:T(8,128)(2,1)} custom-call(bf16[128,1664]{1,0:T(8,128)(2,1)} %refs_8_.2, bf16[128,1664]{1,0:T(8,128)(2,1)} %refs_1_.2, bf16[1664,1664]{1,0:T(8,128)(2,1)} %refs_2_.1, s32[12]{0:T(128)} %refs_3_.1, f32[1664]{0:T(1024)} %refs_4_.1, f32[1664]{0:T(1024)} %refs_5_.2), custom_call_target="tpu_custom_call" | custom-call | flops 88604672 | bytes 6389760 | tf_op jit(solution)/shard_map/refresh/pallas_call | solution.py:94
  25.9 1.3 collective-permute-start.3
  27.2 3.8 %collective-permute-start.2 = (bf16[128,1664]{1,0:T(8,128)(2,1)}, bf16[128,1664]{1,0:T(8,128)(2,1)}, u32[]{:S(2)}, u32[]{:S(2)}) collective-permute-start(bf16[128,1664]{1,0:T(8,128)(2,1)} %refresh.1.refs_3_), channel_id=1, source_target_pairs={{0,4},{4,8},{8,12},{12,16},{16,20},{20,24},{24,28},{28,32},{32,36}... | collective-permute-start | bytes 1277960 | tf_op jit(solution)/shard_map/ppermute | solution.py:18
  31.0 2.5 %collective-permute-start.13 = (bf16[768,256]{1,0:T(8,128)(2,1)}, bf16[768,256]{1,0:T(8,128)(2,1)}, u32[]{:S(2)}, u32[]{:S(2)}) collective-permute-start(bf16[768,256]{1,0:T(8,128)(2,1)} %slice.21.refs_9_), channel_id=1, source_target_pairs={{0,96},{32,0},{64,32},{96,64},{1,97},{33,1},{65,33},{97,65},{2,98}... | collective-permute-start | bytes 1179656 | tf_op jit(solution)/shard_map/ppermute | solution.py:23
  33.6 14.4 %collective-permute-start.14 = (bf16[896,256]{1,0:T(8,128)(2,1)S(1)}, bf16[896,256]{1,0:T(8,128)(2,1)S(1)}, u32[]{:S(2)}, u32[]{:S(2)}) collective-permute-start(bf16[896,256]{1,0:T(8,128)(2,1)S(1)} %slice.22.refs_10_), channel_id=1, source_target_pairs={{0,96},{32,0},{64,32},{96,64},{1,97},{33,1},{65,33},{97,65},{2,98}... | collective-permute-start | bytes 1376264 | tf_op jit(solution)/shard_map/ppermute | solution.py:23
  47.9 8.7 %attention.1 = (bf16[128,1664]{1,0:T(8,128)(2,1)}, f32[32,1664]{1,0:T(8,128)}) custom-call(s32[1]{0:T(128)} %bitcast.1.refs_0_, bf16[128,1664]{1,0:T(8,128)(2,1)} %refs_1_.3, bf16[128,1664]{1,0:T(8,128)(2,1)} %collective-permute-done.2.refs_2_, bf16[128,1664]{1,0:T(8,128)(2,1)} %refresh.1.refs_3_, bf16[128,1664]{1,0:T(8,128)(2,1)} %copy-done.5, ...), custom_call_target="tpu_custom_call" | custom-call | flops 654311424 | bytes 3407872 | tf_op jit(solution)/shard_map/attention/pallas_call | solution.py:94
  56.9 2.0 %collective-permute-start.4 = (bf16[128,1664]{1,0:T(8,128)(2,1)}, bf16[128,1664]{1,0:T(8,128)(2,1)S(1)}, u32[]{:S(2)}, u32[]{:S(2)}) collective-permute-start(bf16[128,1664]{1,0:T(8,128)(2,1)} %get-tuple-element.10.refs_1_), channel_id=1, source_target_pairs={{0,8},{8,16},{16,24},{24,0},{1,9},{9,17},{17,25},{25,1},{2,10},{10... | collective-permute-start | bytes 1277960 | tf_op jit(solution)/shard_map/ppermute | solution.py:23
  59.0 11.9 %collective-permute-done.14.refs_14_ = bf16[896,256]{1,0:T(8,128)(2,1)S(1)} collective-permute-done((bf16[896,256]{1,0:T(8,128)(2,1)S(1)}, bf16[896,256]{1,0:T(8,128)(2,1)S(1)}, u32[]{:S(2)}, u32[]{:S(2)}) %collective-permute-start.14) | collective-permute-done | bytes 458784 | tf_op jit(solution)/shard_map/ppermute | solution.py:23
  70.9 0.8 collective-permute-start.16
  71.7 2.5 %collective-permute-done.5.refs_3_ = bf16[128,1664]{1,0:T(8,128)(2,1)S(1)} collective-permute-done((bf16[128,1664]{1,0:T(8,128)(2,1)}, bf16[128,1664]{1,0:T(8,128)(2,1)S(1)}, u32[]{:S(2)}, u32[]{:S(2)}) %collective-permute-start.5) | collective-permute-done | bytes 426016 | tf_op jit(solution)/shard_map/ppermute | solution.py:23
  74.2 5.7 %collective-permute-done.4.refs_2_ = bf16[128,1664]{1,0:T(8,128)(2,1)S(1)} collective-permute-done((bf16[128,1664]{1,0:T(8,128)(2,1)}, bf16[128,1664]{1,0:T(8,128)(2,1)S(1)}, u32[]{:S(2)}, u32[]{:S(2)}) %collective-permute-start.4) | collective-permute-done | bytes 426016 | tf_op jit(solution)/shard_map/ppermute | solution.py:23
  79.9 1.7 %collective-permute-done.8.refs_6_ = bf16[128,1664]{1,0:T(8,128)(2,1)S(1)} collective-permute-done((bf16[128,1664]{1,0:T(8,128)(2,1)S(1)}, bf16[128,1664]{1,0:T(8,128)(2,1)S(1)}, u32[]{:S(2)}, u32[]{:S(2)}) %collective-permute-start.8) | collective-permute-done | bytes 426016 | tf_op jit(solution)/shard_map/ppermute | solution.py:23
  81.6 0.8 copy-done.18
  82.4 0.7 collective-permute-done.16.refs_16_
  83.2 0.7 copy-done.11
  83.9 18.3 %mlp.1 = (f32[128,1664]{1,0:T(8,128)}, bf16[128,1664]{1,0:T(8,128)(2,1)}) custom-call(s32[1]{0:T(128)} %bitcast.refs_0_, bf16[128,1664]{1,0:T(8,128)(2,1)} %get-tuple-element.10.refs_1_, bf16[128,1664]{1,0:T(8,128)(2,1)} %copy-done.15, bf16[128,1664]{1,0:T(8,128)(2,1)} %copy-done.14, bf16[128,1664]{1,0:T(8,128)(2,1)} %copy-done.13, ...), custom_call_target="tpu_custom_call" | custom-call | flops 4362076160 | bytes 11075584 | tf_op jit(solution)/shard_map/mlp/pallas_call | solution.py:94
  102.3 2.0 %collective-permute-done.17 = bf16[128,1664]{1,0:T(8,128)(2,1)S(1)} collective-permute-done((bf16[128,1664]{1,0:T(8,128)(2,1)}, bf16[128,1664]{1,0:T(8,128)(2,1)S(1)}, u32[]{:S(2)}, u32[]{:S(2)}) %collective-permute-start.17) | collective-permute-done | bytes 426016 | tf_op jit(solution)/shard_map/ppermute | solution.py:23
  104.3 1.2 fusion.10
  105.7 0.7 collective-permute-start.19
  106.4 1.4 collective-permute-start.18
  107.8 0.7 slice.27.refs_0_
  108.5 4.5 %collective-permute-done.20.refs_3_ = bf16[32,1664]{1,0:T(8,128)(2,1)S(1)} collective-permute-done((bf16[32,1664]{1,0:T(8,128)(2,1)S(1)}, bf16[32,1664]{1,0:T(8,128)(2,1)S(1)}, u32[]{:S(2)}, u32[]{:S(2)}) %collective-permute-start.20) | collective-permute-done | bytes 106528 | tf_op jit(solution)/shard_map/ppermute | solution.py:23
  113.0 1.5 %collective-permute-done.18.refs_1_ = bf16[32,1664]{1,0:T(8,128)(2,1)S(1)} collective-permute-done((bf16[32,1664]{1,0:T(8,128)(2,1)S(1)}, bf16[32,1664]{1,0:T(8,128)(2,1)S(1)}, u32[]{:S(2)}, u32[]{:S(2)}) %collective-permute-start.18) | collective-permute-done | bytes 106528 | tf_op jit(solution)/shard_map/ppermute | solution.py:23
  115.1 5.2 %merge.1 = bf16[128,1664]{1,0:T(8,128)(2,1)} custom-call(f32[32,1664]{1,0:T(8,128)} %slice.27.refs_0_, bf16[32,1664]{1,0:T(8,128)(2,1)} %copy-done.8, bf16[32,1664]{1,0:T(8,128)(2,1)} %copy-done.7, bf16[32,1664]{1,0:T(8,128)(2,1)} %copy-done.6, f32[32,1664]{1,0:T(8,128)} %get-tuple-element.15.refs_4_, bf16[1664,1664]{1,0:T(8,128)(2,1)} %refs_5_.3, ...), custom_call_target="tpu_custom_call" | custom-call | flops 177209344 | bytes 6283264 | tf_op jit(solution)/shard_map/merge/pallas_call | solution.py:94
  120.3 13.1 %all_to_all.5 = bf16[4,32,1664]{2,1,0:T(8,128)(2,1)S(1)} all-to-all(bf16[4,32,1664]{2,1,0:T(8,128)(2,1)} %bitcast.7), channel_id=1, replica_groups=mesh['x'=4,'z'=4,'c'=2,'tok'=4] {'tok'}, dimensions={0} | all-to-all | bytes 851968 | tf_op jit(solution)/shard_map/all_to_all | solution.py:408
  133.4 0.8 copy.21
  (69 shorter events, 1.6 us)
Async XLA Ops:
  7.2 26.3 %copy-start.1 = (bf16[1664,256]{1,0:T(8,128)(2,1)S(1)}, bf16[1664,256]{1,0:T(8,128)(2,1)}, u32[]{:S(2)}) copy-start(bf16[1664,256]{1,0:T(8,128)(2,1)} %param.29) | copy-start | bytes 2555908
  7.2 75.9 %all-gather.3.cloned.1.call-start = ((), (), s32[]{:S(2)}) async-start(), calls=%async_computation.1 | async-start | bytes 4526080 | tf_op jit(solution)/shard_map/all_gather | solution.py:348
  9.2 16.7 %collective-permute-start = (bf16[128,1664]{1,0:T(8,128)(2,1)}, bf16[128,1664]{1,0:T(8,128)(2,1)S(1)}, u32[]{:S(2)}, u32[]{:S(2)}) collective-permute-start(bf16[128,1664]{1,0:T(8,128)(2,1)} %refs_6_.2), channel_id=1, source_target_pairs={{0,4},{4,8},{8,12},{12,16},{16,20},{20,24},{24,28},{28,32},{32,36}... | collective-permute-start | bytes 1277960 | tf_op jit(solution)/shard_map/ppermute | solution.py:18
  10.5 15.4 %collective-permute-start.1 = (bf16[128,1664]{1,0:T(8,128)(2,1)}, bf16[128,1664]{1,0:T(8,128)(2,1)S(1)}, u32[]{:S(2)}, u32[]{:S(2)}) collective-permute-start(bf16[128,1664]{1,0:T(8,128)(2,1)} %refs_6_.2), channel_id=1, source_target_pairs={{4,0},{8,4},{12,8},{16,12},{20,16},{24,20},{28,24},{32,28},{36,32}... | collective-permute-start | bytes 1277960 | tf_op jit(solution)/shard_map/ppermute | solution.py:18
  13.6 19.9 %collective-permute-start.11 = (bf16[768,256]{1,0:T(8,128)(2,1)}, bf16[768,256]{1,0:T(8,128)(2,1)}, u32[]{:S(2)}, u32[]{:S(2)}) collective-permute-start(bf16[768,256]{1,0:T(8,128)(2,1)} %slice.21.refs_9_), channel_id=1, source_target_pairs={{0,32},{32,64},{64,96},{96,0},{1,33},{33,65},{65,97},{97,1},{2,34}... | collective-permute-start | bytes 1179656 | tf_op jit(solution)/shard_map/ppermute | solution.py:23
  25.9 22.1 %copy-start.3 = (bf16[128,1664]{1,0:T(8,128)(2,1)}, bf16[128,1664]{1,0:T(8,128)(2,1)S(1)}, u32[]{:S(2)}) copy-start(bf16[128,1664]{1,0:T(8,128)(2,1)S(1)} %collective-permute-done.refs_5_) | copy-start | bytes 1277956
  25.9 22.1 %copy-start.4 = (bf16[128,1664]{1,0:T(8,128)(2,1)}, bf16[128,1664]{1,0:T(8,128)(2,1)S(1)}, u32[]{:S(2)}) copy-start(bf16[128,1664]{1,0:T(8,128)(2,1)S(1)} %collective-permute-done.1.refs_7_) | copy-start | bytes 1277956
  25.9 7.6 %collective-permute-start.3 = (bf16[128,1664]{1,0:T(8,128)(2,1)}, bf16[128,1664]{1,0:T(8,128)(2,1)S(1)}, u32[]{:S(2)}, u32[]{:S(2)}) collective-permute-start(bf16[128,1664]{1,0:T(8,128)(2,1)} %refresh.1.refs_3_), channel_id=1, source_target_pairs={{4,0},{8,4},{12,8},{16,12},{20,16},{24,20},{28,24},{32,28},{36,32}... | collective-permute-start | bytes 1277960 | tf_op jit(solution)/shard_map/ppermute | solution.py:18
  27.2 6.4 %collective-permute-start.2 = (bf16[128,1664]{1,0:T(8,128)(2,1)}, bf16[128,1664]{1,0:T(8,128)(2,1)}, u32[]{:S(2)}, u32[]{:S(2)}) collective-permute-start(bf16[128,1664]{1,0:T(8,128)(2,1)} %refresh.1.refs_3_), channel_id=1, source_target_pairs={{0,4},{4,8},{8,12},{12,16},{16,20},{20,24},{24,28},{28,32},{32,36}... | collective-permute-start | bytes 1277960 | tf_op jit(solution)/shard_map/ppermute | solution.py:18
  31.0 25.9 %collective-permute-start.13 = (bf16[768,256]{1,0:T(8,128)(2,1)}, bf16[768,256]{1,0:T(8,128)(2,1)}, u32[]{:S(2)}, u32[]{:S(2)}) collective-permute-start(bf16[768,256]{1,0:T(8,128)(2,1)} %slice.21.refs_9_), channel_id=1, source_target_pairs={{0,96},{32,0},{64,32},{96,64},{1,97},{33,1},{65,33},{97,65},{2,98}... | collective-permute-start | bytes 1179656 | tf_op jit(solution)/shard_map/ppermute | solution.py:23
  33.5 23.5 %collective-permute-start.15 = (bf16[768,256]{1,0:T(8,128)(2,1)}, bf16[768,256]{1,0:T(8,128)(2,1)}, u32[]{:S(2)}, u32[]{:S(2)}) collective-permute-start(bf16[768,256]{1,0:T(8,128)(2,1)} %collective-permute-done.11.refs_11_), channel_id=1, source_target_pairs={{0,32},{32,64},{64,96},{96,0},{1,33},{33,65},{65,97},{97,1},{2,34}... | collective-permute-start | bytes 1179656 | tf_op jit(solution)/shard_map/ppermute | solution.py:23
  33.5 49.6 %copy-start.2 = (bf16[896,256]{1,0:T(8,128)(2,1)}, bf16[896,256]{1,0:T(8,128)(2,1)S(1)}, u32[]{:S(2)}) copy-start(bf16[896,256]{1,0:T(8,128)(2,1)S(1)} %slice.22.refs_10_) | copy-start | bytes 1376260
  33.5 14.4 %copy-start.5 = (bf16[128,1664]{1,0:T(8,128)(2,1)}, bf16[128,1664]{1,0:T(8,128)(2,1)S(1)}, u32[]{:S(2)}) copy-start(bf16[128,1664]{1,0:T(8,128)(2,1)S(1)} %collective-permute-done.3.refs_4_) | copy-start | bytes 1277956
  33.6 37.3 %collective-permute-start.14 = (bf16[896,256]{1,0:T(8,128)(2,1)S(1)}, bf16[896,256]{1,0:T(8,128)(2,1)S(1)}, u32[]{:S(2)}, u32[]{:S(2)}) collective-permute-start(bf16[896,256]{1,0:T(8,128)(2,1)S(1)} %slice.22.refs_10_), channel_id=1, source_target_pairs={{0,96},{32,0},{64,32},{96,64},{1,97},{33,1},{65,33},{97,65},{2,98}... | collective-permute-start | bytes 1376264 | tf_op jit(solution)/shard_map/ppermute | solution.py:23
  56.7 2.3 %collective-permute-start.7 = (bf16[128,1664]{1,0:T(8,128)(2,1)}, bf16[128,1664]{1,0:T(8,128)(2,1)S(1)}, u32[]{:S(2)}, u32[]{:S(2)}) collective-permute-start(bf16[128,1664]{1,0:T(8,128)(2,1)} %get-tuple-element.10.refs_1_), channel_id=1, source_target_pairs={{0,4},{4,0},{1,5},{5,1},{2,6},{6,2},{3,7},{7,3},{8,12},{12,8},{9,1... | collective-permute-start | bytes 1277960 | tf_op jit(solution)/shard_map/ppermute | solution.py:23
  56.8 14.9 %collective-permute-start.6 = (bf16[128,1664]{1,0:T(8,128)(2,1)}, bf16[128,1664]{1,0:T(8,128)(2,1)S(1)}, u32[]{:S(2)}, u32[]{:S(2)}) collective-permute-start(bf16[128,1664]{1,0:T(8,128)(2,1)} %get-tuple-element.10.refs_1_), channel_id=1, source_target_pairs={{0,16},{8,24},{16,0},{24,8},{1,17},{9,25},{17,1},{25,9},{2,18},{10... | collective-permute-start | bytes 1277960 | tf_op jit(solution)/shard_map/ppermute | solution.py:23
  56.9 17.3 %collective-permute-start.5 = (bf16[128,1664]{1,0:T(8,128)(2,1)}, bf16[128,1664]{1,0:T(8,128)(2,1)S(1)}, u32[]{:S(2)}, u32[]{:S(2)}) collective-permute-start(bf16[128,1664]{1,0:T(8,128)(2,1)} %get-tuple-element.10.refs_1_), channel_id=1, source_target_pairs={{0,24},{8,0},{16,8},{24,16},{1,25},{9,1},{17,9},{25,17},{2,26},{10... | collective-permute-start | bytes 1277960 | tf_op jit(solution)/shard_map/ppermute | solution.py:23
  56.9 22.9 %collective-permute-start.4 = (bf16[128,1664]{1,0:T(8,128)(2,1)}, bf16[128,1664]{1,0:T(8,128)(2,1)S(1)}, u32[]{:S(2)}, u32[]{:S(2)}) collective-permute-start(bf16[128,1664]{1,0:T(8,128)(2,1)} %get-tuple-element.10.refs_1_), channel_id=1, source_target_pairs={{0,8},{8,16},{16,24},{24,0},{1,9},{9,17},{17,25},{25,1},{2,10},{10... | collective-permute-start | bytes 1277960 | tf_op jit(solution)/shard_map/ppermute | solution.py:23
  59.0 24.2 %copy-start.12 = (bf16[128,1664]{1,0:T(8,128)(2,1)}, bf16[128,1664]{1,0:T(8,128)(2,1)S(1)}, u32[]{:S(2)}) copy-start(bf16[128,1664]{1,0:T(8,128)(2,1)S(1)} %collective-permute-done.7.refs_5_) | copy-start | bytes 1277956
  59.0 20.9 %collective-permute-start.12 = (bf16[896,256]{1,0:T(8,128)(2,1)S(1)}, bf16[896,256]{1,0:T(8,128)(2,1)S(1)}, u32[]{:S(2)}, u32[]{:S(2)}) collective-permute-start(bf16[896,256]{1,0:T(8,128)(2,1)S(1)} %slice.22.refs_10_), channel_id=1, source_target_pairs={{0,32},{32,64},{64,96},{96,0},{1,33},{33,65},{65,97},{97,1},{2,34}... | collective-permute-start | bytes 1376264 | tf_op jit(solution)/shard_map/ppermute | solution.py:23
  70.9 12.2 %copy-start.9 = (bf16[896,256]{1,0:T(8,128)(2,1)}, bf16[896,256]{1,0:T(8,128)(2,1)S(1)}, u32[]{:S(2)}) copy-start(bf16[896,256]{1,0:T(8,128)(2,1)S(1)} %collective-permute-done.14.refs_14_) | copy-start | bytes 1376260
  70.9 12.2 %collective-permute-start.16 = (bf16[896,256]{1,0:T(8,128)(2,1)S(1)}, bf16[896,256]{1,0:T(8,128)(2,1)S(1)}, u32[]{:S(2)}, u32[]{:S(2)}) collective-permute-start(bf16[896,256]{1,0:T(8,128)(2,1)S(1)} %collective-permute-done.14.refs_14_), channel_id=1, source_target_pairs={{0,96},{32,0},{64,32},{96,64},{1,97},{33,1},{65,33},{97,65},{2,98}... | collective-permute-start | bytes 1376264 | tf_op jit(solution)/shard_map/ppermute | solution.py:23
  71.7 8.2 %copy-start.13 = (bf16[128,1664]{1,0:T(8,128)(2,1)}, bf16[128,1664]{1,0:T(8,128)(2,1)S(1)}, u32[]{:S(2)}) copy-start(bf16[128,1664]{1,0:T(8,128)(2,1)S(1)} %collective-permute-done.6.refs_4_) | copy-start | bytes 1277956
  71.7 8.2 %collective-permute-start.10 = (bf16[128,1664]{1,0:T(8,128)(2,1)S(1)}, bf16[128,1664]{1,0:T(8,128)(2,1)S(1)}, u32[]{:S(2)}, u32[]{:S(2)}) collective-permute-start(bf16[128,1664]{1,0:T(8,128)(2,1)S(1)} %collective-permute-done.6.refs_4_), channel_id=1, source_target_pairs={{0,4},{4,0},{1,5},{5,1},{2,6},{6,2},{3,7},{7,3},{8,12},{12,8},{9,1... | collective-permute-start | bytes 1277960 | tf_op jit(solution)/shard_map/ppermute | solution.py:23
  74.2 7.4 %copy-start.14 = (bf16[128,1664]{1,0:T(8,128)(2,1)}, bf16[128,1664]{1,0:T(8,128)(2,1)S(1)}, u32[]{:S(2)}) copy-start(bf16[128,1664]{1,0:T(8,128)(2,1)S(1)} %collective-permute-done.5.refs_3_) | copy-start | bytes 1277956
  74.2 5.7 %collective-permute-start.9 = (bf16[128,1664]{1,0:T(8,128)(2,1)S(1)}, bf16[128,1664]{1,0:T(8,128)(2,1)S(1)}, u32[]{:S(2)}, u32[]{:S(2)}) collective-permute-start(bf16[128,1664]{1,0:T(8,128)(2,1)S(1)} %collective-permute-done.5.refs_3_), channel_id=1, source_target_pairs={{0,4},{4,0},{1,5},{5,1},{2,6},{6,2},{3,7},{7,3},{8,12},{12,8},{9,1... | collective-permute-start | bytes 1277960 | tf_op jit(solution)/shard_map/ppermute | solution.py:23
  79.8 1.8 %collective-permute-start.8 = (bf16[128,1664]{1,0:T(8,128)(2,1)S(1)}, bf16[128,1664]{1,0:T(8,128)(2,1)S(1)}, u32[]{:S(2)}, u32[]{:S(2)}) collective-permute-start(bf16[128,1664]{1,0:T(8,128)(2,1)S(1)} %collective-permute-done.4.refs_2_), channel_id=1, source_target_pairs={{0,4},{4,0},{1,5},{5,1},{2,6},{6,2},{3,7},{7,3},{8,12},{12,8},{9,1... | collective-permute-start | bytes 1277960 | tf_op jit(solution)/shard_map/ppermute | solution.py:23
  79.9 3.3 %copy-start.10 = (bf16[896,256]{1,0:T(8,128)(2,1)}, bf16[896,256]{1,0:T(8,128)(2,1)S(1)}, u32[]{:S(2)}) copy-start(bf16[896,256]{1,0:T(8,128)(2,1)S(1)} %collective-permute-done.12.refs_12_) | copy-start | bytes 1376260
  102.2 2.1 %collective-permute-start.17 = (bf16[128,1664]{1,0:T(8,128)(2,1)}, bf16[128,1664]{1,0:T(8,128)(2,1)S(1)}, u32[]{:S(2)}, u32[]{:S(2)}) collective-permute-start(bf16[128,1664]{1,0:T(8,128)(2,1)} %get-tuple-element.14), channel_id=1, source_target_pairs={{0,4},{4,0},{1,5},{5,1},{2,6},{6,2},{3,7},{7,3},{8,12},{12,8},{9,1... | collective-permute-start | bytes 1277960 | tf_op jit(solution)/shard_map/ppermute | solution.py:23
  105.6 7.4 %collective-permute-start.20 = (bf16[32,1664]{1,0:T(8,128)(2,1)S(1)}, bf16[32,1664]{1,0:T(8,128)(2,1)S(1)}, u32[]{:S(2)}, u32[]{:S(2)}) collective-permute-start(bf16[32,1664]{1,0:T(8,128)(2,1)S(1)} %get-tuple-element.18), channel_id=1, source_target_pairs={{0,16},{8,24},{16,0},{24,8},{1,17},{9,25},{17,1},{25,9},{2,18},{10... | collective-permute-start | bytes 319496 | tf_op jit(solution)/shard_map/ppermute | solution.py:23
  105.7 7.3 %collective-permute-start.19 = (bf16[32,1664]{1,0:T(8,128)(2,1)S(1)}, bf16[32,1664]{1,0:T(8,128)(2,1)S(1)}, u32[]{:S(2)}, u32[]{:S(2)}) collective-permute-start(bf16[32,1664]{1,0:T(8,128)(2,1)S(1)} %get-tuple-element.19), channel_id=1, source_target_pairs={{0,24},{8,0},{16,8},{24,16},{1,25},{9,1},{17,9},{25,17},{2,26},{10... | collective-permute-start | bytes 319496 | tf_op jit(solution)/shard_map/ppermute | solution.py:23
  106.4 8.1 %collective-permute-start.18 = (bf16[32,1664]{1,0:T(8,128)(2,1)S(1)}, bf16[32,1664]{1,0:T(8,128)(2,1)S(1)}, u32[]{:S(2)}, u32[]{:S(2)}) collective-permute-start(bf16[32,1664]{1,0:T(8,128)(2,1)S(1)} %get-tuple-element.20), channel_id=1, source_target_pairs={{0,8},{8,16},{16,24},{24,0},{1,9},{9,17},{17,25},{25,1},{2,10},{10... | collective-permute-start | bytes 319496 | tf_op jit(solution)/shard_map/ppermute | solution.py:23
  (9 other events, 11.5 us)
Sparse Core Ops, SparseCore 0:
  10.2 69.4 all-gather.2

commit v5 on v4

--- a/solution.py
+++ b/solution.py
@@ -180,7 +180,7 @@
     row_blocks = fetch_all(sources[:n_rows], targets[:n_rows], semaphores)
     gathered = sources[-1]
     shards, pieces, depth, width = gathered.shape
-    depth = depth - 16
+    depth = depth - 8
     fc, terms, proj = [], [], []
     at = n_rows
     units = targets[-1].shape[0]
@@ -239,7 +239,7 @@
     buffers = [pltpu.VMEM(a.shape, a.dtype) for a in (*mine, *other)]
     for number in range(shards):
         buffers += [pltpu.VMEM(a.shape, a.dtype) for a in fc[2 * number : 2 * number + 2]]
-        buffers.append(pltpu.VMEM((16, units), proj.dtype))
+        buffers.append(pltpu.VMEM((8, units), proj.dtype))
     buffers += [pltpu.VMEM((units, width), proj.dtype)] * shards
     pooled_mine, pooled_other = len(mine) * rows // 4, len(other) * rows // 4
     return call(
@@ -344,11 +344,11 @@
     far_b = shift(right_b, "x", -1)
     proj_part = units_here // tok_count
     proj_piece = lax.dynamic_slice_in_dim(w_proj, tok * proj_part, proj_part, 0)
-    terms = jnp.pad(three_terms(b_fc), ((0, 13), (0, model_width - units_here)))
+    terms = jnp.pad(three_terms(b_fc), ((0, 5), (0, model_width - units_here)))
     gathered = lax.all_gather(
         jnp.concatenate([proj_piece, terms], axis=0), ("x", "tok"), axis=0, tiled=False
     )
-    gathered = gathered.reshape(x_count, tok_count, proj_part + 16, model_width)
+    gathered = gathered.reshape(x_count, tok_count, proj_part + 8, model_width)
     weights = (fc_a, fc_b, left_a, left_b, right_a, right_b, far_a, far_b, gathered)
 
     normed, mixed_mean = call(

time: 142 us -> 140 us (0.986)
  transfers between devices with their start and end apart: 22 -> 22, of which waited for: 8 -> 7; matrix products, arithmetic and copies ran while one was open for 2% -> 2% of each run, Pallas kernels for 10% -> 10%
where the time goes in v5:
time: 140 us; the launch traced here: 139 us
  Pallas kernels  37.8 us (27%)
  starting transfers between devices  36.4 us (26%)
  waiting for transfers between devices  29.9 us (21%)
  between operations  14.4 us (10%)
  blocking collectives  12.2 us (9%)
  local copies, waits for them, and re-layouts  5.85 us (4%)
  other arithmetic  2.78 us (2%)
    pallas_call x4, Pallas kernels, call(): pl.pallas_call(wrapped, out_shape=outs, in_specs=[pl.BlockSpec(memory_spa...  37.8 us
    ppermute x17, waiting for transfers between devices, shift(): lax.ppermute(block, axis, [(i, (i + distance) % count) for i in range(cou...  29.9 us
    ppermute x17, starting transfers between devices, shift(): lax.ppermute(block, axis, [(i, (i + distance) % count) for i in range(cou...  28.6 us
    all_to_all x1, blocking collectives, body(): lax.all_to_all(outgoing, 'tok', split_axis=0, concat_axis=0, tiled=True)  12.2 us
    ppermute x4, starting transfers between devices, passed_along(): return lax.ppermute(block, BLK, route)  7.7 us
    unnamed x39, local copies, waits for them, and re-layouts  3.29 us
  transfers between devices with their start and end apart: 22, of which 7 were waited for; matrix products, arithmetic and copies ran while one was open for 2% of the time, Pallas kernels for 10%

profile of v5, /device:TPU:0, one launch (start us, length us, event | category | flops | bytes accessed | tf_op | source)
XLA Modules:
  0.0 139.3 jit_solution(14651369722175386871)
XLA Ops:
  7.2 0.8 fusion.12
  8.4 0.7 pad_maximum_fusion
  9.1 1.3 collective-permute-start
  10.5 1.3 collective-permute-start.1
  11.8 1.8 %slice.21.refs_9_ = bf16[768,256]{1,0:T(8,128)(2,1)} slice(bf16[1664,256]{1,0:T(8,128)(2,1)} %param.29), slice={[0:768], [0:256]} | slice | bytes 786432 | tf_op jit(solution)/shard_map/slice | solution.py:334
  13.5 6.6 %collective-permute-start.11 = (bf16[768,256]{1,0:T(8,128)(2,1)}, bf16[768,256]{1,0:T(8,128)(2,1)}, u32[]{:S(2)}, u32[]{:S(2)}) collective-permute-start(bf16[768,256]{1,0:T(8,128)(2,1)} %slice.21.refs_9_), channel_id=1, source_target_pairs={{0,32},{32,64},{64,96},{96,0},{1,33},{33,65},{65,97},{97,1},{2,34}... | collective-permute-start | bytes 1179656 | tf_op jit(solution)/shard_map/ppermute | solution.py:23
  20.2 5.6 %refresh.1.refs_3_ = bf16[128,1664]{1,0:T(8,128)(2,1)} custom-call(bf16[128,1664]{1,0:T(8,128)(2,1)} %refs_8_.2, bf16[128,1664]{1,0:T(8,128)(2,1)} %refs_1_.2, bf16[1664,1664]{1,0:T(8,128)(2,1)} %refs_2_.1, s32[12]{0:T(128)} %refs_3_.1, f32[1664]{0:T(1024)} %refs_4_.1, f32[1664]{0:T(1024)} %refs_5_.2), custom_call_target="tpu_custom_call" | custom-call | flops 88604672 | bytes 6389760 | tf_op jit(solution)/shard_map/refresh/pallas_call | solution.py:94
  25.8 1.3 collective-permute-start.3
  27.1 3.8 %collective-permute-start.2 = (bf16[128,1664]{1,0:T(8,128)(2,1)}, bf16[128,1664]{1,0:T(8,128)(2,1)}, u32[]{:S(2)}, u32[]{:S(2)}) collective-permute-start(bf16[128,1664]{1,0:T(8,128)(2,1)} %refresh.1.refs_3_), channel_id=1, source_target_pairs={{0,4},{4,8},{8,12},{12,16},{16,20},{20,24},{24,28},{28,32},{32,36}... | collective-permute-start | bytes 1277960 | tf_op jit(solution)/shard_map/ppermute | solution.py:18
  30.9 2.5 %collective-permute-start.13 = (bf16[768,256]{1,0:T(8,128)(2,1)}, bf16[768,256]{1,0:T(8,128)(2,1)}, u32[]{:S(2)}, u32[]{:S(2)}) collective-permute-start(bf16[768,256]{1,0:T(8,128)(2,1)} %slice.21.refs_9_), channel_id=1, source_target_pairs={{0,96},{32,0},{64,32},{96,64},{1,97},{33,1},{65,33},{97,65},{2,98}... | collective-permute-start | bytes 1179656 | tf_op jit(solution)/shard_map/ppermute | solution.py:23
  33.5 14.3 %collective-permute-start.14 = (bf16[896,256]{1,0:T(8,128)(2,1)S(1)}, bf16[896,256]{1,0:T(8,128)(2,1)S(1)}, u32[]{:S(2)}, u32[]{:S(2)}) collective-permute-start(bf16[896,256]{1,0:T(8,128)(2,1)S(1)} %slice.22.refs_10_), channel_id=1, source_target_pairs={{0,96},{32,0},{64,32},{96,64},{1,97},{33,1},{65,33},{97,65},{2,98}... | collective-permute-start | bytes 1376264 | tf_op jit(solution)/shard_map/ppermute | solution.py:23
  47.8 8.7 %attention.1 = (bf16[128,1664]{1,0:T(8,128)(2,1)}, f32[32,1664]{1,0:T(8,128)}) custom-call(s32[1]{0:T(128)} %bitcast.1.refs_0_, bf16[128,1664]{1,0:T(8,128)(2,1)} %refs_1_.3, bf16[128,1664]{1,0:T(8,128)(2,1)} %collective-permute-done.2.refs_2_, bf16[128,1664]{1,0:T(8,128)(2,1)} %refresh.1.refs_3_, bf16[128,1664]{1,0:T(8,128)(2,1)} %copy-done.5, ...), custom_call_target="tpu_custom_call" | custom-call | flops 654311424 | bytes 3407872 | tf_op jit(solution)/shard_map/attention/pallas_call | solution.py:94
  56.8 2.0 %collective-permute-start.4 = (bf16[128,1664]{1,0:T(8,128)(2,1)}, bf16[128,1664]{1,0:T(8,128)(2,1)S(1)}, u32[]{:S(2)}, u32[]{:S(2)}) collective-permute-start(bf16[128,1664]{1,0:T(8,128)(2,1)} %get-tuple-element.10.refs_1_), channel_id=1, source_target_pairs={{0,8},{8,16},{16,24},{24,0},{1,9},{9,17},{17,25},{25,1},{2,10},{10... | collective-permute-start | bytes 1277960 | tf_op jit(solution)/shard_map/ppermute | solution.py:23
  58.9 12.0 %collective-permute-done.14.refs_14_ = bf16[896,256]{1,0:T(8,128)(2,1)S(1)} collective-permute-done((bf16[896,256]{1,0:T(8,128)(2,1)S(1)}, bf16[896,256]{1,0:T(8,128)(2,1)S(1)}, u32[]{:S(2)}, u32[]{:S(2)}) %collective-permute-start.14) | collective-permute-done | bytes 458784 | tf_op jit(solution)/shard_map/ppermute | solution.py:23
  70.9 0.3 collective-permute-start.16
  71.2 2.8 %collective-permute-done.5.refs_3_ = bf16[128,1664]{1,0:T(8,128)(2,1)S(1)} collective-permute-done((bf16[128,1664]{1,0:T(8,128)(2,1)}, bf16[128,1664]{1,0:T(8,128)(2,1)S(1)}, u32[]{:S(2)}, u32[]{:S(2)}) %collective-permute-start.5) | collective-permute-done | bytes 426016 | tf_op jit(solution)/shard_map/ppermute | solution.py:23
  74.0 5.7 %collective-permute-done.4.refs_2_ = bf16[128,1664]{1,0:T(8,128)(2,1)S(1)} collective-permute-done((bf16[128,1664]{1,0:T(8,128)(2,1)}, bf16[128,1664]{1,0:T(8,128)(2,1)S(1)}, u32[]{:S(2)}, u32[]{:S(2)}) %collective-permute-start.4) | collective-permute-done | bytes 426016 | tf_op jit(solution)/shard_map/ppermute | solution.py:23
  79.8 1.7 %collective-permute-done.8.refs_6_ = bf16[128,1664]{1,0:T(8,128)(2,1)S(1)} collective-permute-done((bf16[128,1664]{1,0:T(8,128)(2,1)S(1)}, bf16[128,1664]{1,0:T(8,128)(2,1)S(1)}, u32[]{:S(2)}, u32[]{:S(2)}) %collective-permute-start.8) | collective-permute-done | bytes 426016 | tf_op jit(solution)/shard_map/ppermute | solution.py:23
  81.5 0.8 copy-done.18
  82.4 0.7 copy-done.11
  83.1 18.3 %mlp.1 = (f32[128,1664]{1,0:T(8,128)}, bf16[128,1664]{1,0:T(8,128)(2,1)}) custom-call(s32[1]{0:T(128)} %bitcast.refs_0_, bf16[128,1664]{1,0:T(8,128)(2,1)} %get-tuple-element.10.refs_1_, bf16[128,1664]{1,0:T(8,128)(2,1)} %copy-done.15, bf16[128,1664]{1,0:T(8,128)(2,1)} %copy-done.14, bf16[128,1664]{1,0:T(8,128)(2,1)} %copy-done.13, ...), custom_call_target="tpu_custom_call" | custom-call | flops 4362076160 | bytes 10649600 | tf_op jit(solution)/shard_map/mlp/pallas_call | solution.py:94
  101.7 1.9 %collective-permute-done.17 = bf16[128,1664]{1,0:T(8,128)(2,1)S(1)} collective-permute-done((bf16[128,1664]{1,0:T(8,128)(2,1)}, bf16[128,1664]{1,0:T(8,128)(2,1)S(1)}, u32[]{:S(2)}, u32[]{:S(2)}) %collective-permute-start.17) | collective-permute-done | bytes 426016 | tf_op jit(solution)/shard_map/ppermute | solution.py:23
  103.5 1.2 fusion.10
  105.1 1.2 collective-permute-start.19
  106.4 0.8 collective-permute-start.18
  107.2 0.7 slice.27.refs_0_
  107.9 4.3 %collective-permute-done.20.refs_3_ = bf16[32,1664]{1,0:T(8,128)(2,1)S(1)} collective-permute-done((bf16[32,1664]{1,0:T(8,128)(2,1)S(1)}, bf16[32,1664]{1,0:T(8,128)(2,1)S(1)}, u32[]{:S(2)}, u32[]{:S(2)}) %collective-permute-start.20) | collective-permute-done | bytes 106528 | tf_op jit(solution)/shard_map/ppermute | solution.py:23
  112.2 1.5 %collective-permute-done.18.refs_1_ = bf16[32,1664]{1,0:T(8,128)(2,1)S(1)} collective-permute-done((bf16[32,1664]{1,0:T(8,128)(2,1)S(1)}, bf16[32,1664]{1,0:T(8,128)(2,1)S(1)}, u32[]{:S(2)}, u32[]{:S(2)}) %collective-permute-start.18) | collective-permute-done | bytes 106528 | tf_op jit(solution)/shard_map/ppermute | solution.py:23
  113.7 0.6 copy-done.8
  114.3 5.2 %merge.1 = bf16[128,1664]{1,0:T(8,128)(2,1)} custom-call(f32[32,1664]{1,0:T(8,128)} %slice.27.refs_0_, bf16[32,1664]{1,0:T(8,128)(2,1)} %copy-done.8, bf16[32,1664]{1,0:T(8,128)(2,1)} %copy-done.7, bf16[32,1664]{1,0:T(8,128)(2,1)} %copy-done.6, f32[32,1664]{1,0:T(8,128)} %get-tuple-element.15.refs_4_, bf16[1664,1664]{1,0:T(8,128)(2,1)} %refs_5_.3, ...), custom_call_target="tpu_custom_call" | custom-call | flops 177209344 | bytes 6283264 | tf_op jit(solution)/shard_map/merge/pallas_call | solution.py:94
  119.5 12.2 %all_to_all.5 = bf16[4,32,1664]{2,1,0:T(8,128)(2,1)S(1)} all-to-all(bf16[4,32,1664]{2,1,0:T(8,128)(2,1)} %bitcast.7), channel_id=1, replica_groups=mesh['x'=4,'z'=4,'c'=2,'tok'=4] {'tok'}, dimensions={0} | all-to-all | bytes 851968 | tf_op jit(solution)/shard_map/all_to_all | solution.py:408
  131.7 0.8 copy.21
  (69 shorter events, 1.4 us)
Async XLA Ops:
  7.2 26.2 %copy-start.1 = (bf16[1664,256]{1,0:T(8,128)(2,1)S(1)}, bf16[1664,256]{1,0:T(8,128)(2,1)}, u32[]{:S(2)}) copy-start(bf16[1664,256]{1,0:T(8,128)(2,1)} %param.29) | copy-start | bytes 2555908
  7.2 75.1 %all-gather.3.cloned.1.call-start = ((), (), s32[]{:S(2)}) async-start(), calls=%async_computation.1 | async-start | bytes 4073472 | tf_op jit(solution)/shard_map/all_gather | solution.py:348
  9.1 16.7 %collective-permute-start = (bf16[128,1664]{1,0:T(8,128)(2,1)}, bf16[128,1664]{1,0:T(8,128)(2,1)S(1)}, u32[]{:S(2)}, u32[]{:S(2)}) collective-permute-start(bf16[128,1664]{1,0:T(8,128)(2,1)} %refs_6_.2), channel_id=1, source_target_pairs={{0,4},{4,8},{8,12},{12,16},{16,20},{20,24},{24,28},{28,32},{32,36}... | collective-permute-start | bytes 1277960 | tf_op jit(solution)/shard_map/ppermute | solution.py:18
  10.5 15.4 %collective-permute-start.1 = (bf16[128,1664]{1,0:T(8,128)(2,1)}, bf16[128,1664]{1,0:T(8,128)(2,1)S(1)}, u32[]{:S(2)}, u32[]{:S(2)}) collective-permute-start(bf16[128,1664]{1,0:T(8,128)(2,1)} %refs_6_.2), channel_id=1, source_target_pairs={{4,0},{8,4},{12,8},{16,12},{20,16},{24,20},{28,24},{32,28},{36,32}... | collective-permute-start | bytes 1277960 | tf_op jit(solution)/shard_map/ppermute | solution.py:18
  13.5 19.9 %collective-permute-start.11 = (bf16[768,256]{1,0:T(8,128)(2,1)}, bf16[768,256]{1,0:T(8,128)(2,1)}, u32[]{:S(2)}, u32[]{:S(2)}) collective-permute-start(bf16[768,256]{1,0:T(8,128)(2,1)} %slice.21.refs_9_), channel_id=1, source_target_pairs={{0,32},{32,64},{64,96},{96,0},{1,33},{33,65},{65,97},{97,1},{2,34}... | collective-permute-start | bytes 1179656 | tf_op jit(solution)/shard_map/ppermute | solution.py:23
  25.8 22.0 %copy-start.3 = (bf16[128,1664]{1,0:T(8,128)(2,1)}, bf16[128,1664]{1,0:T(8,128)(2,1)S(1)}, u32[]{:S(2)}) copy-start(bf16[128,1664]{1,0:T(8,128)(2,1)S(1)} %collective-permute-done.refs_5_) | copy-start | bytes 1277956
  25.8 22.0 %copy-start.4 = (bf16[128,1664]{1,0:T(8,128)(2,1)}, bf16[128,1664]{1,0:T(8,128)(2,1)S(1)}, u32[]{:S(2)}) copy-start(bf16[128,1664]{1,0:T(8,128)(2,1)S(1)} %collective-permute-done.1.refs_7_) | copy-start | bytes 1277956
  25.8 7.7 %collective-permute-start.3 = (bf16[128,1664]{1,0:T(8,128)(2,1)}, bf16[128,1664]{1,0:T(8,128)(2,1)S(1)}, u32[]{:S(2)}, u32[]{:S(2)}) collective-permute-start(bf16[128,1664]{1,0:T(8,128)(2,1)} %refresh.1.refs_3_), channel_id=1, source_target_pairs={{4,0},{8,4},{12,8},{16,12},{20,16},{24,20},{28,24},{32,28},{36,32}... | collective-permute-start | bytes 1277960 | tf_op jit(solution)/shard_map/ppermute | solution.py:18
  27.1 6.4 %collective-permute-start.2 = (bf16[128,1664]{1,0:T(8,128)(2,1)}, bf16[128,1664]{1,0:T(8,128)(2,1)}, u32[]{:S(2)}, u32[]{:S(2)}) collective-permute-start(bf16[128,1664]{1,0:T(8,128)(2,1)} %refresh.1.refs_3_), channel_id=1, source_target_pairs={{0,4},{4,8},{8,12},{12,16},{16,20},{20,24},{24,28},{28,32},{32,36}... | collective-permute-start | bytes 1277960 | tf_op jit(solution)/shard_map/ppermute | solution.py:18
  30.9 25.8 %collective-permute-start.13 = (bf16[768,256]{1,0:T(8,128)(2,1)}, bf16[768,256]{1,0:T(8,128)(2,1)}, u32[]{:S(2)}, u32[]{:S(2)}) collective-permute-start(bf16[768,256]{1,0:T(8,128)(2,1)} %slice.21.refs_9_), channel_id=1, source_target_pairs={{0,96},{32,0},{64,32},{96,64},{1,97},{33,1},{65,33},{97,65},{2,98}... | collective-permute-start | bytes 1179656 | tf_op jit(solution)/shard_map/ppermute | solution.py:23
  33.4 23.4 %collective-permute-start.15 = (bf16[768,256]{1,0:T(8,128)(2,1)}, bf16[768,256]{1,0:T(8,128)(2,1)}, u32[]{:S(2)}, u32[]{:S(2)}) collective-permute-start(bf16[768,256]{1,0:T(8,128)(2,1)} %collective-permute-done.11.refs_11_), channel_id=1, source_target_pairs={{0,32},{32,64},{64,96},{96,0},{1,33},{33,65},{65,97},{97,1},{2,34}... | collective-permute-start | bytes 1179656 | tf_op jit(solution)/shard_map/ppermute | solution.py:23
  33.5 48.9 %copy-start.2 = (bf16[896,256]{1,0:T(8,128)(2,1)}, bf16[896,256]{1,0:T(8,128)(2,1)S(1)}, u32[]{:S(2)}) copy-start(bf16[896,256]{1,0:T(8,128)(2,1)S(1)} %slice.22.refs_10_) | copy-start | bytes 1376260
  33.5 14.3 %copy-start.5 = (bf16[128,1664]{1,0:T(8,128)(2,1)}, bf16[128,1664]{1,0:T(8,128)(2,1)S(1)}, u32[]{:S(2)}) copy-start(bf16[128,1664]{1,0:T(8,128)(2,1)S(1)} %collective-permute-done.3.refs_4_) | copy-start | bytes 1277956
  33.5 37.3 %collective-permute-start.14 = (bf16[896,256]{1,0:T(8,128)(2,1)S(1)}, bf16[896,256]{1,0:T(8,128)(2,1)S(1)}, u32[]{:S(2)}, u32[]{:S(2)}) collective-permute-start(bf16[896,256]{1,0:T(8,128)(2,1)S(1)} %slice.22.refs_10_), channel_id=1, source_target_pairs={{0,96},{32,0},{64,32},{96,64},{1,97},{33,1},{65,33},{97,65},{2,98}... | collective-permute-start | bytes 1376264 | tf_op jit(solution)/shard_map/ppermute | solution.py:23
  56.6 2.3 %collective-permute-start.7 = (bf16[128,1664]{1,0:T(8,128)(2,1)}, bf16[128,1664]{1,0:T(8,128)(2,1)S(1)}, u32[]{:S(2)}, u32[]{:S(2)}) collective-permute-start(bf16[128,1664]{1,0:T(8,128)(2,1)} %get-tuple-element.10.refs_1_), channel_id=1, source_target_pairs={{0,4},{4,0},{1,5},{5,1},{2,6},{6,2},{3,7},{7,3},{8,12},{12,8},{9,1... | collective-permute-start | bytes 1277960 | tf_op jit(solution)/shard_map/ppermute | solution.py:23
  56.6 14.6 %collective-permute-start.6 = (bf16[128,1664]{1,0:T(8,128)(2,1)}, bf16[128,1664]{1,0:T(8,128)(2,1)S(1)}, u32[]{:S(2)}, u32[]{:S(2)}) collective-permute-start(bf16[128,1664]{1,0:T(8,128)(2,1)} %get-tuple-element.10.refs_1_), channel_id=1, source_target_pairs={{0,16},{8,24},{16,0},{24,8},{1,17},{9,25},{17,1},{25,9},{2,18},{10... | collective-permute-start | bytes 1277960 | tf_op jit(solution)/shard_map/ppermute | solution.py:23
  56.8 17.3 %collective-permute-start.5 = (bf16[128,1664]{1,0:T(8,128)(2,1)}, bf16[128,1664]{1,0:T(8,128)(2,1)S(1)}, u32[]{:S(2)}, u32[]{:S(2)}) collective-permute-start(bf16[128,1664]{1,0:T(8,128)(2,1)} %get-tuple-element.10.refs_1_), channel_id=1, source_target_pairs={{0,24},{8,0},{16,8},{24,16},{1,25},{9,1},{17,9},{25,17},{2,26},{10... | collective-permute-start | bytes 1277960 | tf_op jit(solution)/shard_map/ppermute | solution.py:23
  56.8 22.9 %collective-permute-start.4 = (bf16[128,1664]{1,0:T(8,128)(2,1)}, bf16[128,1664]{1,0:T(8,128)(2,1)S(1)}, u32[]{:S(2)}, u32[]{:S(2)}) collective-permute-start(bf16[128,1664]{1,0:T(8,128)(2,1)} %get-tuple-element.10.refs_1_), channel_id=1, source_target_pairs={{0,8},{8,16},{16,24},{24,0},{1,9},{9,17},{17,25},{25,1},{2,10},{10... | collective-permute-start | bytes 1277960 | tf_op jit(solution)/shard_map/ppermute | solution.py:23
  58.9 23.5 %copy-start.12 = (bf16[128,1664]{1,0:T(8,128)(2,1)}, bf16[128,1664]{1,0:T(8,128)(2,1)S(1)}, u32[]{:S(2)}) copy-start(bf16[128,1664]{1,0:T(8,128)(2,1)S(1)} %collective-permute-done.7.refs_5_) | copy-start | bytes 1277956
  58.9 20.9 %collective-permute-start.12 = (bf16[896,256]{1,0:T(8,128)(2,1)S(1)}, bf16[896,256]{1,0:T(8,128)(2,1)S(1)}, u32[]{:S(2)}, u32[]{:S(2)}) collective-permute-start(bf16[896,256]{1,0:T(8,128)(2,1)S(1)} %slice.22.refs_10_), channel_id=1, source_target_pairs={{0,32},{32,64},{64,96},{96,0},{1,33},{33,65},{65,97},{97,1},{2,34}... | collective-permute-start | bytes 1376264 | tf_op jit(solution)/shard_map/ppermute | solution.py:23
  70.9 11.5 %copy-start.9 = (bf16[896,256]{1,0:T(8,128)(2,1)}, bf16[896,256]{1,0:T(8,128)(2,1)S(1)}, u32[]{:S(2)}) copy-start(bf16[896,256]{1,0:T(8,128)(2,1)S(1)} %collective-permute-done.14.refs_14_) | copy-start | bytes 1376260
  70.9 11.5 %collective-permute-start.16 = (bf16[896,256]{1,0:T(8,128)(2,1)S(1)}, bf16[896,256]{1,0:T(8,128)(2,1)S(1)}, u32[]{:S(2)}, u32[]{:S(2)}) collective-permute-start(bf16[896,256]{1,0:T(8,128)(2,1)S(1)} %collective-permute-done.14.refs_14_), channel_id=1, source_target_pairs={{0,96},{32,0},{64,32},{96,64},{1,97},{33,1},{65,33},{97,65},{2,98}... | collective-permute-start | bytes 1376264 | tf_op jit(solution)/shard_map/ppermute | solution.py:23
  71.2 8.6 %copy-start.13 = (bf16[128,1664]{1,0:T(8,128)(2,1)}, bf16[128,1664]{1,0:T(8,128)(2,1)S(1)}, u32[]{:S(2)}) copy-start(bf16[128,1664]{1,0:T(8,128)(2,1)S(1)} %collective-permute-done.6.refs_4_) | copy-start | bytes 1277956
  71.2 8.6 %collective-permute-start.10 = (bf16[128,1664]{1,0:T(8,128)(2,1)S(1)}, bf16[128,1664]{1,0:T(8,128)(2,1)S(1)}, u32[]{:S(2)}, u32[]{:S(2)}) collective-permute-start(bf16[128,1664]{1,0:T(8,128)(2,1)S(1)} %collective-permute-done.6.refs_4_), channel_id=1, source_target_pairs={{0,4},{4,0},{1,5},{5,1},{2,6},{6,2},{3,7},{7,3},{8,12},{12,8},{9,1... | collective-permute-start | bytes 1277960 | tf_op jit(solution)/shard_map/ppermute | solution.py:23
  74.0 7.5 %copy-start.14 = (bf16[128,1664]{1,0:T(8,128)(2,1)}, bf16[128,1664]{1,0:T(8,128)(2,1)S(1)}, u32[]{:S(2)}) copy-start(bf16[128,1664]{1,0:T(8,128)(2,1)S(1)} %collective-permute-done.5.refs_3_) | copy-start | bytes 1277956
  74.0 5.8 %collective-permute-start.9 = (bf16[128,1664]{1,0:T(8,128)(2,1)S(1)}, bf16[128,1664]{1,0:T(8,128)(2,1)S(1)}, u32[]{:S(2)}, u32[]{:S(2)}) collective-permute-start(bf16[128,1664]{1,0:T(8,128)(2,1)S(1)} %collective-permute-done.5.refs_3_), channel_id=1, source_target_pairs={{0,4},{4,0},{1,5},{5,1},{2,6},{6,2},{3,7},{7,3},{8,12},{12,8},{9,1... | collective-permute-start | bytes 1277960 | tf_op jit(solution)/shard_map/ppermute | solution.py:23
  79.7 1.8 %collective-permute-start.8 = (bf16[128,1664]{1,0:T(8,128)(2,1)S(1)}, bf16[128,1664]{1,0:T(8,128)(2,1)S(1)}, u32[]{:S(2)}, u32[]{:S(2)}) collective-permute-start(bf16[128,1664]{1,0:T(8,128)(2,1)S(1)} %collective-permute-done.4.refs_2_), channel_id=1, source_target_pairs={{0,4},{4,0},{1,5},{5,1},{2,6},{6,2},{3,7},{7,3},{8,12},{12,8},{9,1... | collective-permute-start | bytes 1277960 | tf_op jit(solution)/shard_map/ppermute | solution.py:23
  79.8 2.6 %copy-start.10 = (bf16[896,256]{1,0:T(8,128)(2,1)}, bf16[896,256]{1,0:T(8,128)(2,1)S(1)}, u32[]{:S(2)}) copy-start(bf16[896,256]{1,0:T(8,128)(2,1)S(1)} %collective-permute-done.12.refs_12_) | copy-start | bytes 1376260
  101.5 2.1 %collective-permute-start.17 = (bf16[128,1664]{1,0:T(8,128)(2,1)}, bf16[128,1664]{1,0:T(8,128)(2,1)S(1)}, u32[]{:S(2)}, u32[]{:S(2)}) collective-permute-start(bf16[128,1664]{1,0:T(8,128)(2,1)} %get-tuple-element.14), channel_id=1, source_target_pairs={{0,4},{4,0},{1,5},{5,1},{2,6},{6,2},{3,7},{7,3},{8,12},{12,8},{9,1... | collective-permute-start | bytes 1277960 | tf_op jit(solution)/shard_map/ppermute | solution.py:23
  104.8 7.4 %collective-permute-start.20 = (bf16[32,1664]{1,0:T(8,128)(2,1)S(1)}, bf16[32,1664]{1,0:T(8,128)(2,1)S(1)}, u32[]{:S(2)}, u32[]{:S(2)}) collective-permute-start(bf16[32,1664]{1,0:T(8,128)(2,1)S(1)} %get-tuple-element.18), channel_id=1, source_target_pairs={{0,16},{8,24},{16,0},{24,8},{1,17},{9,25},{17,1},{25,9},{2,18},{10... | collective-permute-start | bytes 319496 | tf_op jit(solution)/shard_map/ppermute | solution.py:23
  105.1 7.1 %collective-permute-start.19 = (bf16[32,1664]{1,0:T(8,128)(2,1)S(1)}, bf16[32,1664]{1,0:T(8,128)(2,1)S(1)}, u32[]{:S(2)}, u32[]{:S(2)}) collective-permute-start(bf16[32,1664]{1,0:T(8,128)(2,1)S(1)} %get-tuple-element.19), channel_id=1, source_target_pairs={{0,24},{8,0},{16,8},{24,16},{1,25},{9,1},{17,9},{25,17},{2,26},{10... | collective-permute-start | bytes 319496 | tf_op jit(solution)/shard_map/ppermute | solution.py:23
  106.4 7.3 %collective-permute-start.18 = (bf16[32,1664]{1,0:T(8,128)(2,1)S(1)}, bf16[32,1664]{1,0:T(8,128)(2,1)S(1)}, u32[]{:S(2)}, u32[]{:S(2)}) collective-permute-start(bf16[32,1664]{1,0:T(8,128)(2,1)S(1)} %get-tuple-element.20), channel_id=1, source_target_pairs={{0,8},{8,16},{16,24},{24,0},{1,9},{9,17},{17,25},{25,1},{2,10},{10... | collective-permute-start | bytes 319496 | tf_op jit(solution)/shard_map/ppermute | solution.py:23
  (9 other events, 11.6 us)
Sparse Core Ops, SparseCore 0:
  10.2 65.6 all-gather.2
